TPU v7x, 32 devices: a whole 2x2x4 slice. The times are simulated.
32 devices in a mesh: dp: 16 (over z, x, core), rows: 2 (over y).
Axes of the slice: x: 2, y: 2, z: 4, core: 2. Of those that a mesh axis runs over, the one named last changes fastest.
Arguments:
- features: bfloat16 [32, 12, 64, 1024], P('dp', 'rows'), may hold values from -8 to 8
- first_atrous_weight: bfloat16 [3, 3, 1024, 256], P(None, None, 'dp'), may hold values from -0.0625 to 0.0625
- second_atrous_weight: bfloat16 [3, 3, 1024, 256], P(None, None, 'dp'), may hold values from -0.0625 to 0.0625
- third_atrous_weight: bfloat16 [3, 3, 1024, 256], P(None, None, 'dp'), may hold values from -0.0625 to 0.0625
- pointwise_weight: bfloat16 [1024, 256], replicated, may hold values from -0.1875 to 0.1875
- pooling_weight: bfloat16 [1024, 256], replicated, may hold values from -0.1875 to 0.1875
- projection_weight: bfloat16 [1280, 256], replicated, may hold values from -0.15625 to 0.15625
- branch_norm_gain: float32 [4, 256], replicated, may hold values from 0.25 to 1.75
- branch_norm_shift: float32 [4, 256], replicated, may hold values from -3 to 3
- projection_norm_gain: float32 [256], replicated, may hold values from 0.25 to 1.75
- projection_norm_shift: float32 [256], replicated, may hold values from -3 to 3
- ghost_group_index: int32 [32], replicated, may hold values from 0 to 7, as said below
Outputs:
- decoder_in: bfloat16 [32, 12, 64, 256], P(None, 'rows', 'dp')
Inputs may be any that keep to these rules, and one draw needn't show every extreme that they name: `ghost_group_index`: each of the 8 group ids names exactly 4 images.
All inputs are finite; a program needn't handle non-finite values.
Results may differ from a plain program's by a relative error of at most 0.0014.
The roundings to bfloat16 on the way count: a program that leaves them out, or rounds other values in their place, can miss the bound.
Values may be sent and summed in bfloat16 or wider, within the bound.
No kernel may reach another device: no remote copies, remote signals or barrier semaphores. Data moves between devices by JAX's collectives and lax.ppermute only.
A program may use at most 128 MiB of HBM per device.

v0:
```python
import jax
import jax.numpy as jnp
from jax import lax
from jax.sharding import PartitionSpec as P

DILATION_FIRST = 12
DILATION_SECOND = 24
DILATION_THIRD = 36


def from_behind(array, axis, by):
    count = lax.axis_size(axis)
    pairs = [(i, i + by) for i in range(count) if 0 <= i + by < count]
    return lax.ppermute(array, axis, pairs)


def row_tap_list(block_tensor, kernel_row_slice, dilation_rate):
    partial_terms = jnp.einsum(
        "irwc,kco->irwko", block_tensor, kernel_row_slice, preferred_element_type=jnp.float32
    )
    map_width = block_tensor.shape[2]
    left_padding = jnp.pad(partial_terms[:, :, :, 0], ((0, 0), (0, 0), (dilation_rate, 0), (0, 0)))[
        :, :, :map_width
    ]
    right_padding = jnp.pad(
        partial_terms[:, :, :, 2], ((0, 0), (0, 0), (0, dilation_rate), (0, 0))
    )[:, :, dilation_rate:]
    return partial_terms[:, :, :, 1] + left_padding + right_padding


def dilated_result(features, kernel_weight, dilation_rate):
    step_offsets = dilation_rate // features.shape[1]
    running_sum = row_tap_list(features, kernel_weight[1], dilation_rate)
    for by_dev, tap_offset in ((step_offsets, 0), (-step_offsets, 2)):
        partial_taps = row_tap_list(features, kernel_weight[tap_offset], dilation_rate)
        running_sum = running_sum + from_behind(partial_taps, "rows", by_dev)
    return running_sum


def stats_terms(pre, onehot):
    first = jnp.sum(pre, axis=(1, 2))
    second = jnp.sum(pre * pre, axis=(1, 2))
    group_first = jnp.dot(onehot.T, first, precision=lax.Precision.HIGHEST)
    group_second = jnp.dot(onehot.T, second, precision=lax.Precision.HIGHEST)
    return (group_first, group_second)


def apply_norm(pre, onehot, total_first, total_second, count, gain, shift):
    mean = total_first / count
    var = total_second / count - mean * mean
    inv = lax.rsqrt(var + 1e-05)
    img_mean = jnp.dot(onehot, mean, precision=lax.Precision.HIGHEST)
    img_inv = jnp.dot(onehot, inv, precision=lax.Precision.HIGHEST)
    scaled = (pre - img_mean[:, None, None, :]) * img_inv[:, None, None, :] * gain + shift
    return jax.nn.relu(scaled).astype(jnp.bfloat16)


def project(joined, onehot, projection_weight, count, projection_norm_gain, projection_norm_shift):
    proj = jnp.einsum(
        "irwc,co->irwo", joined, projection_weight, preferred_element_type=jnp.float32
    )
    group_first, group_second = stats_terms(proj, onehot)
    total_first, total_second = lax.psum((group_first, group_second), ("dp", "rows"))
    return apply_norm(
        proj, onehot, total_first, total_second, count, projection_norm_gain, projection_norm_shift
    )


def shards(
    features,
    first_atrous_weight,
    second_atrous_weight,
    third_atrous_weight,
    pointwise_weight,
    pooling_weight,
    projection_weight,
    branch_norm_gain,
    branch_norm_shift,
    projection_norm_gain,
    projection_norm_shift,
    ghost_group_index,
):
    img_dev, rows_dev, cols, chans = features.shape
    dp_size = lax.axis_size("dp")
    rows_size = lax.axis_size("rows")
    images = img_dev * dp_size
    groups = images // 4
    pixels = rows_dev * rows_size * cols
    count = 4.0 * pixels
    start = lax.axis_index("dp") * img_dev
    labels = jnp.arange(groups, dtype=jnp.int32)
    all_hot = (ghost_group_index[:, None] == labels[None, :]).astype(jnp.float32)
    own_hot = lax.dynamic_slice_in_dim(all_hot, start, img_dev, 0)
    first_kernel, second_kernel, third_kernel = (
        lax.all_gather(first_atrous_weight, "dp", axis=2, tiled=True),
        lax.all_gather(second_atrous_weight, "dp", axis=2, tiled=True),
        lax.all_gather(third_atrous_weight, "dp", axis=2, tiled=True),
    )
    pointwise_output = jnp.einsum(
        "irwc,co->irwo", features, pointwise_weight, preferred_element_type=jnp.float32
    )
    pre = jnp.concatenate(
        [
            pointwise_output,
            dilated_result(features, first_kernel, DILATION_FIRST),
            dilated_result(features, second_kernel, DILATION_SECOND),
            dilated_result(features, third_kernel, DILATION_THIRD),
        ],
        -1,
    )
    group_first, group_second = stats_terms(pre, own_hot)
    pool_part = jnp.sum(features, axis=(1, 2), dtype=jnp.float32)
    pool_total = lax.psum(pool_part, "rows")
    total_first, total_second = lax.psum((group_first, group_second), ("dp", "rows"))
    branches = apply_norm(
        pre,
        own_hot,
        total_first,
        total_second,
        count,
        branch_norm_gain.reshape(-1),
        branch_norm_shift.reshape(-1),
    )
    pooled = (pool_total / pixels).astype(jnp.bfloat16)
    pool_act = jax.nn.relu(
        jnp.dot(pooled, pooling_weight, preferred_element_type=jnp.float32)
    ).astype(jnp.bfloat16)
    pool_map = jnp.broadcast_to(
        pool_act[:, None, None, :], (img_dev, rows_dev, cols, pool_act.shape[1])
    )
    joined = jnp.concatenate([branches, pool_map], -1)
    local_out = project(
        joined, own_hot, projection_weight, count, projection_norm_gain, projection_norm_shift
    )
    return lax.all_to_all(local_out, "dp", split_axis=2, concat_axis=0, tiled=True)


def solution(mesh):
    in_specs = (
        P("dp", "rows", None, None),
        P(None, None, "dp", None),
        P(None, None, "dp", None),
        P(None, None, "dp", None),
        P(),
        P(),
        P(),
        P(),
        P(),
        P(),
        P(),
        P(),
    )
    out_specs = P(None, "rows", "dp", None)
    return jax.shard_map(shards, mesh=mesh, in_specs=in_specs, out_specs=out_specs, check_vma=False)
```

profile of v0, /device:TPU:0, one launch (start us, length us, event | category | flops | bytes accessed | tf_op | source)
XLA Modules:
  0.0 381.6 jit_solution(11481842989761349140)
XLA Ops:
  6.5 0.7 all-gather.4.cloned.1.call-update
  7.3 0.7 all-gather.6.cloned.1.call-update
  8.1 0.7 all-gather.8.cloned.1.call-update
  8.8 0.7 dynamic-slice
  9.5 1.7 convert_reduce_fusion
  11.2 6.0 %psum.37 = f32[2,1024]{1,0:T(2,128)S(1)} all-reduce(f32[2,1024]{1,0:T(2,128)S(1)} %convert_reduce_fusion), channel_id=1, replica_groups=mesh['dp'=16,'rows'=2] {'rows'}, use_global_device_ids=true, to_apply=%region_5.6 | all-reduce | flops 2048 | bytes 16384 | tf_op jit(solution)/shard_map/psum | solution.py:113
  17.2 1.5 fusion.49
  18.7 46.5 %all-gather.4.cloned.1.call-done = bf16[3,3,1024,256]{3,2,1,0:T(8,128)(2,1)} async-done(((bf16[3,3,64,256]{3,2,1,0:T(8,128)(2,1)}), bf16[3,3,1024,256]{3,2,1,0:T(8,128)(2,1)}) %all-gather.4.cloned.1.call-update) | async-done | bytes 4718608 | tf_op jit(solution)/shard_map/all_gather | solution.py:95
  65.2 2.8 fusion.11
  68.1 1.0 fusion.28
  69.2 1.5 collective-permute-start
  70.7 2.8 fusion.10
  73.6 1.1 fusion.30
  74.7 1.5 collective-permute-start.1
  76.2 42.7 %all-gather.6.cloned.1.call-done = bf16[3,3,1024,256]{3,2,1,0:T(8,128)(2,1)} async-done(((bf16[3,3,64,256]{3,2,1,0:T(8,128)(2,1)}), bf16[3,3,1024,256]{3,2,1,0:T(8,128)(2,1)}) %all-gather.6.cloned.1.call-update) | async-done | bytes 4718608 | tf_op jit(solution)/shard_map/all_gather | solution.py:96
  119.0 2.8 fusion.8
  121.9 1.0 fusion.36
  122.9 1.6 collective-permute-start.2
  124.4 2.8 fusion.7
  127.3 1.0 fusion.38
  128.3 1.5 collective-permute-start.3
  129.9 2.8 fusion.12
  132.7 1.4 copy-done.4
  134.1 1.0 slice_bitcast_fusion.42
  135.1 37.6 %all-gather.8.cloned.1.call-done = bf16[3,3,1024,256]{3,2,1,0:T(8,128)(2,1)} async-done(((bf16[3,3,64,256]{3,2,1,0:T(8,128)(2,1)}), bf16[3,3,1024,256]{3,2,1,0:T(8,128)(2,1)}) %all-gather.8.cloned.1.call-update) | async-done | bytes 4718608 | tf_op jit(solution)/shard_map/all_gather | solution.py:97
  172.7 2.8 fusion.5
  175.7 1.0 collective-permute-start.4
  176.8 3.0 fusion.9
  179.8 1.4 fusion.4
  181.2 1.4 fusion.6
  183.0 0.8 collective-permute-start.5
  184.1 1.9 fusion.26
  186.0 1.6 fusion.34
  187.9 0.9 copy-done.1
  188.8 0.4 fusion.48
  189.2 0.9 fusion.79
  190.1 0.9 fusion.78
  191.2 0.7 copy.120
  191.9 117.9 %all-reduce.22.cloned.1.call-done = (f32[8,1024]{1,0:T(8,128)}, f32[8,1024]{1,0:T(8,128)}) async-done(((f32[8,1024]{1,0:T(8,128)}, f32[8,1024]{1,0:T(8,128)}), (f32[8,1024]{1,0:T(8,128)}, f32[8,1024]{1,0:T(8,128)})) %all-reduce.22.cloned.1.call-update) | async-done | bytes 65552 | tf_op jit(solution)/shard_map/psum | solution.py:114
  309.8 1.0 fusion.58
  310.7 1.0 fusion.51
  311.7 1.7 maximum_convert_fusion
  313.5 0.7 fusion.96
  314.5 0.3 fusion.76
  314.7 41.1 %all-reduce.18 = (f32[8,256]{1,0:T(8,128)S(1)}, f32[8,256]{1,0:T(8,128)S(1)}) all-reduce(f32[8,256]{1,0:T(8,128)S(1)} %fusion.76, f32[8,256]{1,0:T(8,128)S(1)} %fusion.77), channel_id=1, replica_groups=mesh['dp'=16,'rows'=2] {'dp','rows'}, use_global_device_ids=true, to_apply=%region_9.10 | all-reduce | flops 4096 | bytes 32768 | tf_op jit(solution)/shard_map/psum | solution.py:63
  356.4 0.4 copy.97
  356.8 17.3 %all_to_all.18 = bf16[2,6,64,256]{3,0,1,2:T(2,128)(2,1)S(1)} all-to-all(bf16[2,6,64,256]{3,0,1,2:T(2,128)(2,1)S(1)} %copy.97), channel_id=1, replica_groups=mesh['dp'=16,'rows'=2] {'dp'}, dimensions={2} | all-to-all | bytes 786432 | tf_op jit(solution)/shard_map/all_to_all | solution.py:135
  374.1 0.9 copy.98
  (56 shorter events, 2.7 us)
Async XLA Ops:
  6.5 306.9 %copy-start = (bf16[1280,256]{1,0:T(8,128)(2,1)S(1)}, bf16[1280,256]{1,0:T(8,128)(2,1)}, u32[]{:S(2)}) copy-start(bf16[1280,256]{1,0:T(8,128)(2,1)} %param.18) | copy-start | bytes 1966084
  6.5 10.7 %copy-start.2 = (bf16[2,6,64,1024]{3,2,1,0:T(8,128)(2,1)S(1)}, bf16[2,6,64,1024]{3,2,1,0:T(8,128)(2,1)}, u32[]{:S(2)}) copy-start(bf16[2,6,64,1024]{3,2,1,0:T(8,128)(2,1)} %param.12) | copy-start | bytes 4718596
  6.5 10.7 %copy-start.6 = (bf16[1024,256]{1,0:T(8,128)(2,1)S(1)}, bf16[1024,256]{1,0:T(8,128)(2,1)}, u32[]{:S(2)}) copy-start(bf16[1024,256]{1,0:T(8,128)(2,1)} %param.16) | copy-start | bytes 1572868
  6.5 58.7 %all-gather.4.cloned.1.call-start = ((), (), s32[]{:S(2)}) async-start(), calls=%async_computation.1 | async-start | bytes 5013504 | tf_op jit(solution)/shard_map/all_gather | solution.py:95
  7.3 111.7 %all-gather.6.cloned.1.call-start = ((), (), s32[]{:S(2)}) async-start(), calls=%async_computation.2 | async-start | bytes 5013504 | tf_op jit(solution)/shard_map/all_gather | solution.py:96
  8.0 164.7 %all-gather.8.cloned.1.call-start = ((), (), s32[]{:S(2)}) async-start(), calls=%async_computation.3 | async-start | bytes 5013504 | tf_op jit(solution)/shard_map/all_gather | solution.py:97
  8.7 301.0 %all-reduce.22.cloned.1.call-start = ((), (), s32[]{:S(2)}) async-start(), calls=%async_computation.4 | async-start | bytes 131072 | tf_op jit(solution)/shard_map/psum | solution.py:114
  9.5 180.5 %copy-start.10 = (s32[2]{0:T(128)}, s32[2]{0:T(128)S(1)}, u32[]{:S(2)}) copy-start(s32[2]{0:T(128)S(1)} %dynamic-slice) | copy-start | bytes 28
  69.2 113.8 %collective-permute-start = (f32[2,6,64,256]{3,2,1,0:T(8,128)}, f32[2,6,64,256]{3,2,1,0:T(8,128)}, u32[]{:S(2)}, u32[]{:S(2)}) collective-permute-start(f32[2,6,64,256]{3,2,1,0:T(8,128)} %fusion.28), channel_id=1, source_target_pairs={} | collective-permute-start | bytes 2359304 | tf_op jit(solution)/shard_map/ppermute | solution.py:14
  74.7 109.3 %collective-permute-start.1 = (f32[2,6,64,256]{3,2,1,0:T(8,128)}, f32[2,6,64,256]{3,2,1,0:T(8,128)}, u32[]{:S(2)}, u32[]{:S(2)}) collective-permute-start(f32[2,6,64,256]{3,2,1,0:T(8,128)} %fusion.30), channel_id=1, source_target_pairs={} | collective-permute-start | bytes 2359304 | tf_op jit(solution)/shard_map/ppermute | solution.py:14
  122.9 63.2 %collective-permute-start.2 = (f32[2,6,64,256]{3,2,1,0:T(8,128)}, f32[2,6,64,256]{3,2,1,0:T(8,128)}, u32[]{:S(2)}, u32[]{:S(2)}) collective-permute-start(f32[2,6,64,256]{3,2,1,0:T(8,128)} %fusion.36), channel_id=1, source_target_pairs={} | collective-permute-start | bytes 2359304 | tf_op jit(solution)/shard_map/ppermute | solution.py:14
  128.3 57.7 %collective-permute-start.3 = (f32[2,6,64,256]{3,2,1,0:T(8,128)}, f32[2,6,64,256]{3,2,1,0:T(8,128)}, u32[]{:S(2)}, u32[]{:S(2)}) collective-permute-start(f32[2,6,64,256]{3,2,1,0:T(8,128)} %fusion.38), channel_id=1, source_target_pairs={} | collective-permute-start | bytes 2359304 | tf_op jit(solution)/shard_map/ppermute | solution.py:14
  132.7 1.4 copy-start.4
  175.6 4.2 %slice-start = ((s8[4718592]{0:T(1024)(128)(4,1)}), s8[4194304]{0:T(1024)(128)(4,1)S(1)}, s32[]{:S(2)}) async-start(s8[4718592]{0:T(1024)(128)(4,1)} %bitcast.185), calls=%async_computation.5 | async-start | bytes 8388608
  175.7 4.1 %slice-start.1 = ((s8[4718592]{0:T(1024)(128)(4,1)}), s8[524288]{0:T(1024)(128)(4,1)S(1)}, s32[]{:S(2)}) async-start(s8[4718592]{0:T(1024)(128)(4,1)} %bitcast.185), calls=%async_computation.6 | async-start | bytes 1048576
  175.7 11.9 %collective-permute-start.4 = (f32[2,6,64,256]{3,2,1,0:T(8,128)S(1)}, f32[2,6,64,256]{3,2,1,0:T(8,128)S(1)}, u32[]{:S(2)}, u32[]{:S(2)}) collective-permute-start(f32[2,6,64,256]{3,2,1,0:T(8,128)S(1)} %fusion.44), channel_id=1, source_target_pairs={} | collective-permute-start | bytes 2359304 | tf_op jit(solution)/shard_map/ppermute | solution.py:14
  183.0 1.1 copy-start.3
  183.0 4.6 %collective-permute-start.5 = (f32[2,6,64,256]{3,2,1,0:T(8,128)S(1)}, f32[2,6,64,256]{3,2,1,0:T(8,128)S(1)}, u32[]{:S(2)}, u32[]{:S(2)}) collective-permute-start(f32[2,6,64,256]{3,2,1,0:T(8,128)S(1)} %fusion.46), channel_id=1, source_target_pairs={} | collective-permute-start | bytes 2359304 | tf_op jit(solution)/shard_map/ppermute | solution.py:14
  187.7 1.1 copy-start.1
  188.8 2.2 copy-start.5
  188.8 2.4 copy-start.7
  313.5 0.7 copy-start.11
  313.5 42.7 %copy-start.8 = (f32[256]{0:T(256)S(1)}, f32[256]{0:T(256)}, u32[]{:S(2)}) copy-start(f32[256]{0:T(256)} %param.22) | copy-start | bytes 3076
  313.5 42.7 %copy-start.9 = (f32[256]{0:T(256)S(1)}, f32[256]{0:T(256)}, u32[]{:S(2)}) copy-start(f32[256]{0:T(256)} %param.21) | copy-start | bytes 3076
Sparse Core Ops, SparseCore 0:
  9.5 55.6 all-gather.3
  67.4 51.4 all-gather.5
  121.1 51.4 all-gather.7
  191.1 118.6 all-reduce.21
where the time goes:
time: 382 us
  waiting for transfers between devices  247 us (65%)
  blocking collectives  64.4 us (17%)
  matrix products  29.5 us (8%)
  between operations  13.5 us (4%)
  other arithmetic  12 us (3%)
  starting transfers between devices  8.15 us (2%)
  local copies, waits for them, and re-layouts  7.13 us (2%)
    psum x1, waiting for transfers between devices, shards(): lax.psum((group_first, group_second), ('dp', 'rows'))  118 us
    all_gather x1, waiting for transfers between devices, shards(): lax.all_gather(first_atrous_weight, 'dp', axis=2, tiled=True)  46.5 us
    all_gather x1, waiting for transfers between devices, shards(): lax.all_gather(second_atrous_weight, 'dp', axis=2, tiled=True)  42.7 us
    psum x1, blocking collectives, project(): lax.psum((group_first, group_second), ('dp', 'rows'))  41.1 us
    all_gather x1, waiting for transfers between devices, shards(): lax.all_gather(third_atrous_weight, 'dp', axis=2, tiled=True)  37.6 us
    dot_general x9, matrix products, row_tap_list(): jnp.einsum('irwc,kco->irwko', block_tensor, kernel_row_slice, preferred_e...  22.5 us
    all_to_all x1, blocking collectives, shards(): lax.all_to_all(local_out, 'dp', split_axis=2, concat_axis=0, tiled=True)  17.3 us
    ppermute x6, starting transfers between devices, from_behind(): return lax.ppermute(array, axis, pairs)  8.03 us
  transfers between devices with their start and end apart: 10, of which 4 were waited for; matrix products, arithmetic and copies ran while one was open for 10% of the time, Pallas kernels for 0%

commit v1 on v0

v1 whole, which is shorter than its diff:
```python
import functools

import jax
import jax.numpy as jnp
from jax import lax
from jax.experimental import pallas as pl
from jax.experimental.pallas import tpu as pltpu
from jax.sharding import PartitionSpec as P

DILATIONS = (12, 24, 36)
VMEM = pltpu.VMEM
SMEM = pltpu.SMEM


def from_behind(array, axis, by):
    count = lax.axis_size(axis)
    pairs = [(i, i + by) for i in range(count) if 0 <= i + by < count]
    return lax.ppermute(array, axis, pairs)


def swap(array, axis, mask):
    return lax.ppermute(array, axis, [(i, i ^ mask) for i in range(lax.axis_size(axis))])


def masks_of(axis):
    size, mask, out = lax.axis_size(axis), 1, []
    while mask < size:
        out.append(mask)
        mask *= 2
    return out


def sum_over(array, axes):
    for axis in axes:
        size = lax.axis_size(axis)
        if size & (size - 1):
            array = lax.psum(array, axis)
            continue
        for mask in masks_of(axis):
            array = array + swap(array, axis, mask)
    return array


def tap_span(cols, shift):
    low = max(0, -shift) // 16 * 16
    high = min(cols, -(-(cols - max(0, shift)) // 16) * 16)
    return low, high


def moved(part, low, cols, shift):
    rows, wide, chans = part.shape
    if shift > 0:
        zeros = jnp.zeros((rows, shift, chans), part.dtype)
        return jnp.concatenate([zeros, part[:, : cols - shift]], axis=1)
    zeros = jnp.zeros((rows, -shift, chans), part.dtype)
    return jnp.concatenate([part[:, -shift - low :], zeros], axis=1)


def group_rows(groups, group, values):
    rows = lax.broadcasted_iota(jnp.int32, (groups, values.shape[-1]), 0)
    return jnp.where(rows == group, jnp.broadcast_to(values, rows.shape), 0.0)


def pick_row(table, group):
    rows = lax.broadcasted_iota(jnp.int32, table.shape, 0)
    return jnp.sum(jnp.where(rows == group, table, 0.0), axis=0, keepdims=True)


def conv_kernel(groups, n_blocks, owners, gids, x_ref, *rest):
    pieces, (pw_ref, pre_ref, stats_ref, w_ref) = rest[:n_blocks], rest[n_blocks:]
    images, rows, cols, chans = x_ref.shape
    outs = pw_ref.shape[1]
    depth = pieces[0].shape[2]
    at = 0
    for block in pieces:
        for j in range(block.shape[0]):
            start = pl.multiple_of(owners[at] * depth, depth)
            w_ref[:, pl.ds(start, depth), :] = block[j]
            at += 1
    stats_ref[...] = jnp.zeros_like(stats_ref)

    def product(x, w):
        r, c, _ = x.shape
        y = jnp.dot(x.reshape(r * c, chans), w, preferred_element_type=jnp.float32)
        return y.reshape(r, c, outs)

    def image(i, carry):
        group = gids[i]

        def emit(branch, value):
            span = pl.ds(branch * outs, outs)
            pre_ref[i, :, :, span] = value
            first = jnp.sum(value, axis=(0, 1)).reshape(1, outs)
            second = jnp.sum(value * value, axis=(0, 1)).reshape(1, outs)
            stats_ref[pl.ds(0, groups), span] += group_rows(groups, group, first)
            stats_ref[pl.ds(groups, groups), span] += group_rows(groups, group, second)

        emit(0, product(x_ref[i], pw_ref[...]))
        for k, dilation in enumerate(DILATIONS):
            total = product(x_ref[i], w_ref[3 * k + 1])
            for tap, shift in ((0, dilation), (2, -dilation)):
                if abs(shift) < cols:
                    low, high = tap_span(cols, shift)
                    part = product(x_ref[i, :, pl.ds(low, high - low), :], w_ref[3 * k + tap])
                    total = total + moved(part, low, cols, shift)
            emit(k + 1, total)
        return carry

    lax.fori_loop(0, images, image, 0)


def conv_and_stats(features, pieces, owners, own_groups, pointwise_weight, groups):
    images, rows, cols, chans = features.shape
    taps = pieces[0].shape[1]
    outs = pointwise_weight.shape[1]
    width = outs * (1 + len(DILATIONS))
    return pl.pallas_call(
        functools.partial(conv_kernel, groups, len(pieces)),
        out_shape=(
            jax.ShapeDtypeStruct((images, rows, cols, width), jnp.float32),
            jax.ShapeDtypeStruct((2 * groups, width), jnp.float32),
        ),
        in_specs=[pl.BlockSpec(memory_space=SMEM)] * 2
        + [pl.BlockSpec(memory_space=VMEM)] * (2 + len(pieces)),
        out_specs=(pl.BlockSpec(memory_space=VMEM),) * 2,
        scratch_shapes=[pltpu.VMEM((taps, chans, outs), pointwise_weight.dtype)],
        name="conv",
    )(owners, own_groups, features, *pieces, pointwise_weight)


def project_kernel(groups, count, gids, pre_ref, total_ref, gain_ref, shift_ref, w_ref, pool_ref, proj_ref, stats_ref):
    images, rows, cols, width = pre_ref.shape
    outs = w_ref.shape[1]
    stats_ref[...] = jnp.zeros_like(stats_ref)

    def image(i, carry):
        group = gids[i]
        mean = pick_row(total_ref[pl.ds(0, groups), :], group) / count
        var = pick_row(total_ref[pl.ds(groups, groups), :], group) / count - mean * mean
        inv = lax.rsqrt(var + 1e-05)
        pre = pre_ref[i].reshape(rows * cols, width)
        scaled = (pre - mean) * inv * gain_ref[...] + shift_ref[...]
        branches = jnp.maximum(scaled, 0.0).astype(w_ref.dtype)
        proj = jnp.dot(branches, w_ref[...], preferred_element_type=jnp.float32)
        proj = proj + pool_ref[pl.ds(i, 1), :]
        proj_ref[i] = proj.reshape(rows, cols, outs)
        first = jnp.sum(proj, axis=0, keepdims=True)
        second = jnp.sum(proj * proj, axis=0, keepdims=True)
        stats_ref[pl.ds(0, groups), :] += group_rows(groups, group, first)
        stats_ref[pl.ds(groups, groups), :] += group_rows(groups, group, second)
        return carry

    lax.fori_loop(0, images, image, 0)


def normed_project(pre, totals, own_groups, gain, shift, weight, pool_term, groups, count):
    images, rows, cols, _ = pre.shape
    outs = weight.shape[1]
    return pl.pallas_call(
        functools.partial(project_kernel, groups, count),
        out_shape=(
            jax.ShapeDtypeStruct((images, rows, cols, outs), jnp.float32),
            jax.ShapeDtypeStruct((2 * groups, outs), jnp.float32),
        ),
        in_specs=[pl.BlockSpec(memory_space=SMEM)] + [pl.BlockSpec(memory_space=VMEM)] * 6,
        out_specs=(pl.BlockSpec(memory_space=VMEM),) * 2,
        name="project",
    )(own_groups, pre, totals, gain, shift, weight, pool_term)


def gathered_pieces(own):
    size = lax.axis_size("dp")
    me = lax.axis_index("dp")
    quarter = size // 4
    far = [quarter * j for j in range(1, 4)]
    near = list(range(2, quarter, 2))
    line = {0: own}
    for mask in far:
        line[mask] = swap(own, "dp", mask)
    relayed = {}
    for mask in line:
        for other in near:
            relayed[mask ^ other] = swap(line[mask], "dp", other)
    early = [m for m in line] + [m for m in near]
    late = [m for m in relayed if m not in near]
    everything = {**line, **relayed}
    pieces, order = [], []
    for masks in (early, late):
        stack = jnp.stack([everything[m] for m in masks])
        pieces += [stack, swap(stack, "dp", 1)]
        order += [m for m in masks] + [m ^ 1 for m in masks]
    owners = jnp.stack([me ^ m for m in order]).astype(jnp.int32)
    return pieces, owners


def row_tap_list(block_tensor, kernel_row_slice, dilation_rate):
    partial_terms = jnp.einsum(
        "irwc,kco->irwko", block_tensor, kernel_row_slice, preferred_element_type=jnp.float32
    )
    map_width = block_tensor.shape[2]
    left = jnp.pad(partial_terms[:, :, :, 0], ((0, 0), (0, 0), (dilation_rate, 0), (0, 0)))
    right = jnp.pad(partial_terms[:, :, :, 2], ((0, 0), (0, 0), (0, dilation_rate), (0, 0)))
    return partial_terms[:, :, :, 1] + left[:, :, :map_width] + right[:, :, dilation_rate:]


def general_pre(features, kernels, pointwise_weight):
    branches = [
        jnp.einsum("irwc,co->irwo", features, pointwise_weight, preferred_element_type=jnp.float32)
    ]
    for kernel, dilation in zip(kernels, DILATIONS):
        whole = lax.all_gather(kernel, "dp", axis=2, tiled=True)
        total = row_tap_list(features, whole[1], dilation)
        step = dilation // features.shape[1]
        if step < lax.axis_size("rows"):
            for by, tap in ((step, 0), (-step, 2)):
                total = total + from_behind(row_tap_list(features, whole[tap], dilation), "rows", by)
        branches.append(total)
    return jnp.concatenate(branches, -1)


def shards(
    features,
    first_atrous_weight,
    second_atrous_weight,
    third_atrous_weight,
    pointwise_weight,
    pooling_weight,
    projection_weight,
    branch_norm_gain,
    branch_norm_shift,
    projection_norm_gain,
    projection_norm_shift,
    ghost_group_index,
):
    images, rows_dev, cols, chans = features.shape
    dp_size = lax.axis_size("dp")
    rows_size = lax.axis_size("rows")
    groups = images * dp_size // 4
    pixels = rows_dev * rows_size * cols
    count = 4.0 * pixels
    width = branch_norm_gain.size
    own_groups = lax.dynamic_slice_in_dim(
        ghost_group_index, lax.axis_index("dp") * images, images, 0
    )
    kernels = (first_atrous_weight, second_atrous_weight, third_atrous_weight)
    middle_only = all(d // rows_dev >= rows_size for d in DILATIONS)
    if middle_only and dp_size >= 8 and dp_size & (dp_size - 1) == 0:
        own = jnp.concatenate([kernel[1] for kernel in kernels], 0)
        pieces, owners = gathered_pieces(own)
        pre, stats = conv_and_stats(
            features, pieces, owners, own_groups, pointwise_weight, groups
        )
    else:
        pre = general_pre(features, kernels, pointwise_weight)
        hot = (own_groups[:, None] == jnp.arange(groups, dtype=jnp.int32)[None, :]).astype(jnp.float32)
        stats = jnp.concatenate(
            [
                jnp.dot(hot.T, jnp.sum(t, axis=(1, 2)), precision=lax.Precision.HIGHEST)
                for t in (pre, pre * pre)
            ],
            0,
        )
    pool_total = sum_over(jnp.sum(features, axis=(1, 2), dtype=jnp.float32), ("rows",))
    pooled = (pool_total / pixels).astype(jnp.bfloat16)
    pool_act = jax.nn.relu(
        jnp.dot(pooled, pooling_weight, preferred_element_type=jnp.float32)
    ).astype(jnp.bfloat16)
    pool_term = jnp.dot(pool_act, projection_weight[width:], preferred_element_type=jnp.float32)
    totals = sum_over(stats, ("dp", "rows"))
    proj, proj_stats = normed_project(
        pre,
        totals,
        own_groups,
        branch_norm_gain.reshape(1, -1),
        branch_norm_shift.reshape(1, -1),
        projection_weight[:width],
        pool_term,
        groups,
        count,
    )
    proj_totals = sum_over(proj_stats, ("dp", "rows"))
    hot = own_groups[:, None] == jnp.arange(groups, dtype=jnp.int32)[None, :]
    own_totals = jnp.sum(
        jnp.where(hot[None, :, :, None], proj_totals.reshape(2, 1, groups, -1), 0.0), axis=2
    )
    mean = own_totals[0] / count
    var = own_totals[1] / count - mean * mean
    inv = lax.rsqrt(var + 1e-05)
    scaled = (proj - mean[:, None, None, :]) * inv[:, None, None, :]
    scaled = scaled * projection_norm_gain + projection_norm_shift
    local_out = jax.nn.relu(scaled).astype(jnp.bfloat16)
    return lax.all_to_all(local_out, "dp", split_axis=2, concat_axis=0, tiled=True)


def solution(mesh):
    in_specs = (
        P("dp", "rows", None, None),
        P(None, None, "dp", None),
        P(None, None, "dp", None),
        P(None, None, "dp", None),
        P(),
        P(),
        P(),
        P(),
        P(),
        P(),
        P(),
        P(),
    )
    out_specs = P(None, "rows", "dp", None)
    return jax.shard_map(shards, mesh=mesh, in_specs=in_specs, out_specs=out_specs, check_vma=False)
```

time: 382 us -> 130 us (0.34)
  waiting for transfers between devices: 247 us -> 61.5 us
  blocking collectives: 64.4 us -> 15.6 us
  matrix products: 29.5 us -> 0.9 us
  starting transfers between devices: 8.15 us -> 27.1 us
  between operations: 13.5 us -> 0.22 us
  Pallas kernels: 0 us -> 12.9 us
  other arithmetic: 12 us -> 4.17 us
    all_gather x3 -> x0, waiting for transfers between devices: 127 us -> none  [the longest x1 46.5 us: shards(): lax.all_gather(first_atrous_weight, 'dp', axis=2, tiled=True)]
    psum x1 -> x0, waiting for transfers between devices: 118 us -> none  [shards(): lax.psum((group_first, group_second), ('dp', 'rows'))]
    ppermute x6 -> x20, waiting for transfers between devices: 0.02 us -> 61.5 us  [swap(): lax.ppermute(array, axis, [(i, i ^ mask) for i in range(lax.axis_size(axi...]
    psum x2 -> x0, blocking collectives: 47.1 us -> none  [the longest x1 41.1 us: project(): lax.psum((group_first, group_second), ('dp', 'rows'))]
    dot_general x20 -> x1, matrix products: 29.5 us -> 0.9 us  [shards(): jnp.dot(pool_act, projection_weight[width:], preferred_element_type=jnp.f...]
    ppermute x6 -> x20, starting transfers between devices: 8.03 us -> 27.1 us  [swap(): lax.ppermute(array, axis, [(i, i ^ mask) for i in range(lax.axis_size(axi...]
    pallas_call x0 -> x2, Pallas kernels: none -> 12.9 us  [the longest x1 8.89 us: conv_and_stats(): pl.pallas_call(functools.partial(conv_kernel, groups, len(pieces)), out_s...]
    add x9, other arithmetic: 8.03 us -> 2.25 us  [sum_over(): array = array + swap(array, axis, mask)]
  transfers between devices with their start and end apart: 10 -> 20, of which waited for: 4 -> 15; matrix products, arithmetic and copies ran while one was open for 10% -> 4% of each run, Pallas kernels for 0% -> 0%
where the time goes in v1:
time: 130 us; the launch traced here: 129 us
  waiting for transfers between devices  61.5 us (47%)
  starting transfers between devices  27.1 us (21%)
  blocking collectives  15.6 us (12%)
  Pallas kernels  12.9 us (10%)
  local copies, waits for them, and re-layouts  6.75 us (5%)
  other arithmetic  4.17 us (3%)
    ppermute x20, waiting for transfers between devices, swap(): lax.ppermute(array, axis, [(i, i ^ mask) for i in range(lax.axis_size(axi...  61.5 us
    ppermute x20, starting transfers between devices, swap(): lax.ppermute(array, axis, [(i, i ^ mask) for i in range(lax.axis_size(axi...  27.1 us
    all_to_all x1, blocking collectives, shards(): lax.all_to_all(local_out, 'dp', split_axis=2, concat_axis=0, tiled=True)  15.6 us
    pallas_call x1, Pallas kernels, conv_and_stats(): pl.pallas_call(functools.partial(conv_kernel, groups, len(pieces)), out_s...  8.89 us
    pallas_call x1, Pallas kernels, normed_project(): pl.pallas_call(functools.partial(project_kernel, groups, count), out_shap...  3.98 us
  transfers between devices with their start and end apart: 20, of which 15 were waited for; matrix products, arithmetic and copies ran while one was open for 4% of the time, Pallas kernels for 0%

profile of v1, /device:TPU:0, one launch (start us, length us, event | category | flops | bytes accessed | tf_op | source)
XLA Modules:
  0.0 129.2 jit_solution(10178952228731690435)
XLA Ops:
  0.0 1.0 slice_bitcast_fusion.2
  1.0 1.0 slice_bitcast_fusion
  2.0 3.1 %collective-permute-start = (bf16[9,64,256]{2,1,0:T(8,128)(2,1)S(1)}, bf16[9,64,256]{2,1,0:T(8,128)(2,1)S(1)}, u32[]{:S(2)}, u32[]{:S(2)}) collective-permute-start(bf16[9,64,256]{2,1,0:T(8,128)(2,1)S(1)} %pad_maximum_fusion.1), channel_id=1, source_target_pairs={{0,8},{2,10},{4,12},{6,14},{8,0},{10,2},{12,4},{14,6},{16,24},{18,... | collective-permute-start | bytes 884744 | tf_op jit(solution)/shard_map/ppermute | solution.py:22
  5.1 2.6 %collective-permute-start.1 = (bf16[9,64,256]{2,1,0:T(8,128)(2,1)S(1)}, bf16[9,64,256]{2,1,0:T(8,128)(2,1)S(1)}, u32[]{:S(2)}, u32[]{:S(2)}) collective-permute-start(bf16[9,64,256]{2,1,0:T(8,128)(2,1)S(1)} %pad_maximum_fusion.1), channel_id=1, source_target_pairs={{0,16},{2,18},{4,20},{6,22},{8,24},{10,26},{12,28},{14,30},{16,0},... | collective-permute-start | bytes 884744 | tf_op jit(solution)/shard_map/ppermute | solution.py:22
  7.7 1.7 %collective-permute-start.3 = (bf16[9,64,256]{2,1,0:T(8,128)(2,1)S(1)}, bf16[9,64,256]{2,1,0:T(8,128)(2,1)S(1)}, u32[]{:S(2)}, u32[]{:S(2)}) collective-permute-start(bf16[9,64,256]{2,1,0:T(8,128)(2,1)S(1)} %pad_maximum_fusion.1), channel_id=1, source_target_pairs={{0,4},{2,6},{4,0},{6,2},{8,12},{10,14},{12,8},{14,10},{16,20},{18,... | collective-permute-start | bytes 884744 | tf_op jit(solution)/shard_map/ppermute | solution.py:22
  9.4 8.3 %collective-permute-done = bf16[9,64,256]{2,1,0:T(8,128)(2,1)S(1)} collective-permute-done((bf16[9,64,256]{2,1,0:T(8,128)(2,1)S(1)}, bf16[9,64,256]{2,1,0:T(8,128)(2,1)S(1)}, u32[]{:S(2)}, u32[]{:S(2)}) %collective-permute-start) | collective-permute-done | bytes 294944 | tf_op jit(solution)/shard_map/ppermute | solution.py:22
  17.7 10.8 %collective-permute-done.1 = bf16[9,64,256]{2,1,0:T(8,128)(2,1)S(1)} collective-permute-done((bf16[9,64,256]{2,1,0:T(8,128)(2,1)S(1)}, bf16[9,64,256]{2,1,0:T(8,128)(2,1)S(1)}, u32[]{:S(2)}, u32[]{:S(2)}) %collective-permute-start.1) | collective-permute-done | bytes 294944 | tf_op jit(solution)/shard_map/ppermute | solution.py:22
  28.7 1.6 %collective-permute-start.5 = (bf16[9,64,256]{2,1,0:T(8,128)(2,1)S(1)}, bf16[9,64,256]{2,1,0:T(8,128)(2,1)S(1)}, u32[]{:S(2)}, u32[]{:S(2)}) collective-permute-start(bf16[9,64,256]{2,1,0:T(8,128)(2,1)S(1)} %collective-permute-done), channel_id=1, source_target_pairs={{0,4},{2,6},{4,0},{6,2},{8,12},{10,14},{12,8},{14,10},{16,20},{18,... | collective-permute-start | bytes 884744 | tf_op jit(solution)/shard_map/ppermute | solution.py:22
  30.3 0.5 collective-permute-start.6
  30.8 1.5 %collective-permute-start.7 = (bf16[9,64,256]{2,1,0:T(8,128)(2,1)S(1)}, bf16[9,64,256]{2,1,0:T(8,128)(2,1)S(1)}, u32[]{:S(2)}, u32[]{:S(2)}) collective-permute-start(bf16[9,64,256]{2,1,0:T(8,128)(2,1)S(1)} %collective-permute-done.2), channel_id=1, source_target_pairs={{0,4},{2,6},{4,0},{6,2},{8,12},{10,14},{12,8},{14,10},{16,20},{18,... | collective-permute-start | bytes 884744 | tf_op jit(solution)/shard_map/ppermute | solution.py:22
  32.3 6.4 %collective-permute-done.5 = bf16[9,64,256]{2,1,0:T(8,128)(2,1)S(1)} collective-permute-done((bf16[9,64,256]{2,1,0:T(8,128)(2,1)S(1)}, bf16[9,64,256]{2,1,0:T(8,128)(2,1)S(1)}, u32[]{:S(2)}, u32[]{:S(2)}) %collective-permute-start.5) | collective-permute-done | bytes 294944 | tf_op jit(solution)/shard_map/ppermute | solution.py:22
  38.7 6.3 %collective-permute-done.6 = bf16[9,64,256]{2,1,0:T(8,128)(2,1)S(1)} collective-permute-done((bf16[9,64,256]{2,1,0:T(8,128)(2,1)S(1)}, bf16[9,64,256]{2,1,0:T(8,128)(2,1)S(1)}, u32[]{:S(2)}, u32[]{:S(2)}) %collective-permute-start.6) | collective-permute-done | bytes 294944 | tf_op jit(solution)/shard_map/ppermute | solution.py:22
  45.0 5.8 %collective-permute-done.7 = bf16[9,64,256]{2,1,0:T(8,128)(2,1)S(1)} collective-permute-done((bf16[9,64,256]{2,1,0:T(8,128)(2,1)S(1)}, bf16[9,64,256]{2,1,0:T(8,128)(2,1)S(1)}, u32[]{:S(2)}, u32[]{:S(2)}) %collective-permute-start.7) | collective-permute-done | bytes 294944 | tf_op jit(solution)/shard_map/ppermute | solution.py:22
  51.0 0.7 dynamic_slice.3.gids
  51.7 0.7 stack.97.owners
  52.4 1.1 collective-permute-done.8.rest_3_
  53.5 8.9 %conv.1 = (f32[2,6,64,1024]{3,2,1,0:T(8,128)}, f32[16,1024]{1,0:T(8,128)}) custom-call(s32[16]{0:T(128)} %stack.97.owners, s32[2]{0:T(128)} %dynamic_slice.3.gids, bf16[2,6,64,1024]{3,2,1,0:T(8,128)(2,1)} %x_ref.1, bf16[5,9,64,256]{3,2,1,0:T(8,128)(2,1)} %copy-done.3, bf16[5,9,64,256]{3,2,1,0:T(8,128)(2,1)} %collective-permute-done.4.rest_1_, ...), custom_call_target="tpu_custom_call" | custom-call | tf_op jit(solution)/shard_map/conv/pallas_call | solution.py:117
  62.5 1.3 %collective-permute-done.9 = f32[16,1024]{1,0:T(8,128)S(1)} collective-permute-done((f32[16,1024]{1,0:T(8,128)}, f32[16,1024]{1,0:T(8,128)S(1)}, u32[]{:S(2)}, u32[]{:S(2)}) %collective-permute-start.9) | collective-permute-done | bytes 65568 | tf_op jit(solution)/shard_map/ppermute | solution.py:22
  63.9 0.9 add.55
  64.7 1.6 %collective-permute-start.10 = (f32[16,1024]{1,0:T(8,128)S(1)}, f32[16,1024]{1,0:T(8,128)S(1)}, u32[]{:S(2)}, u32[]{:S(2)}) collective-permute-start(f32[16,1024]{1,0:T(8,128)S(1)} %add.55), channel_id=1, source_target_pairs={{0,4},{2,6},{4,0},{6,2},{8,12},{10,14},{12,8},{14,10},{16,20},{18,... | collective-permute-start | bytes 196616 | tf_op jit(solution)/shard_map/ppermute | solution.py:22
  66.3 2.8 %collective-permute-done.10 = f32[16,1024]{1,0:T(8,128)S(1)} collective-permute-done((f32[16,1024]{1,0:T(8,128)S(1)}, f32[16,1024]{1,0:T(8,128)S(1)}, u32[]{:S(2)}, u32[]{:S(2)}) %collective-permute-start.10) | collective-permute-done | bytes 65568 | tf_op jit(solution)/shard_map/ppermute | solution.py:22
  69.1 5.5 %collective-permute-start.11 = (f32[16,1024]{1,0:T(8,128)S(1)}, f32[16,1024]{1,0:T(8,128)S(1)}, u32[]{:S(2)}, u32[]{:S(2)}) collective-permute-start(f32[16,1024]{1,0:T(8,128)S(1)} %add.56), channel_id=1, source_target_pairs={{0,8},{2,10},{4,12},{6,14},{8,0},{10,2},{12,4},{14,6},{16,24},{18,... | collective-permute-start | bytes 196616 | tf_op jit(solution)/shard_map/ppermute | solution.py:22
  74.6 2.2 %collective-permute-done.11 = f32[16,1024]{1,0:T(8,128)S(1)} collective-permute-done((f32[16,1024]{1,0:T(8,128)S(1)}, f32[16,1024]{1,0:T(8,128)S(1)}, u32[]{:S(2)}, u32[]{:S(2)}) %collective-permute-start.11) | collective-permute-done | bytes 65568 | tf_op jit(solution)/shard_map/ppermute | solution.py:22
  76.9 3.1 %collective-permute-start.12 = (f32[16,1024]{1,0:T(8,128)S(1)}, f32[16,1024]{1,0:T(8,128)S(1)}, u32[]{:S(2)}, u32[]{:S(2)}) collective-permute-start(f32[16,1024]{1,0:T(8,128)S(1)} %add.57), channel_id=1, source_target_pairs={{0,16},{2,18},{4,20},{6,22},{8,24},{10,26},{12,28},{14,30},{16,0},... | collective-permute-start | bytes 196616 | tf_op jit(solution)/shard_map/ppermute | solution.py:22
  80.0 0.3 convert_reduce_fusion
  80.3 1.6 %collective-permute-start.14 = (f32[2,1024]{1,0:T(2,128)S(1)}, f32[2,1024]{1,0:T(2,128)S(1)}, u32[]{:S(2)}, u32[]{:S(2)}) collective-permute-start(f32[2,1024]{1,0:T(2,128)S(1)} %convert_reduce_fusion), channel_id=1, source_target_pairs={{0,1},{1,0},{2,3},{3,2},{4,5},{5,4},{6,7},{7,6},{8,9},{9,8},{10,11... | collective-permute-start | bytes 24584 | tf_op jit(solution)/shard_map/ppermute | solution.py:22
  81.9 0.8 slice.24.w_ref
  82.7 0.6 copy.20
  83.3 0.6 copy.21
  83.9 0.6 collective-permute-start.13
  84.5 0.9 fusion.1.pool_ref
  85.4 2.9 %collective-permute-done.13 = f32[16,1024]{1,0:T(8,128)S(1)} collective-permute-done((f32[16,1024]{1,0:T(8,128)S(1)}, f32[16,1024]{1,0:T(8,128)S(1)}, u32[]{:S(2)}, u32[]{:S(2)}) %collective-permute-start.13) | collective-permute-done | bytes 65568 | tf_op jit(solution)/shard_map/ppermute | solution.py:22
  88.2 0.6 add.59.total_ref
  88.9 4.0 %project.1 = (f32[2,6,64,256]{3,2,1,0:T(8,128)}, f32[16,256]{1,0:T(8,128)}) custom-call(s32[2]{0:T(128)} %dynamic_slice.3.gids, f32[2,6,64,1024]{3,2,1,0:T(8,128)} %get-tuple-element.9.pre_ref, f32[16,1024]{1,0:T(8,128)} %add.59.total_ref, f32[1,1024]{1,0:T(1,128)} %bitcast.64, f32[1,1024]{1,0:T(1,128)} %bitcast.65, bf16[1024,256]{1,0:T(8,128)(2,1)} %slice.24.w_ref, ...), custom_call_target="tpu_custom_call" | custom-call | tf_op jit(solution)/shard_map/project/pallas_call | solution.py:159
  92.8 1.4 %collective-permute-done.15 = f32[16,256]{1,0:T(8,128)S(1)} collective-permute-done((f32[16,256]{1,0:T(8,128)}, f32[16,256]{1,0:T(8,128)S(1)}, u32[]{:S(2)}, u32[]{:S(2)}) %collective-permute-start.15) | collective-permute-done | bytes 16416 | tf_op jit(solution)/shard_map/ppermute | solution.py:22
  94.2 0.7 add.61
  95.0 1.5 %collective-permute-start.16 = (f32[16,256]{1,0:T(8,128)S(1)}, f32[16,256]{1,0:T(8,128)S(1)}, u32[]{:S(2)}, u32[]{:S(2)}) collective-permute-start(f32[16,256]{1,0:T(8,128)S(1)} %add.61), channel_id=1, source_target_pairs={{0,4},{2,6},{4,0},{6,2},{8,12},{10,14},{12,8},{14,10},{16,20},{18,... | collective-permute-start | bytes 49160 | tf_op jit(solution)/shard_map/ppermute | solution.py:22
  96.5 2.2 %collective-permute-done.16 = f32[16,256]{1,0:T(8,128)S(1)} collective-permute-done((f32[16,256]{1,0:T(8,128)S(1)}, f32[16,256]{1,0:T(8,128)S(1)}, u32[]{:S(2)}, u32[]{:S(2)}) %collective-permute-start.16) | collective-permute-done | bytes 16416 | tf_op jit(solution)/shard_map/ppermute | solution.py:22
  98.7 0.3 collective-permute-start.17
  99.0 3.5 %collective-permute-done.17 = f32[16,256]{1,0:T(8,128)S(1)} collective-permute-done((f32[16,256]{1,0:T(8,128)S(1)}, f32[16,256]{1,0:T(8,128)S(1)}, u32[]{:S(2)}, u32[]{:S(2)}) %collective-permute-start.17) | collective-permute-done | bytes 16416 | tf_op jit(solution)/shard_map/ppermute | solution.py:22
  102.5 1.3 collective-permute-start.18
  103.7 3.4 %collective-permute-done.18 = f32[16,256]{1,0:T(8,128)S(1)} collective-permute-done((f32[16,256]{1,0:T(8,128)S(1)}, f32[16,256]{1,0:T(8,128)S(1)}, u32[]{:S(2)}, u32[]{:S(2)}) %collective-permute-start.18) | collective-permute-done | bytes 16416 | tf_op jit(solution)/shard_map/ppermute | solution.py:22
  107.1 0.5 collective-permute-start.19
  107.7 3.2 %collective-permute-done.19 = f32[16,256]{1,0:T(8,128)S(1)} collective-permute-done((f32[16,256]{1,0:T(8,128)S(1)}, f32[16,256]{1,0:T(8,128)S(1)}, u32[]{:S(2)}, u32[]{:S(2)}) %collective-permute-start.19) | collective-permute-done | bytes 16416 | tf_op jit(solution)/shard_map/ppermute | solution.py:22
  111.0 1.3 maximum_convert_fusion
  112.3 0.4 copy.18
  112.7 15.6 %all_to_all.18 = bf16[2,6,64,256]{3,0,1,2:T(2,128)(2,1)S(1)} all-to-all(bf16[2,6,64,256]{3,0,1,2:T(2,128)(2,1)S(1)} %copy.18), channel_id=1, replica_groups=mesh['dp'=16,'rows'=2] {'dp'}, dimensions={2} | all-to-all | bytes 786432 | tf_op jit(solution)/shard_map/all_to_all | solution.py:292
  128.3 0.9 copy.19
  (50 shorter events, 0.8 us)
Async XLA Ops:
  0.0 84.5 %copy-start = (bf16[1024,256]{1,0:T(8,128)(2,1)S(1)}, bf16[1024,256]{1,0:T(8,128)(2,1)}, u32[]{:S(2)}) copy-start(bf16[1024,256]{1,0:T(8,128)(2,1)} %param.17) | copy-start | bytes 1572868
  2.0 15.7 %collective-permute-start = (bf16[9,64,256]{2,1,0:T(8,128)(2,1)S(1)}, bf16[9,64,256]{2,1,0:T(8,128)(2,1)S(1)}, u32[]{:S(2)}, u32[]{:S(2)}) collective-permute-start(bf16[9,64,256]{2,1,0:T(8,128)(2,1)S(1)} %pad_maximum_fusion.1), channel_id=1, source_target_pairs={{0,8},{2,10},{4,12},{6,14},{8,0},{10,2},{12,4},{14,6},{16,24},{18,... | collective-permute-start | bytes 884744 | tf_op jit(solution)/shard_map/ppermute | solution.py:22
  5.1 23.4 %collective-permute-start.1 = (bf16[9,64,256]{2,1,0:T(8,128)(2,1)S(1)}, bf16[9,64,256]{2,1,0:T(8,128)(2,1)S(1)}, u32[]{:S(2)}, u32[]{:S(2)}) collective-permute-start(bf16[9,64,256]{2,1,0:T(8,128)(2,1)S(1)} %pad_maximum_fusion.1), channel_id=1, source_target_pairs={{0,16},{2,18},{4,20},{6,22},{8,24},{10,26},{12,28},{14,30},{16,0},... | collective-permute-start | bytes 884744 | tf_op jit(solution)/shard_map/ppermute | solution.py:22
  7.7 20.9 %collective-permute-start.2 = (bf16[9,64,256]{2,1,0:T(8,128)(2,1)S(1)}, bf16[9,64,256]{2,1,0:T(8,128)(2,1)S(1)}, u32[]{:S(2)}, u32[]{:S(2)}) collective-permute-start(bf16[9,64,256]{2,1,0:T(8,128)(2,1)S(1)} %pad_maximum_fusion.1), channel_id=1, source_target_pairs={{0,24},{2,26},{4,28},{6,30},{8,16},{10,18},{12,20},{14,22},{16,8},... | collective-permute-start | bytes 884744 | tf_op jit(solution)/shard_map/ppermute | solution.py:22
  7.7 20.9 %collective-permute-start.3 = (bf16[9,64,256]{2,1,0:T(8,128)(2,1)S(1)}, bf16[9,64,256]{2,1,0:T(8,128)(2,1)S(1)}, u32[]{:S(2)}, u32[]{:S(2)}) collective-permute-start(bf16[9,64,256]{2,1,0:T(8,128)(2,1)S(1)} %pad_maximum_fusion.1), channel_id=1, source_target_pairs={{0,4},{2,6},{4,0},{6,2},{8,12},{10,14},{12,8},{14,10},{16,20},{18,... | collective-permute-start | bytes 884744 | tf_op jit(solution)/shard_map/ppermute | solution.py:22
  28.5 22.4 %copy-start.10 = (s32[32]{0:T(128)S(1)}, s32[32]{0:T(128)}, u32[]{:S(2)}) copy-start(s32[32]{0:T(128)} %param.23) | copy-start | bytes 388
  28.6 24.9 %copy-start.3 = (bf16[5,9,64,256]{3,2,1,0:T(8,128)(2,1)}, bf16[5,9,64,256]{3,2,1,0:T(8,128)(2,1)S(1)}, u32[]{:S(2)}) copy-start(bf16[5,9,64,256]{3,2,1,0:T(8,128)(2,1)S(1)} %bitcast_dynamic-update-slice_fusion.rest_0_) | copy-start | bytes 4423684
  28.6 24.9 %collective-permute-start.4 = (bf16[5,9,64,256]{3,2,1,0:T(8,128)(2,1)S(1)}, bf16[5,9,64,256]{3,2,1,0:T(8,128)(2,1)}, u32[]{:S(2)}, u32[]{:S(2)}) collective-permute-start(bf16[5,9,64,256]{3,2,1,0:T(8,128)(2,1)S(1)} %bitcast_dynamic-update-slice_fusion.rest_0_), channel_id=1, source_target_pairs={{0,2},{2,0},{4,6},{6,4},{8,10},{10,8},{12,14},{14,12},{16,18},{18,... | collective-permute-start | bytes 4423688 | tf_op jit(solution)/shard_map/ppermute | solution.py:22
  28.7 9.9 %collective-permute-start.5 = (bf16[9,64,256]{2,1,0:T(8,128)(2,1)S(1)}, bf16[9,64,256]{2,1,0:T(8,128)(2,1)S(1)}, u32[]{:S(2)}, u32[]{:S(2)}) collective-permute-start(bf16[9,64,256]{2,1,0:T(8,128)(2,1)S(1)} %collective-permute-done), channel_id=1, source_target_pairs={{0,4},{2,6},{4,0},{6,2},{8,12},{10,14},{12,8},{14,10},{16,20},{18,... | collective-permute-start | bytes 884744 | tf_op jit(solution)/shard_map/ppermute | solution.py:22
  30.3 14.7 %collective-permute-start.6 = (bf16[9,64,256]{2,1,0:T(8,128)(2,1)S(1)}, bf16[9,64,256]{2,1,0:T(8,128)(2,1)S(1)}, u32[]{:S(2)}, u32[]{:S(2)}) collective-permute-start(bf16[9,64,256]{2,1,0:T(8,128)(2,1)S(1)} %collective-permute-done.1), channel_id=1, source_target_pairs={{0,4},{2,6},{4,0},{6,2},{8,12},{10,14},{12,8},{14,10},{16,20},{18,... | collective-permute-start | bytes 884744 | tf_op jit(solution)/shard_map/ppermute | solution.py:22
  30.8 20.0 %collective-permute-start.7 = (bf16[9,64,256]{2,1,0:T(8,128)(2,1)S(1)}, bf16[9,64,256]{2,1,0:T(8,128)(2,1)S(1)}, u32[]{:S(2)}, u32[]{:S(2)}) collective-permute-start(bf16[9,64,256]{2,1,0:T(8,128)(2,1)S(1)} %collective-permute-done.2), channel_id=1, source_target_pairs={{0,4},{2,6},{4,0},{6,2},{8,12},{10,14},{12,8},{14,10},{16,20},{18,... | collective-permute-start | bytes 884744 | tf_op jit(solution)/shard_map/ppermute | solution.py:22
  50.9 2.6 %copy-start.2 = (bf16[3,9,64,256]{3,2,1,0:T(8,128)(2,1)}, bf16[3,9,64,256]{3,2,1,0:T(8,128)(2,1)S(1)}, u32[]{:S(2)}) copy-start(bf16[3,9,64,256]{3,2,1,0:T(8,128)(2,1)S(1)} %pad_maximum_fusion.rest_2_) | copy-start | bytes 2654212
  50.9 2.6 %collective-permute-start.8 = (bf16[3,9,64,256]{3,2,1,0:T(8,128)(2,1)S(1)}, bf16[3,9,64,256]{3,2,1,0:T(8,128)(2,1)}, u32[]{:S(2)}, u32[]{:S(2)}) collective-permute-start(bf16[3,9,64,256]{3,2,1,0:T(8,128)(2,1)S(1)} %pad_maximum_fusion.rest_2_), channel_id=1, source_target_pairs={{0,2},{2,0},{4,6},{6,4},{8,10},{10,8},{12,14},{14,12},{16,18},{18,... | collective-permute-start | bytes 2654216 | tf_op jit(solution)/shard_map/ppermute | solution.py:22
  53.5 26.5 %copy-start.1 = (bf16[2,6,64,1024]{3,2,1,0:T(8,128)(2,1)S(1)}, bf16[2,6,64,1024]{3,2,1,0:T(8,128)(2,1)}, u32[]{:S(2)}) copy-start(bf16[2,6,64,1024]{3,2,1,0:T(8,128)(2,1)} %x_ref.1) | copy-start | bytes 4718596
  62.4 19.4 %copy-start.4 = (bf16[1280,256]{1,0:T(8,128)(2,1)S(1)}, bf16[1280,256]{1,0:T(8,128)(2,1)}, u32[]{:S(2)}) copy-start(bf16[1280,256]{1,0:T(8,128)(2,1)} %param.18) | copy-start | bytes 1966084
  62.4 1.5 %collective-permute-start.9 = (f32[16,1024]{1,0:T(8,128)}, f32[16,1024]{1,0:T(8,128)S(1)}, u32[]{:S(2)}, u32[]{:S(2)}) collective-permute-start(f32[16,1024]{1,0:T(8,128)} %get-tuple-element.10), channel_id=1, source_target_pairs={{0,2},{2,0},{4,6},{6,4},{8,10},{10,8},{12,14},{14,12},{16,18},{18,... | collective-permute-start | bytes 196616 | tf_op jit(solution)/shard_map/ppermute | solution.py:22
  64.7 18.0 %copy-start.5 = (f32[4,256]{1,0:T(4,128)S(1)}, f32[4,256]{1,0:T(4,128)}, u32[]{:S(2)}) copy-start(f32[4,256]{1,0:T(4,128)} %param.19) | copy-start | bytes 12292
  64.7 18.5 %copy-start.6 = (f32[4,256]{1,0:T(4,128)S(1)}, f32[4,256]{1,0:T(4,128)}, u32[]{:S(2)}) copy-start(f32[4,256]{1,0:T(4,128)} %param.20) | copy-start | bytes 12292
  64.7 4.3 %collective-permute-start.10 = (f32[16,1024]{1,0:T(8,128)S(1)}, f32[16,1024]{1,0:T(8,128)S(1)}, u32[]{:S(2)}, u32[]{:S(2)}) collective-permute-start(f32[16,1024]{1,0:T(8,128)S(1)} %add.55), channel_id=1, source_target_pairs={{0,4},{2,6},{4,0},{6,2},{8,12},{10,14},{12,8},{14,10},{16,20},{18,... | collective-permute-start | bytes 196616 | tf_op jit(solution)/shard_map/ppermute | solution.py:22
  69.1 7.8 %collective-permute-start.11 = (f32[16,1024]{1,0:T(8,128)S(1)}, f32[16,1024]{1,0:T(8,128)S(1)}, u32[]{:S(2)}, u32[]{:S(2)}) collective-permute-start(f32[16,1024]{1,0:T(8,128)S(1)} %add.56), channel_id=1, source_target_pairs={{0,8},{2,10},{4,12},{6,14},{8,0},{10,2},{12,4},{14,6},{16,24},{18,... | collective-permute-start | bytes 196616 | tf_op jit(solution)/shard_map/ppermute | solution.py:22
  76.9 7.0 %collective-permute-start.12 = (f32[16,1024]{1,0:T(8,128)S(1)}, f32[16,1024]{1,0:T(8,128)S(1)}, u32[]{:S(2)}, u32[]{:S(2)}) collective-permute-start(f32[16,1024]{1,0:T(8,128)S(1)} %add.57), channel_id=1, source_target_pairs={{0,16},{2,18},{4,20},{6,22},{8,24},{10,26},{12,28},{14,30},{16,0},... | collective-permute-start | bytes 196616 | tf_op jit(solution)/shard_map/ppermute | solution.py:22
  80.3 4.2 %collective-permute-start.14 = (f32[2,1024]{1,0:T(2,128)S(1)}, f32[2,1024]{1,0:T(2,128)S(1)}, u32[]{:S(2)}, u32[]{:S(2)}) collective-permute-start(f32[2,1024]{1,0:T(2,128)S(1)} %convert_reduce_fusion), channel_id=1, source_target_pairs={{0,1},{1,0},{2,3},{3,2},{4,5},{5,4},{6,7},{7,6},{8,9},{9,8},{10,11... | collective-permute-start | bytes 24584 | tf_op jit(solution)/shard_map/ppermute | solution.py:22
  83.9 4.3 %collective-permute-start.13 = (f32[16,1024]{1,0:T(8,128)S(1)}, f32[16,1024]{1,0:T(8,128)S(1)}, u32[]{:S(2)}, u32[]{:S(2)}) collective-permute-start(f32[16,1024]{1,0:T(8,128)S(1)} %add.58), channel_id=1, source_target_pairs={{0,1},{1,0},{2,3},{3,2},{4,5},{5,4},{6,7},{7,6},{8,9},{9,8},{10,11... | collective-permute-start | bytes 196616 | tf_op jit(solution)/shard_map/ppermute | solution.py:22
  88.9 18.7 %copy-start.7 = (s32[2]{0:T(128)S(1)}, s32[2]{0:T(128)}, u32[]{:S(2)}) copy-start(s32[2]{0:T(128)} %dynamic_slice.3.gids) | copy-start | bytes 28
  88.9 22.1 %copy-start.8 = (f32[256]{0:T(256)S(1)}, f32[256]{0:T(256)}, u32[]{:S(2)}) copy-start(f32[256]{0:T(256)} %param.22) | copy-start | bytes 3076
  88.9 22.1 %copy-start.9 = (f32[256]{0:T(256)S(1)}, f32[256]{0:T(256)}, u32[]{:S(2)}) copy-start(f32[256]{0:T(256)} %param.21) | copy-start | bytes 3076
  92.8 1.4 %collective-permute-start.15 = (f32[16,256]{1,0:T(8,128)}, f32[16,256]{1,0:T(8,128)S(1)}, u32[]{:S(2)}, u32[]{:S(2)}) collective-permute-start(f32[16,256]{1,0:T(8,128)} %get-tuple-element.12), channel_id=1, source_target_pairs={{0,2},{2,0},{4,6},{6,4},{8,10},{10,8},{12,14},{14,12},{16,18},{18,... | collective-permute-start | bytes 49160 | tf_op jit(solution)/shard_map/ppermute | solution.py:22
  95.0 3.7 %collective-permute-start.16 = (f32[16,256]{1,0:T(8,128)S(1)}, f32[16,256]{1,0:T(8,128)S(1)}, u32[]{:S(2)}, u32[]{:S(2)}) collective-permute-start(f32[16,256]{1,0:T(8,128)S(1)} %add.61), channel_id=1, source_target_pairs={{0,4},{2,6},{4,0},{6,2},{8,12},{10,14},{12,8},{14,10},{16,20},{18,... | collective-permute-start | bytes 49160 | tf_op jit(solution)/shard_map/ppermute | solution.py:22
  98.7 3.7 %collective-permute-start.17 = (f32[16,256]{1,0:T(8,128)S(1)}, f32[16,256]{1,0:T(8,128)S(1)}, u32[]{:S(2)}, u32[]{:S(2)}) collective-permute-start(f32[16,256]{1,0:T(8,128)S(1)} %add.62), channel_id=1, source_target_pairs={{0,8},{2,10},{4,12},{6,14},{8,0},{10,2},{12,4},{14,6},{16,24},{18,... | collective-permute-start | bytes 49160 | tf_op jit(solution)/shard_map/ppermute | solution.py:22
  102.5 4.6 %collective-permute-start.18 = (f32[16,256]{1,0:T(8,128)S(1)}, f32[16,256]{1,0:T(8,128)S(1)}, u32[]{:S(2)}, u32[]{:S(2)}) collective-permute-start(f32[16,256]{1,0:T(8,128)S(1)} %add.63), channel_id=1, source_target_pairs={{0,16},{2,18},{4,20},{6,22},{8,24},{10,26},{12,28},{14,30},{16,0},... | collective-permute-start | bytes 49160 | tf_op jit(solution)/shard_map/ppermute | solution.py:22
  107.1 3.7 %collective-permute-start.19 = (f32[16,256]{1,0:T(8,128)S(1)}, f32[16,256]{1,0:T(8,128)S(1)}, u32[]{:S(2)}, u32[]{:S(2)}) collective-permute-start(f32[16,256]{1,0:T(8,128)S(1)} %add.64), channel_id=1, source_target_pairs={{0,1},{1,0},{2,3},{3,2},{4,5},{5,4},{6,7},{7,6},{8,9},{9,8},{10,11... | collective-permute-start | bytes 49160 | tf_op jit(solution)/shard_map/ppermute | solution.py:22

commit v2 on v1

v2 whole, which is shorter than its diff:
```python
import functools

import jax
import jax.numpy as jnp
from jax import lax
from jax.experimental import pallas as pl
from jax.experimental.pallas import tpu as pltpu
from jax.sharding import PartitionSpec as P

DILATIONS = (12, 24, 36)
VMEM = pltpu.VMEM
SMEM = pltpu.SMEM
VMEM_LIMIT = 26 * 2**20


def from_behind(array, axis, by):
    count = lax.axis_size(axis)
    pairs = [(i, i + by) for i in range(count) if 0 <= i + by < count]
    return lax.ppermute(array, axis, pairs)


def swap(array, axis, mask):
    return lax.ppermute(array, axis, [(i, i ^ mask) for i in range(lax.axis_size(axis))])


def masks_of(axis):
    size, mask, out = lax.axis_size(axis), 1, []
    while mask < size:
        out.append(mask)
        mask *= 2
    return out


def sum_over(array, axes):
    for axis in axes:
        size = lax.axis_size(axis)
        if size & (size - 1):
            array = lax.psum(array, axis)
            continue
        for mask in masks_of(axis):
            array = array + swap(array, axis, mask)
    return array


def tap_span(cols, shift):
    low = max(0, -shift) // 16 * 16
    high = min(cols, -(-(cols - max(0, shift)) // 16) * 16)
    return low, high


def moved(part, low, cols, shift):
    rows, _, chans = part.shape
    if shift > 0:
        zeros = jnp.zeros((rows, shift, chans), part.dtype)
        return jnp.concatenate([zeros, part[:, : cols - shift]], axis=1)
    zeros = jnp.zeros((rows, -shift, chans), part.dtype)
    return jnp.concatenate([part[:, -shift - low :], zeros], axis=1)


def group_rows(groups, group, values):
    rows = lax.broadcasted_iota(jnp.int32, (groups, values.shape[-1]), 0)
    return jnp.where(rows == group, jnp.broadcast_to(values, rows.shape), 0.0)


def pick_row(table, group):
    rows = lax.broadcasted_iota(jnp.int32, table.shape, 0)
    return jnp.sum(jnp.where(rows == group, table, 0.0), axis=0, keepdims=True)


def conv_kernel(groups, masks, opens, closes, index_ref, x_ref, own_ref, other_ref, *rest):
    if opens:
        pw_ref, pre_ref, *rest = rest
    else:
        done_ref, pre_ref, *rest = rest
    if closes:
        stats_ref, *rest = rest
        stats_ref[...] = jnp.zeros_like(stats_ref)
    w_ref, part_ref = rest
    images, _, cols, _ = x_ref.shape
    outs = w_ref.shape[2]
    depth = own_ref.shape[2]
    pair = 2 * depth
    me = lax.axis_index("dp")
    odd = lax.rem(lax.axis_index("rows"), 2)
    core = lax.rem(me, 2)
    here = pl.multiple_of(core * depth, depth)
    there = pl.multiple_of((1 - core) * depth, depth)
    for j, mask in enumerate(masks):
        w_ref[:, pl.ds(j * pair + here, depth), :] = own_ref[j]
        w_ref[:, pl.ds(j * pair + there, depth), :] = other_ref[j]
        mask = mask[0] + odd * (mask[1] - mask[0])
        block = pl.multiple_of((me ^ mask) // 2 * pair, pair)
        part_ref[:, :, :, pl.ds(j * pair, pair)] = x_ref[:, :, :, pl.ds(block, pair)]

    def product(x, w):
        r, c, k = x.shape
        y = jnp.dot(x.reshape(r * c, k), w, preferred_element_type=jnp.float32)
        return y.reshape(r, c, outs)

    def image(i, carry):
        group = index_ref[me * images + i]

        def emit(branch, value):
            span = pl.ds(branch * outs, outs)
            if branch == 0 and not opens:
                value = done_ref[i, :, :, span]
            elif not opens:
                value = value + done_ref[i, :, :, span]
            pre_ref[i, :, :, span] = value
            if closes:
                first = jnp.sum(value, axis=(0, 1)).reshape(1, outs)
                second = jnp.sum(value * value, axis=(0, 1)).reshape(1, outs)
                stats_ref[pl.ds(0, groups), span] += group_rows(groups, group, first)
                stats_ref[pl.ds(groups, groups), span] += group_rows(groups, group, second)

        if opens:
            emit(0, product(x_ref[i], pw_ref[...]))
        elif closes:
            emit(0, None)
        for k, dilation in enumerate(DILATIONS):
            total = product(part_ref[i], w_ref[3 * k + 1])
            for tap, shift in ((0, dilation), (2, -dilation)):
                if abs(shift) < cols:
                    low, high = tap_span(cols, shift)
                    part = product(part_ref[i, :, pl.ds(low, high - low), :], w_ref[3 * k + tap])
                    total = total + moved(part, low, cols, shift)
            emit(k + 1, total)
        return carry

    lax.fori_loop(0, images, image, 0)


def conv_part(features, stack, index, groups, opening=None, done=None, closes=False):
    masks, own, other = stack
    images, rows, cols, _ = features.shape
    _, taps, depth, outs = own.shape
    share = 2 * depth * len(masks)
    width = outs * (1 + len(DILATIONS))
    pre = jax.ShapeDtypeStruct((images, rows, cols, width), jnp.float32)
    stats = jax.ShapeDtypeStruct((2 * groups, width), jnp.float32)
    opens = done is None
    return pl.pallas_call(
        functools.partial(conv_kernel, groups, masks, opens, closes),
        out_shape=(pre, stats) if closes else (pre,),
        in_specs=[pl.BlockSpec(memory_space=SMEM)] + [pl.BlockSpec(memory_space=VMEM)] * 4,
        out_specs=(pl.BlockSpec(memory_space=VMEM),) * (2 if closes else 1),
        scratch_shapes=[
            pltpu.VMEM((taps, share, outs), own.dtype),
            pltpu.VMEM((images, rows, cols, share), features.dtype),
        ],
        input_output_aliases={} if opens else {4: 0},
        compiler_params=pltpu.CompilerParams(vmem_limit_bytes=VMEM_LIMIT),
    )(index, features, own, other, opening if opens else done)


def pick_kernel(*refs):
    *ins, out, sems = refs
    at, copies = 0, []
    for j, ref in enumerate(ins):
        copy = pltpu.make_async_copy(ref.at[1], out.at[pl.ds(at, ref.shape[1])], sems.at[j])
        copy.start()
        copies.append(copy)
        at += ref.shape[1]
    for copy in copies:
        copy.wait()


def middle_rows(kernels):
    _, taps, depth, outs = kernels[0].shape
    return pl.pallas_call(
        pick_kernel,
        out_shape=jax.ShapeDtypeStruct((taps * len(kernels), depth, outs), kernels[0].dtype),
        in_specs=[pl.BlockSpec(memory_space=pltpu.HBM)] * len(kernels),
        out_specs=pl.BlockSpec(memory_space=VMEM),
        scratch_shapes=[pltpu.SemaphoreType.DMA((len(kernels),))],
        compiler_params=pltpu.CompilerParams(vmem_limit_bytes=VMEM_LIMIT // 4),
        name="pick",
    )(*[pltpu.with_memory_space_constraint(kernel, pltpu.HBM) for kernel in kernels])


def project_kernel(groups, count, index_ref, pre_ref, total_ref, gain_ref, shift_ref, w_ref, pool_ref, proj_ref, stats_ref):
    images, rows, cols, width = pre_ref.shape
    outs = w_ref.shape[1]
    me = lax.axis_index("dp")
    stats_ref[...] = jnp.zeros_like(stats_ref)
    gain = jnp.concatenate([gain_ref[pl.ds(k, 1), :] for k in range(gain_ref.shape[0])], 1)
    shift = jnp.concatenate([shift_ref[pl.ds(k, 1), :] for k in range(shift_ref.shape[0])], 1)

    def image(i, carry):
        group = index_ref[me * images + i]
        mean = pick_row(total_ref[pl.ds(0, groups), :], group) / count
        var = pick_row(total_ref[pl.ds(groups, groups), :], group) / count - mean * mean
        inv = lax.rsqrt(var + 1e-05)
        pre = pre_ref[i].reshape(rows * cols, width)
        scaled = (pre - mean) * inv * gain + shift
        branches = jnp.maximum(scaled, 0.0).astype(w_ref.dtype)
        proj = jnp.dot(branches, w_ref[pl.ds(0, width), :], preferred_element_type=jnp.float32)
        proj = proj + pool_ref[pl.ds(i, 1), :]
        proj_ref[i] = proj.reshape(rows, cols, outs)
        first = jnp.sum(proj, axis=0, keepdims=True)
        second = jnp.sum(proj * proj, axis=0, keepdims=True)
        stats_ref[pl.ds(0, groups), :] += group_rows(groups, group, first)
        stats_ref[pl.ds(groups, groups), :] += group_rows(groups, group, second)
        return carry

    lax.fori_loop(0, images, image, 0)


def normed_project(pre, totals, index, gain, shift, weight, pool_term, groups, count):
    images, rows, cols, _ = pre.shape
    outs = weight.shape[1]
    return pl.pallas_call(
        functools.partial(project_kernel, groups, count),
        out_shape=(
            jax.ShapeDtypeStruct((images, rows, cols, outs), jnp.float32),
            jax.ShapeDtypeStruct((2 * groups, outs), jnp.float32),
        ),
        in_specs=[pl.BlockSpec(memory_space=SMEM)] + [pl.BlockSpec(memory_space=VMEM)] * 6,
        out_specs=(pl.BlockSpec(memory_space=VMEM),) * 2,
        compiler_params=pltpu.CompilerParams(vmem_limit_bytes=VMEM_LIMIT),
        name="project",
    )(index, pre, totals, gain, shift, weight, pool_term)


def both_cores(got, masks):
    stack = jnp.stack([got[m] for m in masks])
    return tuple(masks), stack, swap(stack, "dp", 1)


def far_swap(array, even, odd):
    count = lax.axis_size("rows")
    pairs = []
    for i in range(lax.axis_size("dp")):
        for j in range(count):
            k = i ^ (odd if j % 2 else even)
            pairs.append((i * count + j, k * count + j))
    return lax.ppermute(array, ("dp", "rows"), pairs)


def conv_branches(features, kernels, pointwise_weight, pool_term, index, groups):
    quarter = lax.axis_size("dp") // 4
    near = list(range(2, quarter, 2))
    one, two, three = quarter, 2 * quarter, 3 * quarter
    own = middle_rows(kernels)
    both, first, second = (one, one), (two, three), (three, two)

    def by(share, mask):
        return tuple(m ^ mask for m in share)

    got = {(0, 0): own}
    got[first] = far_swap(own, *first)
    got[both] = swap(own, "dp", one)
    for mask in near:
        got[(mask, mask)] = swap(own, "dp", mask)
    for mask in near:
        got[by(first, mask)] = swap(got[first], "dp", mask)
    got[second] = swap(got[first], "rows", 1)
    for mask in near:
        got[by(both, mask)] = swap(got[both], "dp", mask)
    masks, *stack = both_cores(got, [(0, 0), both] + [(m, m) for m in near])
    stack, pool_term = lax.optimization_barrier((stack, pool_term))
    (done,) = conv_part(features, (masks, *stack), index, groups, pointwise_weight)
    for mask in near:
        late = by(first, mask)
        got[late], done = lax.optimization_barrier((got[late], done))
        got[by(second, mask)] = swap(got[late], "rows", 1)
    middle = [first, second] + [by(both, m) for m in near] + [by(first, m) for m in near]
    last = [by(second, m) for m in near]
    (done,) = conv_part(features, both_cores(got, middle), index, groups, done=done)
    pre, stats = conv_part(features, both_cores(got, last), index, groups, done=done, closes=True)
    return pre, stats, pool_term


def row_tap_list(block_tensor, kernel_row_slice, dilation_rate):
    partial_terms = jnp.einsum(
        "irwc,kco->irwko", block_tensor, kernel_row_slice, preferred_element_type=jnp.float32
    )
    map_width = block_tensor.shape[2]
    left = jnp.pad(partial_terms[:, :, :, 0], ((0, 0), (0, 0), (dilation_rate, 0), (0, 0)))
    right = jnp.pad(partial_terms[:, :, :, 2], ((0, 0), (0, 0), (0, dilation_rate), (0, 0)))
    return partial_terms[:, :, :, 1] + left[:, :, :map_width] + right[:, :, dilation_rate:]


def general_pre(features, kernels, pointwise_weight):
    branches = [
        jnp.einsum("irwc,co->irwo", features, pointwise_weight, preferred_element_type=jnp.float32)
    ]
    for kernel, dilation in zip(kernels, DILATIONS):
        whole = lax.all_gather(kernel, "dp", axis=2, tiled=True)
        total = row_tap_list(features, whole[1], dilation)
        step = dilation // features.shape[1]
        if step < lax.axis_size("rows"):
            for by, tap in ((step, 0), (-step, 2)):
                total = total + from_behind(row_tap_list(features, whole[tap], dilation), "rows", by)
        branches.append(total)
    return jnp.concatenate(branches, -1)


def shards(
    features,
    first_atrous_weight,
    second_atrous_weight,
    third_atrous_weight,
    pointwise_weight,
    pooling_weight,
    projection_weight,
    branch_norm_gain,
    branch_norm_shift,
    projection_norm_gain,
    projection_norm_shift,
    ghost_group_index,
):
    images, rows_dev, cols, _ = features.shape
    dp_size = lax.axis_size("dp")
    rows_size = lax.axis_size("rows")
    groups = images * dp_size // 4
    pixels = rows_dev * rows_size * cols
    count = 4.0 * pixels
    width = branch_norm_gain.size
    own_groups = lax.dynamic_slice_in_dim(
        ghost_group_index, lax.axis_index("dp") * images, images, 0
    )
    kernels = (first_atrous_weight, second_atrous_weight, third_atrous_weight)
    pool_total = sum_over(jnp.sum(features, axis=(1, 2), dtype=jnp.float32), ("rows",))
    pooled = (pool_total / pixels).astype(jnp.bfloat16)
    pool_act = jax.nn.relu(
        jnp.dot(pooled, pooling_weight, preferred_element_type=jnp.float32)
    ).astype(jnp.bfloat16)
    pool_term = jnp.dot(pool_act, projection_weight[width:], preferred_element_type=jnp.float32)
    middle_only = all(d // rows_dev >= rows_size for d in DILATIONS)
    if middle_only and rows_size % 2 == 0 and dp_size >= 8 and dp_size & (dp_size - 1) == 0:
        pre, stats, pool_term = conv_branches(
            features, kernels, pointwise_weight, pool_term, ghost_group_index, groups
        )
    else:
        pre = general_pre(features, kernels, pointwise_weight)
        hot = (own_groups[:, None] == jnp.arange(groups, dtype=jnp.int32)[None, :]).astype(jnp.float32)
        stats = jnp.concatenate(
            [
                jnp.dot(hot.T, jnp.sum(t, axis=(1, 2)), precision=lax.Precision.HIGHEST)
                for t in (pre, pre * pre)
            ],
            0,
        )
    totals = sum_over(stats, ("dp", "rows"))
    proj, proj_stats = normed_project(
        pre,
        totals,
        ghost_group_index,
        branch_norm_gain,
        branch_norm_shift,
        projection_weight,
        pool_term,
        groups,
        count,
    )
    proj_totals = sum_over(proj_stats, ("dp", "rows"))
    hot = own_groups[:, None] == jnp.arange(groups, dtype=jnp.int32)[None, :]
    own_totals = jnp.sum(
        jnp.where(hot[None, :, :, None], proj_totals.reshape(2, 1, groups, -1), 0.0), axis=2
    )
    mean = own_totals[0] / count
    var = own_totals[1] / count - mean * mean
    inv = lax.rsqrt(var + 1e-05)
    scaled = (proj - mean[:, None, None, :]) * inv[:, None, None, :]
    scaled = scaled * projection_norm_gain + projection_norm_shift
    local_out = jax.nn.relu(scaled).astype(jnp.bfloat16)
    return lax.all_to_all(local_out, "dp", split_axis=2, concat_axis=0, tiled=True)


def solution(mesh):
    in_specs = (
        P("dp", "rows", None, None),
        P(None, None, "dp", None),
        P(None, None, "dp", None),
        P(None, None, "dp", None),
        P(),
        P(),
        P(),
        P(),
        P(),
        P(),
        P(),
        P(),
    )
    out_specs = P(None, "rows", "dp", None)

    return jax.shard_map(shards, mesh=mesh, in_specs=in_specs, out_specs=out_specs, check_vma=False)
```

time: 130 us -> 120 us (0.923)
  starting transfers between devices: 27.1 us -> 18 us
  waiting for transfers between devices: 61.5 us -> 67.3 us
  local copies, waits for them, and re-layouts: 6.75 us -> 1.5 us
  Pallas kernels: 12.9 us -> 11.3 us
    ppermute x0 -> x1, waiting for transfers between devices: none -> 13.9 us  [far_swap(): return lax.ppermute(array, ('dp', 'rows'), pairs)]
    ppermute x20, starting transfers between devices: 27.1 us -> 15.4 us  [swap(): lax.ppermute(array, axis, [(i, i ^ mask) for i in range(lax.axis_size(axi...]
    ppermute x20, waiting for transfers between devices: 61.5 us -> 53.4 us  [swap(): lax.ppermute(array, axis, [(i, i ^ mask) for i in range(lax.axis_size(axi...]
    ppermute x0 -> x1, starting transfers between devices: none -> 2.65 us  [far_swap(): return lax.ppermute(array, ('dp', 'rows'), pairs)]
    pallas_call x1, Pallas kernels: 3.98 us -> 1.58 us  [normed_project(): pl.pallas_call(functools.partial(project_kernel, groups, count), out_shap...]
    another operation x1 -> x2, other arithmetic: 0.1 us -> 2.44 us  [both_cores(): stack = jnp.stack([got[m] for m in masks])]
    add x9, other arithmetic: 2.25 us -> 0.06 us  [sum_over(): array = array + swap(array, axis, mask)]
    squeeze x2 -> x0, local copies, waits for them, and re-layouts: 1.91 us -> none  [shards(): own = jnp.concatenate([kernel[1] for kernel in kernels], 0)]
  transfers between devices with their start and end apart: 20 -> 21, of which waited for: 15 -> 15; matrix products, arithmetic and copies ran while one was open for 4% -> 1% of each run, Pallas kernels for 0% -> 6%
where the time goes in v2:
time: 120 us; the launch traced here: 119 us
  waiting for transfers between devices  67.3 us (56%)
  starting transfers between devices  18 us (15%)
  blocking collectives  16.6 us (14%)
  Pallas kernels  11.3 us (9%)
  other arithmetic  3.13 us (3%)
  local copies, waits for them, and re-layouts  1.5 us (1%)
    ppermute x20, waiting for transfers between devices, swap(): lax.ppermute(array, axis, [(i, i ^ mask) for i in range(lax.axis_size(axi...  53.4 us
    all_to_all x1, blocking collectives, shards(): lax.all_to_all(local_out, 'dp', split_axis=2, concat_axis=0, tiled=True)  16.6 us
    ppermute x20, starting transfers between devices, swap(): lax.ppermute(array, axis, [(i, i ^ mask) for i in range(lax.axis_size(axi...  15.4 us
    ppermute x1, waiting for transfers between devices, far_swap(): return lax.ppermute(array, ('dp', 'rows'), pairs)  13.9 us
    pallas_call x3, Pallas kernels, conv_part(): pl.pallas_call(functools.partial(conv_kernel, groups, masks, opens, close...  8.62 us
    ppermute x1, starting transfers between devices, far_swap(): return lax.ppermute(array, ('dp', 'rows'), pairs)  2.65 us
    another operation x2, other arithmetic, both_cores(): stack = jnp.stack([got[m] for m in masks])  2.44 us
  transfers between devices with their start and end apart: 21, of which 15 were waited for; matrix products, arithmetic and copies ran while one was open for 1% of the time, Pallas kernels for 6%

profile of v2, /device:TPU:0, one launch (start us, length us, event | category | flops | bytes accessed | tf_op | source)
XLA Modules:
  0.0 119.3 jit_solution(17617815604041721818)
XLA Ops:
  0.0 1.1 pick.1
  1.1 3.1 %collective-permute-start.2 = (bf16[9,64,256]{2,1,0:T(8,128)(2,1)S(1)}, bf16[9,64,256]{2,1,0:T(8,128)(2,1)}, u32[]{:S(2)}, u32[]{:S(2)}) collective-permute-start(bf16[9,64,256]{2,1,0:T(8,128)(2,1)S(1)} %pick.1), channel_id=1, source_target_pairs={{0,8},{2,10},{4,12},{6,14},{8,0},{10,2},{12,4},{14,6},{16,24},{18,... | collective-permute-start | bytes 884744 | tf_op jit(solution)/shard_map/ppermute | solution.py:23
  4.2 1.5 %collective-permute-start.3 = (bf16[9,64,256]{2,1,0:T(8,128)(2,1)S(1)}, bf16[9,64,256]{2,1,0:T(8,128)(2,1)S(1)}, u32[]{:S(2)}, u32[]{:S(2)}) collective-permute-start(bf16[9,64,256]{2,1,0:T(8,128)(2,1)S(1)} %pick.1), channel_id=1, source_target_pairs={{0,4},{2,6},{4,0},{6,2},{8,12},{10,14},{12,8},{14,10},{16,20},{18,... | collective-permute-start | bytes 884744 | tf_op jit(solution)/shard_map/ppermute | solution.py:23
  5.7 5.6 %collective-permute-done.2 = bf16[9,64,256]{2,1,0:T(8,128)(2,1)} collective-permute-done((bf16[9,64,256]{2,1,0:T(8,128)(2,1)S(1)}, bf16[9,64,256]{2,1,0:T(8,128)(2,1)}, u32[]{:S(2)}, u32[]{:S(2)}) %collective-permute-start.2) | collective-permute-done | bytes 294944 | tf_op jit(solution)/shard_map/ppermute | solution.py:23
  11.3 1.4 %collective-permute-done.3 = bf16[9,64,256]{2,1,0:T(8,128)(2,1)S(1)} collective-permute-done((bf16[9,64,256]{2,1,0:T(8,128)(2,1)S(1)}, bf16[9,64,256]{2,1,0:T(8,128)(2,1)S(1)}, u32[]{:S(2)}, u32[]{:S(2)}) %collective-permute-start.3) | collective-permute-done | bytes 294944 | tf_op jit(solution)/shard_map/ppermute | solution.py:23
  12.7 1.1 pad_maximum_fusion.1.own_ref
  13.8 0.1 collective-permute-start.4
  13.8 2.7 %collective-permute-start = (bf16[9,64,256]{2,1,0:T(8,128)(2,1)S(1)}, bf16[9,64,256]{2,1,0:T(8,128)(2,1)}, u32[]{:S(2)}, u32[]{:S(2)}) collective-permute-start(bf16[9,64,256]{2,1,0:T(8,128)(2,1)S(1)} %pick.1), channel_id=1, source_target_pairs={{0,16},{1,25},{2,18},{3,27},{4,20},{5,29},{6,22},{7,31},{8,24},{9,... | collective-permute-start | bytes 884744 | tf_op jit(solution)/shard_map/ppermute | solution.py:237
  16.5 13.9 %collective-permute-done = bf16[9,64,256]{2,1,0:T(8,128)(2,1)} collective-permute-done((bf16[9,64,256]{2,1,0:T(8,128)(2,1)S(1)}, bf16[9,64,256]{2,1,0:T(8,128)(2,1)}, u32[]{:S(2)}, u32[]{:S(2)}) %collective-permute-start) | collective-permute-done | bytes 294944 | tf_op jit(solution)/shard_map/ppermute | solution.py:237
  30.4 1.5 %collective-permute-start.1 = (bf16[9,64,256]{2,1,0:T(8,128)(2,1)}, bf16[9,64,256]{2,1,0:T(8,128)(2,1)}, u32[]{:S(2)}, u32[]{:S(2)}) collective-permute-start(bf16[9,64,256]{2,1,0:T(8,128)(2,1)} %collective-permute-done), channel_id=1, source_target_pairs={{0,4},{2,6},{4,0},{6,2},{8,12},{10,14},{12,8},{14,10},{16,20},{18,... | collective-permute-start | bytes 884744 | tf_op jit(solution)/shard_map/ppermute | solution.py:23
  32.0 0.5 collective-permute-start.9
  32.4 0.3 convert_reduce_fusion
  32.7 2.1 %collective-permute-start.5 = (f32[2,1024]{1,0:T(2,128)S(1)}, f32[2,1024]{1,0:T(2,128)S(1)}, u32[]{:S(2)}, u32[]{:S(2)}) collective-permute-start(f32[2,1024]{1,0:T(2,128)S(1)} %convert_reduce_fusion), channel_id=1, source_target_pairs={{0,1},{1,0},{2,3},{3,2},{4,5},{5,4},{6,7},{7,6},{8,9},{9,8},{10,11... | collective-permute-start | bytes 24584 | tf_op jit(solution)/shard_map/ppermute | solution.py:23
  34.8 6.2 %collective-permute-done.5 = f32[2,1024]{1,0:T(2,128)S(1)} collective-permute-done((f32[2,1024]{1,0:T(2,128)S(1)}, f32[2,1024]{1,0:T(2,128)S(1)}, u32[]{:S(2)}, u32[]{:S(2)}) %collective-permute-start.5) | collective-permute-done | bytes 8224 | tf_op jit(solution)/shard_map/ppermute | solution.py:23
  41.1 1.2 fusion.1.pool_ref
  42.3 3.7 %shard_map.118.rest_0_ = f32[2,6,64,1024]{3,2,1,0:T(8,128)S(1)} custom-call(s32[32]{0:T(128)S(1)} %copy-done.4, bf16[2,6,64,1024]{3,2,1,0:T(8,128)(2,1)S(1)} %copy-done.1, bf16[3,9,64,256]{3,2,1,0:T(8,128)(2,1)S(1)} %pad_maximum_fusion.1.own_ref, bf16[3,9,64,256]{3,2,1,0:T(8,128)(2,1)} %collective-permute-done.4.other_ref, bf16[1024,256]{1,0:T(8,128)(2,1)S(1)} %copy-done.3), custom_call_target="tpu_custom_call" | custom-call | tf_op jit(solution)/shard_map/pallas_call | solution.py:142
  46.1 1.4 %pad_maximum_fusion.own_ref = bf16[4,9,64,256]{3,2,1,0:T(8,128)(2,1)S(1)} fusion(bf16[1,9,64,256]{3,2,1,0:T(8,128)(2,1)} %bitcast.7, bf16[1,9,64,256]{3,2,1,0:T(8,128)(2,1)} %bitcast.6, bf16[1,9,64,256]{3,2,1,0:T(8,128)(2,1)} %bitcast.5, bf16[1,9,64,256]{3,2,1,0:T(8,128)(2,1)} %bitcast.4), kind=kLoop, calls=%fused_computation.1 | loop fusion | flops 1769472 | bytes 2359296 | tf_op jit(solution)/shard_map/stack | solution.py:226
  47.5 0.1 collective-permute-start.10
  47.5 0.4 collective-permute-start.6
  47.9 9.2 %collective-permute-done.6 = bf16[9,64,256]{2,1,0:T(8,128)(2,1)S(1)} collective-permute-done((bf16[9,64,256]{2,1,0:T(8,128)(2,1)}, bf16[9,64,256]{2,1,0:T(8,128)(2,1)S(1)}, u32[]{:S(2)}, u32[]{:S(2)}) %collective-permute-start.6) | collective-permute-done | bytes 294944 | tf_op jit(solution)/shard_map/ppermute | solution.py:23
  57.2 2.9 %shard_map.119.rest_0_ = f32[2,6,64,1024]{3,2,1,0:T(8,128)S(1)} custom-call(s32[32]{0:T(128)S(1)} %copy-done.4, bf16[2,6,64,1024]{3,2,1,0:T(8,128)(2,1)S(1)} %copy-done.1, bf16[4,9,64,256]{3,2,1,0:T(8,128)(2,1)S(1)} %pad_maximum_fusion.own_ref, bf16[4,9,64,256]{3,2,1,0:T(8,128)(2,1)S(1)} %collective-permute-done.10.other_ref, ...), custom_call_target="tpu_custom_call", output_to_operand_aliasing={{}: (4, {})} | custom-call | tf_op jit(solution)/shard_map/pallas_call | solution.py:142
  60.1 2.0 %shard_map.120 = (f32[2,6,64,1024]{3,2,1,0:T(8,128)S(1)}, f32[16,1024]{1,0:T(8,128)S(1)}) custom-call(s32[32]{0:T(128)S(1)} %copy-done.4, bf16[2,6,64,1024]{3,2,1,0:T(8,128)(2,1)S(1)} %copy-done.1, bf16[1,9,64,256]{3,2,1,0:T(8,128)(2,1)S(1)} %bitcast.29, ...), custom_call_target="tpu_custom_call", output_to_operand_aliasing={{0}: (4, {})} | custom-call | tf_op jit(solution)/shard_map/pallas_call | solution.py:142
  62.1 0.6 collective-permute-start.11
  62.7 0.9 collective-permute-done.11
  63.6 1.6 %collective-permute-start.12 = (f32[16,1024]{1,0:T(8,128)S(1)}, f32[16,1024]{1,0:T(8,128)S(1)}, u32[]{:S(2)}, u32[]{:S(2)}) collective-permute-start(f32[16,1024]{1,0:T(8,128)S(1)} %add.55), channel_id=1, source_target_pairs={{0,4},{2,6},{4,0},{6,2},{8,12},{10,14},{12,8},{14,10},{16,20},{18,... | collective-permute-start | bytes 196616 | tf_op jit(solution)/shard_map/ppermute | solution.py:23
  65.2 2.9 %collective-permute-done.12 = f32[16,1024]{1,0:T(8,128)S(1)} collective-permute-done((f32[16,1024]{1,0:T(8,128)S(1)}, f32[16,1024]{1,0:T(8,128)S(1)}, u32[]{:S(2)}, u32[]{:S(2)}) %collective-permute-start.12) | collective-permute-done | bytes 65568 | tf_op jit(solution)/shard_map/ppermute | solution.py:23
  68.0 0.3 collective-permute-start.13
  68.3 4.1 %collective-permute-done.13 = f32[16,1024]{1,0:T(8,128)S(1)} collective-permute-done((f32[16,1024]{1,0:T(8,128)S(1)}, f32[16,1024]{1,0:T(8,128)S(1)}, u32[]{:S(2)}, u32[]{:S(2)}) %collective-permute-start.13) | collective-permute-done | bytes 65568 | tf_op jit(solution)/shard_map/ppermute | solution.py:23
  72.4 1.2 collective-permute-start.14
  73.6 4.4 %collective-permute-done.14 = f32[16,1024]{1,0:T(8,128)S(1)} collective-permute-done((f32[16,1024]{1,0:T(8,128)S(1)}, f32[16,1024]{1,0:T(8,128)S(1)}, u32[]{:S(2)}, u32[]{:S(2)}) %collective-permute-start.14) | collective-permute-done | bytes 65568 | tf_op jit(solution)/shard_map/ppermute | solution.py:23
  78.0 0.1 collective-permute-start.15
  78.0 4.3 %collective-permute-done.15 = f32[16,1024]{1,0:T(8,128)S(1)} collective-permute-done((f32[16,1024]{1,0:T(8,128)S(1)}, f32[16,1024]{1,0:T(8,128)S(1)}, u32[]{:S(2)}, u32[]{:S(2)}) %collective-permute-start.15) | collective-permute-done | bytes 65568 | tf_op jit(solution)/shard_map/ppermute | solution.py:23
  82.4 1.6 %project.1 = (f32[2,6,64,256]{3,2,1,0:T(8,128)S(1)}, f32[16,256]{1,0:T(8,128)S(1)}) custom-call(s32[32]{0:T(128)S(1)} %copy-done.4, f32[2,6,64,1024]{3,2,1,0:T(8,128)S(1)} %get-tuple-element.18.pre_ref, f32[16,1024]{1,0:T(8,128)S(1)} %add.59.total_ref, f32[4,256]{1,0:T(4,128)S(1)} %copy-done.5, f32[4,256]{1,0:T(4,128)S(1)} %copy-done.6, ...), custom_call_target="tpu_custom_call" | custom-call | tf_op jit(solution)/shard_map/project/pallas_call | solution.py:212
  84.0 0.1 collective-permute-start.16
  84.0 1.2 collective-permute-done.16
  85.2 1.5 %collective-permute-start.17 = (f32[16,256]{1,0:T(8,128)S(1)}, f32[16,256]{1,0:T(8,128)S(1)}, u32[]{:S(2)}, u32[]{:S(2)}) collective-permute-start(f32[16,256]{1,0:T(8,128)S(1)} %add.61), channel_id=1, source_target_pairs={{0,4},{2,6},{4,0},{6,2},{8,12},{10,14},{12,8},{14,10},{16,20},{18,... | collective-permute-start | bytes 49160 | tf_op jit(solution)/shard_map/ppermute | solution.py:23
  86.7 2.3 %collective-permute-done.17 = f32[16,256]{1,0:T(8,128)S(1)} collective-permute-done((f32[16,256]{1,0:T(8,128)S(1)}, f32[16,256]{1,0:T(8,128)S(1)}, u32[]{:S(2)}, u32[]{:S(2)}) %collective-permute-start.17) | collective-permute-done | bytes 16416 | tf_op jit(solution)/shard_map/ppermute | solution.py:23
  89.0 3.7 %collective-permute-done.18 = f32[16,256]{1,0:T(8,128)S(1)} collective-permute-done((f32[16,256]{1,0:T(8,128)S(1)}, f32[16,256]{1,0:T(8,128)S(1)}, u32[]{:S(2)}, u32[]{:S(2)}) %collective-permute-start.18) | collective-permute-done | bytes 16416 | tf_op jit(solution)/shard_map/ppermute | solution.py:23
  92.7 0.9 collective-permute-start.19
  93.6 0.1 dynamic_slice.3
  93.7 3.6 %collective-permute-done.19 = f32[16,256]{1,0:T(8,128)S(1)} collective-permute-done((f32[16,256]{1,0:T(8,128)S(1)}, f32[16,256]{1,0:T(8,128)S(1)}, u32[]{:S(2)}, u32[]{:S(2)}) %collective-permute-start.19) | collective-permute-done | bytes 16416 | tf_op jit(solution)/shard_map/ppermute | solution.py:23
  97.3 0.1 iota_compare_fusion
  97.4 3.7 %collective-permute-done.20 = f32[16,256]{1,0:T(8,128)S(1)} collective-permute-done((f32[16,256]{1,0:T(8,128)S(1)}, f32[16,256]{1,0:T(8,128)S(1)}, u32[]{:S(2)}, u32[]{:S(2)}) %collective-permute-start.20) | collective-permute-done | bytes 16416 | tf_op jit(solution)/shard_map/ppermute | solution.py:23
  101.1 0.1 select_reduce_fusion
  101.2 0.1 maximum_convert_fusion
  101.4 0.4 copy.20
  101.8 16.6 %all_to_all.18 = bf16[2,6,64,256]{3,0,1,2:T(2,128)(2,1)S(1)} all-to-all(bf16[2,6,64,256]{3,0,1,2:T(2,128)(2,1)S(1)} %copy.20), channel_id=1, replica_groups=mesh['dp'=16,'rows'=2] {'dp'}, dimensions={2} | all-to-all | bytes 786432 | tf_op jit(solution)/shard_map/all_to_all | solution.py:368
  118.4 0.9 copy.21
  (40 shorter events, 0.2 us)
Async XLA Ops:
  0.0 41.1 %copy-start = (bf16[1024,256]{1,0:T(8,128)(2,1)S(1)}, bf16[1024,256]{1,0:T(8,128)(2,1)}, u32[]{:S(2)}) copy-start(bf16[1024,256]{1,0:T(8,128)(2,1)} %param.17) | copy-start | bytes 1572868
  1.1 31.4 %copy-start.1 = (bf16[2,6,64,1024]{3,2,1,0:T(8,128)(2,1)S(1)}, bf16[2,6,64,1024]{3,2,1,0:T(8,128)(2,1)}, u32[]{:S(2)}) copy-start(bf16[2,6,64,1024]{3,2,1,0:T(8,128)(2,1)} %x_ref.5) | copy-start | bytes 4718596
  1.1 10.2 %collective-permute-start.2 = (bf16[9,64,256]{2,1,0:T(8,128)(2,1)S(1)}, bf16[9,64,256]{2,1,0:T(8,128)(2,1)}, u32[]{:S(2)}, u32[]{:S(2)}) collective-permute-start(bf16[9,64,256]{2,1,0:T(8,128)(2,1)S(1)} %pick.1), channel_id=1, source_target_pairs={{0,8},{2,10},{4,12},{6,14},{8,0},{10,2},{12,4},{14,6},{16,24},{18,... | collective-permute-start | bytes 884744 | tf_op jit(solution)/shard_map/ppermute | solution.py:23
  4.2 8.5 %collective-permute-start.3 = (bf16[9,64,256]{2,1,0:T(8,128)(2,1)S(1)}, bf16[9,64,256]{2,1,0:T(8,128)(2,1)S(1)}, u32[]{:S(2)}, u32[]{:S(2)}) collective-permute-start(bf16[9,64,256]{2,1,0:T(8,128)(2,1)S(1)} %pick.1), channel_id=1, source_target_pairs={{0,4},{2,6},{4,0},{6,2},{8,12},{10,14},{12,8},{14,10},{16,20},{18,... | collective-permute-start | bytes 884744 | tf_op jit(solution)/shard_map/ppermute | solution.py:23
  13.7 28.5 %copy-start.3 = (bf16[1024,256]{1,0:T(8,128)(2,1)S(1)}, bf16[1024,256]{1,0:T(8,128)(2,1)}, u32[]{:S(2)}) copy-start(bf16[1024,256]{1,0:T(8,128)(2,1)} %rest_0_.1) | copy-start | bytes 1572868
  13.8 28.5 %copy-start.4 = (s32[32]{0:T(128)S(1)}, s32[32]{0:T(128)}, u32[]{:S(2)}) copy-start(s32[32]{0:T(128)} %index_ref.7) | copy-start | bytes 388
  13.8 28.5 %collective-permute-start.4 = (bf16[3,9,64,256]{3,2,1,0:T(8,128)(2,1)S(1)}, bf16[3,9,64,256]{3,2,1,0:T(8,128)(2,1)}, u32[]{:S(2)}, u32[]{:S(2)}) collective-permute-start(bf16[3,9,64,256]{3,2,1,0:T(8,128)(2,1)S(1)} %pad_maximum_fusion.1.own_ref), channel_id=1, source_target_pairs={{0,2},{2,0},{4,6},{6,4},{8,10},{10,8},{12,14},{14,12},{16,18},{18,... | collective-permute-start | bytes 2654216 | tf_op jit(solution)/shard_map/ppermute | solution.py:23
  13.8 16.6 %collective-permute-start = (bf16[9,64,256]{2,1,0:T(8,128)(2,1)S(1)}, bf16[9,64,256]{2,1,0:T(8,128)(2,1)}, u32[]{:S(2)}, u32[]{:S(2)}) collective-permute-start(bf16[9,64,256]{2,1,0:T(8,128)(2,1)S(1)} %pick.1), channel_id=1, source_target_pairs={{0,16},{1,25},{2,18},{3,27},{4,20},{5,29},{6,22},{7,31},{8,24},{9,... | collective-permute-start | bytes 884744 | tf_op jit(solution)/shard_map/ppermute | solution.py:237
  30.4 15.6 %collective-permute-start.1 = (bf16[9,64,256]{2,1,0:T(8,128)(2,1)}, bf16[9,64,256]{2,1,0:T(8,128)(2,1)}, u32[]{:S(2)}, u32[]{:S(2)}) collective-permute-start(bf16[9,64,256]{2,1,0:T(8,128)(2,1)} %collective-permute-done), channel_id=1, source_target_pairs={{0,4},{2,6},{4,0},{6,2},{8,12},{10,14},{12,8},{14,10},{16,20},{18,... | collective-permute-start | bytes 884744 | tf_op jit(solution)/shard_map/ppermute | solution.py:23
  32.0 14.1 %collective-permute-start.8 = (bf16[9,64,256]{2,1,0:T(8,128)(2,1)}, bf16[9,64,256]{2,1,0:T(8,128)(2,1)}, u32[]{:S(2)}, u32[]{:S(2)}) collective-permute-start(bf16[9,64,256]{2,1,0:T(8,128)(2,1)} %collective-permute-done), channel_id=1, source_target_pairs={{0,1},{1,0},{2,3},{3,2},{4,5},{5,4},{6,7},{7,6},{8,9},{9,8},{10,11... | collective-permute-start | bytes 884744 | tf_op jit(solution)/shard_map/ppermute | solution.py:23
  32.0 14.1 %collective-permute-start.9 = (bf16[9,64,256]{2,1,0:T(8,128)(2,1)}, bf16[9,64,256]{2,1,0:T(8,128)(2,1)}, u32[]{:S(2)}, u32[]{:S(2)}) collective-permute-start(bf16[9,64,256]{2,1,0:T(8,128)(2,1)} %collective-permute-done.2), channel_id=1, source_target_pairs={{0,4},{2,6},{4,0},{6,2},{8,12},{10,14},{12,8},{14,10},{16,20},{18,... | collective-permute-start | bytes 884744 | tf_op jit(solution)/shard_map/ppermute | solution.py:23
  32.7 8.3 %collective-permute-start.5 = (f32[2,1024]{1,0:T(2,128)S(1)}, f32[2,1024]{1,0:T(2,128)S(1)}, u32[]{:S(2)}, u32[]{:S(2)}) collective-permute-start(f32[2,1024]{1,0:T(2,128)S(1)} %convert_reduce_fusion), channel_id=1, source_target_pairs={{0,1},{1,0},{2,3},{3,2},{4,5},{5,4},{6,7},{7,6},{8,9},{9,8},{10,11... | collective-permute-start | bytes 24584 | tf_op jit(solution)/shard_map/ppermute | solution.py:23
  47.5 9.7 %collective-permute-start.10 = (bf16[4,9,64,256]{3,2,1,0:T(8,128)(2,1)S(1)}, bf16[4,9,64,256]{3,2,1,0:T(8,128)(2,1)S(1)}, u32[]{:S(2)}, u32[]{:S(2)}) collective-permute-start(bf16[4,9,64,256]{3,2,1,0:T(8,128)(2,1)S(1)} %pad_maximum_fusion.own_ref), channel_id=1, source_target_pairs={{0,2},{2,0},{4,6},{6,4},{8,10},{10,8},{12,14},{14,12},{16,18},{18,... | collective-permute-start | bytes 3538952 | tf_op jit(solution)/shard_map/ppermute | solution.py:23
  47.5 9.6 %collective-permute-start.6 = (bf16[9,64,256]{2,1,0:T(8,128)(2,1)}, bf16[9,64,256]{2,1,0:T(8,128)(2,1)S(1)}, u32[]{:S(2)}, u32[]{:S(2)}) collective-permute-start(bf16[9,64,256]{2,1,0:T(8,128)(2,1)} %collective-permute-done.1), channel_id=1, source_target_pairs={{0,1},{1,0},{2,3},{3,2},{4,5},{5,4},{6,7},{7,6},{8,9},{9,8},{10,11... | collective-permute-start | bytes 884744 | tf_op jit(solution)/shard_map/ppermute | solution.py:23
  57.2 2.9 %collective-permute-start.7 = (bf16[1,9,64,256]{3,2,1,0:T(8,128)(2,1)S(1)}, bf16[1,9,64,256]{3,2,1,0:T(8,128)(2,1)S(1)}, u32[]{:S(2)}, u32[]{:S(2)}) collective-permute-start(bf16[1,9,64,256]{3,2,1,0:T(8,128)(2,1)S(1)} %bitcast.28), channel_id=1, source_target_pairs={{0,2},{2,0},{4,6},{6,4},{8,10},{10,8},{12,14},{14,12},{16,18},{18,... | collective-permute-start | bytes 884744 | tf_op jit(solution)/shard_map/ppermute | solution.py:23
  60.1 22.2 %copy-start.5 = (f32[4,256]{1,0:T(4,128)S(1)}, f32[4,256]{1,0:T(4,128)}, u32[]{:S(2)}) copy-start(f32[4,256]{1,0:T(4,128)} %gain_ref.1) | copy-start | bytes 12292
  60.1 22.2 %copy-start.6 = (f32[4,256]{1,0:T(4,128)S(1)}, f32[4,256]{1,0:T(4,128)}, u32[]{:S(2)}) copy-start(f32[4,256]{1,0:T(4,128)} %shift_ref.1) | copy-start | bytes 12292
  62.1 20.2 %copy-start.2 = (bf16[1280,256]{1,0:T(8,128)(2,1)S(1)}, bf16[1280,256]{1,0:T(8,128)(2,1)}, u32[]{:S(2)}) copy-start(bf16[1280,256]{1,0:T(8,128)(2,1)} %w_ref.1) | copy-start | bytes 1966084
  62.1 1.5 %collective-permute-start.11 = (f32[16,1024]{1,0:T(8,128)S(1)}, f32[16,1024]{1,0:T(8,128)S(1)}, u32[]{:S(2)}, u32[]{:S(2)}) collective-permute-start(f32[16,1024]{1,0:T(8,128)S(1)} %get-tuple-element.19), channel_id=1, source_target_pairs={{0,2},{2,0},{4,6},{6,4},{8,10},{10,8},{12,14},{14,12},{16,18},{18,... | collective-permute-start | bytes 196616 | tf_op jit(solution)/shard_map/ppermute | solution.py:23
  63.6 4.4 %collective-permute-start.12 = (f32[16,1024]{1,0:T(8,128)S(1)}, f32[16,1024]{1,0:T(8,128)S(1)}, u32[]{:S(2)}, u32[]{:S(2)}) collective-permute-start(f32[16,1024]{1,0:T(8,128)S(1)} %add.55), channel_id=1, source_target_pairs={{0,4},{2,6},{4,0},{6,2},{8,12},{10,14},{12,8},{14,10},{16,20},{18,... | collective-permute-start | bytes 196616 | tf_op jit(solution)/shard_map/ppermute | solution.py:23
  68.0 4.3 %collective-permute-start.13 = (f32[16,1024]{1,0:T(8,128)S(1)}, f32[16,1024]{1,0:T(8,128)S(1)}, u32[]{:S(2)}, u32[]{:S(2)}) collective-permute-start(f32[16,1024]{1,0:T(8,128)S(1)} %add.56), channel_id=1, source_target_pairs={{0,8},{2,10},{4,12},{6,14},{8,0},{10,2},{12,4},{14,6},{16,24},{18,... | collective-permute-start | bytes 196616 | tf_op jit(solution)/shard_map/ppermute | solution.py:23
  72.4 5.6 %collective-permute-start.14 = (f32[16,1024]{1,0:T(8,128)S(1)}, f32[16,1024]{1,0:T(8,128)S(1)}, u32[]{:S(2)}, u32[]{:S(2)}) collective-permute-start(f32[16,1024]{1,0:T(8,128)S(1)} %add.57), channel_id=1, source_target_pairs={{0,16},{2,18},{4,20},{6,22},{8,24},{10,26},{12,28},{14,30},{16,0},... | collective-permute-start | bytes 196616 | tf_op jit(solution)/shard_map/ppermute | solution.py:23
  78.0 4.3 %collective-permute-start.15 = (f32[16,1024]{1,0:T(8,128)S(1)}, f32[16,1024]{1,0:T(8,128)S(1)}, u32[]{:S(2)}, u32[]{:S(2)}) collective-permute-start(f32[16,1024]{1,0:T(8,128)S(1)} %add.58), channel_id=1, source_target_pairs={{0,1},{1,0},{2,3},{3,2},{4,5},{5,4},{6,7},{7,6},{8,9},{9,8},{10,11... | collective-permute-start | bytes 196616 | tf_op jit(solution)/shard_map/ppermute | solution.py:23
  82.3 18.9 %copy-start.7 = (f32[256]{0:T(256)S(1)}, f32[256]{0:T(256)}, u32[]{:S(2)}) copy-start(f32[256]{0:T(256)} %param.22) | copy-start | bytes 3076
  82.3 18.9 %copy-start.8 = (f32[256]{0:T(256)S(1)}, f32[256]{0:T(256)}, u32[]{:S(2)}) copy-start(f32[256]{0:T(256)} %param.21) | copy-start | bytes 3076
  84.0 1.2 %collective-permute-start.16 = (f32[16,256]{1,0:T(8,128)S(1)}, f32[16,256]{1,0:T(8,128)S(1)}, u32[]{:S(2)}, u32[]{:S(2)}) collective-permute-start(f32[16,256]{1,0:T(8,128)S(1)} %get-tuple-element.22), channel_id=1, source_target_pairs={{0,2},{2,0},{4,6},{6,4},{8,10},{10,8},{12,14},{14,12},{16,18},{18,... | collective-permute-start | bytes 49160 | tf_op jit(solution)/shard_map/ppermute | solution.py:23
  85.2 3.7 %collective-permute-start.17 = (f32[16,256]{1,0:T(8,128)S(1)}, f32[16,256]{1,0:T(8,128)S(1)}, u32[]{:S(2)}, u32[]{:S(2)}) collective-permute-start(f32[16,256]{1,0:T(8,128)S(1)} %add.61), channel_id=1, source_target_pairs={{0,4},{2,6},{4,0},{6,2},{8,12},{10,14},{12,8},{14,10},{16,20},{18,... | collective-permute-start | bytes 49160 | tf_op jit(solution)/shard_map/ppermute | solution.py:23
  89.0 3.7 %collective-permute-start.18 = (f32[16,256]{1,0:T(8,128)S(1)}, f32[16,256]{1,0:T(8,128)S(1)}, u32[]{:S(2)}, u32[]{:S(2)}) collective-permute-start(f32[16,256]{1,0:T(8,128)S(1)} %add.62), channel_id=1, source_target_pairs={{0,8},{2,10},{4,12},{6,14},{8,0},{10,2},{12,4},{14,6},{16,24},{18,... | collective-permute-start | bytes 49160 | tf_op jit(solution)/shard_map/ppermute | solution.py:23
  92.7 4.6 %collective-permute-start.19 = (f32[16,256]{1,0:T(8,128)S(1)}, f32[16,256]{1,0:T(8,128)S(1)}, u32[]{:S(2)}, u32[]{:S(2)}) collective-permute-start(f32[16,256]{1,0:T(8,128)S(1)} %add.63), channel_id=1, source_target_pairs={{0,16},{2,18},{4,20},{6,22},{8,24},{10,26},{12,28},{14,30},{16,0},... | collective-permute-start | bytes 49160 | tf_op jit(solution)/shard_map/ppermute | solution.py:23
  97.3 3.7 %collective-permute-start.20 = (f32[16,256]{1,0:T(8,128)S(1)}, f32[16,256]{1,0:T(8,128)S(1)}, u32[]{:S(2)}, u32[]{:S(2)}) collective-permute-start(f32[16,256]{1,0:T(8,128)S(1)} %add.64), channel_id=1, source_target_pairs={{0,1},{1,0},{2,3},{3,2},{4,5},{5,4},{6,7},{7,6},{8,9},{9,8},{10,11... | collective-permute-start | bytes 49160 | tf_op jit(solution)/shard_map/ppermute | solution.py:23

commit v3 on v2

--- a/solution.py
+++ b/solution.py
@@ -67,7 +67,8 @@
     return jnp.sum(jnp.where(rows == group, table, 0.0), axis=0, keepdims=True)
 
 
-def conv_kernel(groups, masks, opens, closes, index_ref, x_ref, own_ref, other_ref, *rest):
+def conv_kernel(groups, masks, opens, closes, index_ref, x_ref, *rest):
+    shares, rest = rest[: 2 * len(masks)], rest[2 * len(masks) :]
     if opens:
         pw_ref, pre_ref, *rest = rest
     else:
@@ -78,7 +79,7 @@
     w_ref, part_ref = rest
     images, _, cols, _ = x_ref.shape
     outs = w_ref.shape[2]
-    depth = own_ref.shape[2]
+    depth = shares[0].shape[1]
     pair = 2 * depth
     me = lax.axis_index("dp")
     odd = lax.rem(lax.axis_index("rows"), 2)
@@ -86,8 +87,8 @@
     here = pl.multiple_of(core * depth, depth)
     there = pl.multiple_of((1 - core) * depth, depth)
     for j, mask in enumerate(masks):
-        w_ref[:, pl.ds(j * pair + here, depth), :] = own_ref[j]
-        w_ref[:, pl.ds(j * pair + there, depth), :] = other_ref[j]
+        w_ref[:, pl.ds(j * pair + here, depth), :] = shares[2 * j][...]
+        w_ref[:, pl.ds(j * pair + there, depth), :] = shares[2 * j + 1][...]
         mask = mask[0] + odd * (mask[1] - mask[0])
         block = pl.multiple_of((me ^ mask) // 2 * pair, pair)
         part_ref[:, :, :, pl.ds(j * pair, pair)] = x_ref[:, :, :, pl.ds(block, pair)]
@@ -130,27 +131,27 @@
     lax.fori_loop(0, images, image, 0)
 
 
-def conv_part(features, stack, index, groups, opening=None, done=None, closes=False):
-    masks, own, other = stack
+def conv_part(features, held, masks, index, groups, opening=None, done=None, closes=False):
+    shares = [share for mask in masks for share in held[mask]]
     images, rows, cols, _ = features.shape
-    _, taps, depth, outs = own.shape
+    taps, depth, outs = shares[0].shape
     share = 2 * depth * len(masks)
     width = outs * (1 + len(DILATIONS))
     pre = jax.ShapeDtypeStruct((images, rows, cols, width), jnp.float32)
     stats = jax.ShapeDtypeStruct((2 * groups, width), jnp.float32)
     opens = done is None
     return pl.pallas_call(
-        functools.partial(conv_kernel, groups, masks, opens, closes),
+        functools.partial(conv_kernel, groups, tuple(masks), opens, closes),
         out_shape=(pre, stats) if closes else (pre,),
-        in_specs=[pl.BlockSpec(memory_space=SMEM)] + [pl.BlockSpec(memory_space=VMEM)] * 4,
+        in_specs=[pl.BlockSpec(memory_space=SMEM)] + [pl.BlockSpec(memory_space=VMEM)] * (2 + len(shares)),
         out_specs=(pl.BlockSpec(memory_space=VMEM),) * (2 if closes else 1),
         scratch_shapes=[
-            pltpu.VMEM((taps, share, outs), own.dtype),
+            pltpu.VMEM((taps, share, outs), shares[0].dtype),
             pltpu.VMEM((images, rows, cols, share), features.dtype),
         ],
-        input_output_aliases={} if opens else {4: 0},
+        input_output_aliases={} if opens else {2 + len(shares): 0},
         compiler_params=pltpu.CompilerParams(vmem_limit_bytes=VMEM_LIMIT),
-    )(index, features, own, other, opening if opens else done)
+    )(index, features, *shares, opening if opens else done)
 
 
 def pick_kernel(*refs):
@@ -181,8 +182,8 @@
 def project_kernel(groups, count, index_ref, pre_ref, total_ref, gain_ref, shift_ref, w_ref, pool_ref, proj_ref, stats_ref):
     images, rows, cols, width = pre_ref.shape
     outs = w_ref.shape[1]
+    copies = stats_ref.shape[0]
     me = lax.axis_index("dp")
-    stats_ref[...] = jnp.zeros_like(stats_ref)
     gain = jnp.concatenate([gain_ref[pl.ds(k, 1), :] for k in range(gain_ref.shape[0])], 1)
     shift = jnp.concatenate([shift_ref[pl.ds(k, 1), :] for k in range(shift_ref.shape[0])], 1)
 
@@ -199,32 +200,65 @@
         proj_ref[i] = proj.reshape(rows, cols, outs)
         first = jnp.sum(proj, axis=0, keepdims=True)
         second = jnp.sum(proj * proj, axis=0, keepdims=True)
-        stats_ref[pl.ds(0, groups), :] += group_rows(groups, group, first)
-        stats_ref[pl.ds(groups, groups), :] += group_rows(groups, group, second)
+        stats_ref[:, pl.ds(2 * i, 1), :] = jnp.broadcast_to(first[None], (copies, 1, outs))
+        stats_ref[:, pl.ds(2 * i + 1, 1), :] = jnp.broadcast_to(second[None], (copies, 1, outs))
         return carry
 
-    lax.fori_loop(0, images, image, 0)
+    for i in range(images):
+        image(i, 0)
+
+
+def finish_kernel(count, index_ref, proj_ref, sums_ref, gain_ref, shift_ref, out_ref):
+    images, rows, cols, outs = proj_ref.shape
+    places, planes = sums_ref.shape[:2]
+    me = lax.axis_index("dp")
+    each = []
+    for p in range(places):
+        both = sums_ref[p, 0]
+        for r in range(1, planes):
+            both = both + sums_ref[p, r]
+        each.append(both)
+    for i in range(images):
+        group = index_ref[me * images + i]
+        total = jnp.zeros((2, outs), jnp.float32)
+        for p in range(places):
+            for k in range(images):
+                hit = index_ref[p * images + k] == group
+                total = total + jnp.where(hit, each[p][2 * k : 2 * k + 2], 0.0)
+        mean = total[0:1] / count
+        var = total[1:2] / count - mean * mean
+        inv = lax.rsqrt(var + 1e-05)
+        proj = proj_ref[i].reshape(rows * cols, outs)
+        scaled = (proj - mean) * inv * gain_ref[...] + shift_ref[...]
+        out_ref[i] = jnp.maximum(scaled, 0.0).astype(out_ref.dtype).reshape(rows, cols, outs)
+
+
+def finished(proj, sums, index, gain, shift, count):
+    return pl.pallas_call(
+        functools.partial(finish_kernel, count),
+        out_shape=jax.ShapeDtypeStruct(proj.shape, jnp.bfloat16),
+        in_specs=[pl.BlockSpec(memory_space=SMEM)] + [pl.BlockSpec(memory_space=VMEM)] * 4,
+        out_specs=pl.BlockSpec(memory_space=VMEM),
+        compiler_params=pltpu.CompilerParams(vmem_limit_bytes=VMEM_LIMIT),
+        name="finish",
+    )(index, proj, sums, gain, shift)
 
 
 def normed_project(pre, totals, index, gain, shift, weight, pool_term, groups, count):
     images, rows, cols, _ = pre.shape
     outs = weight.shape[1]
+    devices = lax.axis_size(("dp", "rows"))
     return pl.pallas_call(
         functools.partial(project_kernel, groups, count),
         out_shape=(
             jax.ShapeDtypeStruct((images, rows, cols, outs), jnp.float32),
-            jax.ShapeDtypeStruct((2 * groups, outs), jnp.float32),
+            jax.ShapeDtypeStruct((devices, 2 * images, outs), jnp.float32),
         ),
         in_specs=[pl.BlockSpec(memory_space=SMEM)] + [pl.BlockSpec(memory_space=VMEM)] * 6,
         out_specs=(pl.BlockSpec(memory_space=VMEM),) * 2,
         compiler_params=pltpu.CompilerParams(vmem_limit_bytes=VMEM_LIMIT),
         name="project",
     )(index, pre, totals, gain, shift, weight, pool_term)
-
-
-def both_cores(got, masks):
-    stack = jnp.stack([got[m] for m in masks])
-    return tuple(masks), stack, swap(stack, "dp", 1)
 
 
 def far_swap(array, even, odd):
@@ -247,27 +281,45 @@
     def by(share, mask):
         return tuple(m ^ mask for m in share)
 
-    got = {(0, 0): own}
+    origin = (0, 0)
+    beside = [(m, m) for m in near]
+    got, held = {origin: own}, {}
+
+    def pass_on(mask):
+        held[mask] = (got[mask], swap(got[mask], "dp", 1))
+
     got[first] = far_swap(own, *first)
     got[both] = swap(own, "dp", one)
-    for mask in near:
-        got[(mask, mask)] = swap(own, "dp", mask)
+    for mask in beside:
+        got[mask] = swap(own, "dp", mask[0])
+    pass_on(origin)
+    for mask in beside:
+        pass_on(mask)
+    held[origin], pool_term = lax.optimization_barrier((held[origin], pool_term))
+    opened = [origin] + beside
+    (done,) = conv_part(features, held, opened, index, groups, pointwise_weight)
     for mask in near:
         got[by(first, mask)] = swap(got[first], "dp", mask)
     got[second] = swap(got[first], "rows", 1)
     for mask in near:
         got[by(both, mask)] = swap(got[both], "dp", mask)
-    masks, *stack = both_cores(got, [(0, 0), both] + [(m, m) for m in near])
-    stack, pool_term = lax.optimization_barrier((stack, pool_term))
-    (done,) = conv_part(features, (masks, *stack), index, groups, pointwise_weight)
+    pass_on(first)
+    pass_on(both)
     for mask in near:
         late = by(first, mask)
         got[late], done = lax.optimization_barrier((got[late], done))
         got[by(second, mask)] = swap(got[late], "rows", 1)
-    middle = [first, second] + [by(both, m) for m in near] + [by(first, m) for m in near]
-    last = [by(second, m) for m in near]
-    (done,) = conv_part(features, both_cores(got, middle), index, groups, done=done)
-    pre, stats = conv_part(features, both_cores(got, last), index, groups, done=done, closes=True)
+    pass_on(second)
+    (done,) = conv_part(features, held, [first, both, second], index, groups, done=done)
+    last = []
+    for mask in near:
+        pass_on(by(first, mask))
+        late, final = by(both, mask), by(second, mask)
+        got[late], done = lax.optimization_barrier((got[late], done))
+        pass_on(late)
+        pass_on(final)
+        last += [by(first, mask), by(both, mask), final]
+    pre, stats = conv_part(features, held, last, index, groups, done=done, closes=True)
     return pre, stats, pool_term
 
 
@@ -354,17 +406,15 @@
         groups,
         count,
     )
-    proj_totals = sum_over(proj_stats, ("dp", "rows"))
-    hot = own_groups[:, None] == jnp.arange(groups, dtype=jnp.int32)[None, :]
-    own_totals = jnp.sum(
-        jnp.where(hot[None, :, :, None], proj_totals.reshape(2, 1, groups, -1), 0.0), axis=2
+    sums = lax.all_to_all(proj_stats, ("dp", "rows"), 0, 0, tiled=True)
+    local_out = finished(
+        proj,
+        sums.reshape(dp_size, rows_size, 2 * images, -1),
+        ghost_group_index,
+        projection_norm_gain.reshape(1, -1),
+        projection_norm_shift.reshape(1, -1),
+        count,
     )
-    mean = own_totals[0] / count
-    var = own_totals[1] / count - mean * mean
-    inv = lax.rsqrt(var + 1e-05)
-    scaled = (proj - mean[:, None, None, :]) * inv[:, None, None, :]
-    scaled = scaled * projection_norm_gain + projection_norm_shift
-    local_out = jax.nn.relu(scaled).astype(jnp.bfloat16)
     return lax.all_to_all(local_out, "dp", split_axis=2, concat_axis=0, tiled=True)
 
 

time: 120 us -> 96.5 us (0.80)
  waiting for transfers between devices: 67.3 us -> 34.2 us
  blocking collectives: 16.6 us -> 28.1 us
  other arithmetic: 3.13 us -> 1.75 us
    ppermute x20, waiting for transfers between devices: 53.4 us -> 25.8 us  [swap(): lax.ppermute(array, axis, [(i, i ^ mask) for i in range(lax.axis_size(axi...]
    all_to_all x0 -> x1, blocking collectives: none -> 13.3 us  [shards(): sums = lax.all_to_all(proj_stats, ('dp', 'rows'), 0, 0, tiled=True)]
    ppermute x1, waiting for transfers between devices: 13.9 us -> 8.38 us  [far_swap(): return lax.ppermute(array, ('dp', 'rows'), pairs)]
    another operation x2 -> x0, other arithmetic: 2.44 us -> none  [both_cores(): stack = jnp.stack([got[m] for m in masks])]
    all_to_all x1, blocking collectives: 16.6 us -> 14.8 us  [shards(): lax.all_to_all(local_out, 'dp', split_axis=2, concat_axis=0, tiled=True)]
    reduce_sum x1, other arithmetic: 0.3 us -> 1.7 us  [shards(): jnp.sum(features, axis=(1, 2), dtype=jnp.float32)]
    pallas_call x3 -> x4, Pallas kernels: 8.62 us -> 9.84 us  [the longest x3 9.05 us: conv_part(): pl.pallas_call(functools.partial(conv_kernel, groups, tuple(masks), opens...]
  transfers between devices with their start and end apart: 21 -> 21, of which waited for: 15 -> 11; matrix products, arithmetic and copies ran while one was open for 1% -> 3% of each run, Pallas kernels for 6% -> 6%
where the time goes in v3:
time: 96.5 us; the launch traced here: 96.3 us
  waiting for transfers between devices  34.2 us (35%)
  blocking collectives  28.1 us (29%)
  starting transfers between devices  17.1 us (18%)
  Pallas kernels  12.4 us (13%)
  other arithmetic  1.75 us (2%)
  local copies, waits for them, and re-layouts  1.35 us (1%)
  matrix products  1.17 us (1%)
    ppermute x20, waiting for transfers between devices, swap(): lax.ppermute(array, axis, [(i, i ^ mask) for i in range(lax.axis_size(axi...  25.8 us
    all_to_all x1, blocking collectives, shards(): lax.all_to_all(local_out, 'dp', split_axis=2, concat_axis=0, tiled=True)  14.8 us
    ppermute x20, starting transfers between devices, swap(): lax.ppermute(array, axis, [(i, i ^ mask) for i in range(lax.axis_size(axi...  14.5 us
    all_to_all x1, blocking collectives, shards(): sums = lax.all_to_all(proj_stats, ('dp', 'rows'), 0, 0, tiled=True)  13.3 us
    pallas_call x3, Pallas kernels, conv_part(): pl.pallas_call(functools.partial(conv_kernel, groups, tuple(masks), opens...  9.05 us
    ppermute x1, waiting for transfers between devices, far_swap(): return lax.ppermute(array, ('dp', 'rows'), pairs)  8.38 us
    ppermute x1, starting transfers between devices, far_swap(): return lax.ppermute(array, ('dp', 'rows'), pairs)  2.59 us
  transfers between devices with their start and end apart: 21, of which 11 were waited for; matrix products, arithmetic and copies ran while one was open for 3% of the time, Pallas kernels for 6%

profile of v3, /device:TPU:0, one launch (start us, length us, event | category | flops | bytes accessed | tf_op | source)
XLA Modules:
  0.0 96.3 jit_solution(10304105296720027048)
XLA Ops:
  0.0 1.2 %pick.1.rest_0_ = bf16[9,64,256]{2,1,0:T(8,128)(2,1)S(1)} custom-call(bf16[3,3,64,256]{3,2,1,0:T(8,128)(2,1)} %refs_0_.1, bf16[3,3,64,256]{3,2,1,0:T(8,128)(2,1)} %refs_1_.1, bf16[3,3,64,256]{3,2,1,0:T(8,128)(2,1)} %refs_2_.1), custom_call_target="tpu_custom_call" | custom-call | tf_op jit(solution)/shard_map/pick/pallas_call | solution.py:171
  1.2 3.0 %collective-permute-start.4 = (bf16[9,64,256]{2,1,0:T(8,128)(2,1)S(1)}, bf16[9,64,256]{2,1,0:T(8,128)(2,1)}, u32[]{:S(2)}, u32[]{:S(2)}) collective-permute-start(bf16[9,64,256]{2,1,0:T(8,128)(2,1)S(1)} %pick.1.rest_0_), channel_id=1, source_target_pairs={{0,4},{2,6},{4,0},{6,2},{8,12},{10,14},{12,8},{14,10},{16,20},{18,... | collective-permute-start | bytes 884744 | tf_op jit(solution)/shard_map/ppermute | solution.py:23
  4.2 2.6 %collective-permute-start = (bf16[9,64,256]{2,1,0:T(8,128)(2,1)S(1)}, bf16[9,64,256]{2,1,0:T(8,128)(2,1)S(1)}, u32[]{:S(2)}, u32[]{:S(2)}) collective-permute-start(bf16[9,64,256]{2,1,0:T(8,128)(2,1)S(1)} %pick.1.rest_0_), channel_id=1, source_target_pairs={{0,16},{1,25},{2,18},{3,27},{4,20},{5,29},{6,22},{7,31},{8,24},{9,... | collective-permute-start | bytes 884744 | tf_op jit(solution)/shard_map/ppermute | solution.py:271
  6.8 1.7 %convert_reduce_fusion = f32[2,1024]{1,0:T(2,128)S(1)} fusion(bf16[2,6,64,1024]{3,2,1,0:T(8,128)(2,1)} %x_ref.5), kind=kLoop, calls=%fused_computation | loop fusion | flops 1570816 | bytes 1581056 | tf_op jit(solution)/shard_map/reduce_sum | solution.py:376
  8.5 2.6 %collective-permute-start.3 = (f32[2,1024]{1,0:T(2,128)S(1)}, f32[2,1024]{1,0:T(2,128)S(1)}, u32[]{:S(2)}, u32[]{:S(2)}) collective-permute-start(f32[2,1024]{1,0:T(2,128)S(1)} %convert_reduce_fusion), channel_id=1, source_target_pairs={{0,1},{1,0},{2,3},{3,2},{4,5},{5,4},{6,7},{7,6},{8,9},{9,8},{10,11... | collective-permute-start | bytes 24584 | tf_op jit(solution)/shard_map/ppermute | solution.py:23
  11.1 0.0 collective-permute-start.2
  11.1 0.0 collective-permute-start.7
  11.1 0.2 collective-permute-done.4.rest_2_
  11.3 0.3 collective-permute-start.5
  11.6 8.4 %collective-permute-done.rest_0_ = bf16[9,64,256]{2,1,0:T(8,128)(2,1)S(1)} collective-permute-done((bf16[9,64,256]{2,1,0:T(8,128)(2,1)S(1)}, bf16[9,64,256]{2,1,0:T(8,128)(2,1)S(1)}, u32[]{:S(2)}, u32[]{:S(2)}) %collective-permute-start) | collective-permute-done | bytes 294944 | tf_op jit(solution)/shard_map/ppermute | solution.py:271
  20.0 0.0 collective-permute-start.11
  20.0 0.5 collective-permute-start.1
  20.5 1.2 %fusion.1.pool_ref = f32[2,256]{1,0:T(2,128)S(1)} fusion(bf16[1024,256]{1,0:T(8,128)(2,1)S(1)} %copy-done, bf16[1280,256]{1,0:T(8,128)(2,1)} %w_ref.1, f32[2,1024]{1,0:T(2,128)S(1)} %convert_reduce_fusion, f32[2,1024]{1,0:T(2,128)S(1)} %collective-permute-done.3), kind=kOutput, calls=%fused_computation.3 | convolution fusion | flops 1317888 | bytes 673792 | tf_op jit(solution)/shard_map/dot_general | solution.py:381
  21.7 0.0 collective-permute-done.2.rest_1_
  21.7 0.0 collective-permute-start.9
  21.7 3.7 %collective-permute-done.7.rest_2_ = bf16[9,64,256]{2,1,0:T(8,128)(2,1)} collective-permute-done((bf16[9,64,256]{2,1,0:T(8,128)(2,1)S(1)}, bf16[9,64,256]{2,1,0:T(8,128)(2,1)}, u32[]{:S(2)}, u32[]{:S(2)}) %collective-permute-start.7) | collective-permute-done | bytes 294944 | tf_op jit(solution)/shard_map/ppermute | solution.py:23
  25.4 0.0 collective-permute-done.5.rest_3_
  25.4 0.5 collective-permute-start.8
  25.9 2.1 %collective-permute-done.11.rest_4_ = bf16[9,64,256]{2,1,0:T(8,128)(2,1)} collective-permute-done((bf16[9,64,256]{2,1,0:T(8,128)(2,1)S(1)}, bf16[9,64,256]{2,1,0:T(8,128)(2,1)}, u32[]{:S(2)}, u32[]{:S(2)}) %collective-permute-start.11) | collective-permute-done | bytes 294944 | tf_op jit(solution)/shard_map/ppermute | solution.py:23
  28.0 2.8 %shard_map.118.rest_6_ = f32[2,6,64,1024]{3,2,1,0:T(8,128)S(1)} custom-call(s32[32]{0:T(128)S(1)} %copy-done.4, bf16[2,6,64,1024]{3,2,1,0:T(8,128)(2,1)S(1)} %copy-done.1, bf16[9,64,256]{2,1,0:T(8,128)(2,1)S(1)} %pick.1.rest_0_, bf16[9,64,256]{2,1,0:T(8,128)(2,1)} %collective-permute-done.2.rest_1_, bf16[9,64,256]{2,1,0:T(8,128)(2,1)} %collective-permute-done.4.rest_2_, ...), custom_call_target="tpu_custom_call" | custom-call | tf_op jit(solution)/shard_map/pallas_call | solution.py:143
  30.8 0.0 collective-permute-done.1.rest_0_
  30.9 1.1 %collective-permute-start.14 = (bf16[9,64,256]{2,1,0:T(8,128)(2,1)S(1)}, bf16[9,64,256]{2,1,0:T(8,128)(2,1)S(1)}, u32[]{:S(2)}, u32[]{:S(2)}) collective-permute-start(bf16[9,64,256]{2,1,0:T(8,128)(2,1)S(1)} %collective-permute-done.1.rest_0_), channel_id=1, source_target_pairs={{0,1},{1,0},{2,3},{3,2},{4,5},{5,4},{6,7},{7,6},{8,9},{9,8},{10,11... | collective-permute-start | bytes 884744 | tf_op jit(solution)/shard_map/ppermute | solution.py:23
  32.0 3.3 %shard_map.119.rest_6_ = f32[2,6,64,1024]{3,2,1,0:T(8,128)S(1)} custom-call(s32[32]{0:T(128)S(1)} %copy-done.4, bf16[2,6,64,1024]{3,2,1,0:T(8,128)(2,1)S(1)} %copy-done.1, bf16[9,64,256]{2,1,0:T(8,128)(2,1)S(1)} %collective-permute-done.rest_0_, bf16[9,64,256]{2,1,0:T(8,128)(2,1)S(1)} %collective-permute-done.9.rest_1_, ...), custom_call_target="tpu_custom_call", output_to_operand_aliasing={{}: (8, {})} | custom-call | tf_op jit(solution)/shard_map/pallas_call | solution.py:143
  35.2 0.0 copy-start.2
  35.3 0.0 copy-start.5
  35.3 0.0 copy-start.6
  35.3 0.6 collective-permute-start.13
  35.9 4.5 %collective-permute-done.14.rest_4_ = bf16[9,64,256]{2,1,0:T(8,128)(2,1)S(1)} collective-permute-done((bf16[9,64,256]{2,1,0:T(8,128)(2,1)S(1)}, bf16[9,64,256]{2,1,0:T(8,128)(2,1)S(1)}, u32[]{:S(2)}, u32[]{:S(2)}) %collective-permute-start.14) | collective-permute-done | bytes 294944 | tf_op jit(solution)/shard_map/ppermute | solution.py:23
  40.3 1.6 %collective-permute-done.15.rest_5_ = bf16[9,64,256]{2,1,0:T(8,128)(2,1)S(1)} collective-permute-done((bf16[9,64,256]{2,1,0:T(8,128)(2,1)S(1)}, bf16[9,64,256]{2,1,0:T(8,128)(2,1)S(1)}, u32[]{:S(2)}, u32[]{:S(2)}) %collective-permute-start.15) | collective-permute-done | bytes 294944 | tf_op jit(solution)/shard_map/ppermute | solution.py:23
  41.9 2.9 %shard_map.120 = (f32[2,6,64,1024]{3,2,1,0:T(8,128)S(1)}, f32[16,1024]{1,0:T(8,128)S(1)}) custom-call(s32[32]{0:T(128)S(1)} %copy-done.4, bf16[2,6,64,1024]{3,2,1,0:T(8,128)(2,1)S(1)} %copy-done.1, bf16[9,64,256]{2,1,0:T(8,128)(2,1)S(1)} %collective-permute-done.1.rest_0_, ...), custom_call_target="tpu_custom_call", output_to_operand_aliasing={{0}: (8, {})} | custom-call | tf_op jit(solution)/shard_map/pallas_call | solution.py:143
  44.8 0.0 copy-start.7
  44.9 0.0 copy-start.8
  44.9 0.2 collective-permute-start.16
  45.1 1.1 %collective-permute-done.16 = f32[16,1024]{1,0:T(8,128)S(1)} collective-permute-done((f32[16,1024]{1,0:T(8,128)S(1)}, f32[16,1024]{1,0:T(8,128)S(1)}, u32[]{:S(2)}, u32[]{:S(2)}) %collective-permute-start.16) | collective-permute-done | bytes 65568 | tf_op jit(solution)/shard_map/ppermute | solution.py:23
  46.2 0.5 collective-permute-start.17
  46.7 3.8 %collective-permute-done.17 = f32[16,1024]{1,0:T(8,128)S(1)} collective-permute-done((f32[16,1024]{1,0:T(8,128)S(1)}, f32[16,1024]{1,0:T(8,128)S(1)}, u32[]{:S(2)}, u32[]{:S(2)}) %collective-permute-start.17) | collective-permute-done | bytes 65568 | tf_op jit(solution)/shard_map/ppermute | solution.py:23
  50.5 1.7 %collective-permute-start.18 = (f32[16,1024]{1,0:T(8,128)S(1)}, f32[16,1024]{1,0:T(8,128)S(1)}, u32[]{:S(2)}, u32[]{:S(2)}) collective-permute-start(f32[16,1024]{1,0:T(8,128)S(1)} %add.20), channel_id=1, source_target_pairs={{0,8},{2,10},{4,12},{6,14},{8,0},{10,2},{12,4},{14,6},{16,24},{18,... | collective-permute-start | bytes 196616 | tf_op jit(solution)/shard_map/ppermute | solution.py:23
  52.3 2.6 %collective-permute-done.18 = f32[16,1024]{1,0:T(8,128)S(1)} collective-permute-done((f32[16,1024]{1,0:T(8,128)S(1)}, f32[16,1024]{1,0:T(8,128)S(1)}, u32[]{:S(2)}, u32[]{:S(2)}) %collective-permute-start.18) | collective-permute-done | bytes 65568 | tf_op jit(solution)/shard_map/ppermute | solution.py:23
  54.9 3.1 %collective-permute-start.19 = (f32[16,1024]{1,0:T(8,128)S(1)}, f32[16,1024]{1,0:T(8,128)S(1)}, u32[]{:S(2)}, u32[]{:S(2)}) collective-permute-start(f32[16,1024]{1,0:T(8,128)S(1)} %add.21), channel_id=1, source_target_pairs={{0,16},{2,18},{4,20},{6,22},{8,24},{10,26},{12,28},{14,30},{16,0},... | collective-permute-start | bytes 196616 | tf_op jit(solution)/shard_map/ppermute | solution.py:23
  58.0 2.2 %collective-permute-done.19 = f32[16,1024]{1,0:T(8,128)S(1)} collective-permute-done((f32[16,1024]{1,0:T(8,128)S(1)}, f32[16,1024]{1,0:T(8,128)S(1)}, u32[]{:S(2)}, u32[]{:S(2)}) %collective-permute-start.19) | collective-permute-done | bytes 65568 | tf_op jit(solution)/shard_map/ppermute | solution.py:23
  60.3 0.4 collective-permute-start.20
  60.6 4.0 %collective-permute-done.20 = f32[16,1024]{1,0:T(8,128)S(1)} collective-permute-done((f32[16,1024]{1,0:T(8,128)S(1)}, f32[16,1024]{1,0:T(8,128)S(1)}, u32[]{:S(2)}, u32[]{:S(2)}) %collective-permute-start.20) | collective-permute-done | bytes 65568 | tf_op jit(solution)/shard_map/ppermute | solution.py:23
  64.6 1.4 %project.1 = (f32[2,6,64,256]{3,2,1,0:T(8,128)S(1)}, f32[32,4,256]{2,1,0:T(4,128)S(1)}) custom-call(s32[32]{0:T(128)S(1)} %copy-done.4, f32[2,6,64,1024]{3,2,1,0:T(8,128)S(1)} %get-tuple-element.22.pre_ref, f32[16,1024]{1,0:T(8,128)S(1)} %add.23.total_ref, f32[4,256]{1,0:T(4,128)S(1)} %copy-done.5, f32[4,256]{1,0:T(4,128)S(1)} %copy-done.6, ...), custom_call_target="tpu_custom_call" | custom-call | tf_op jit(solution)/shard_map/project/pallas_call | solution.py:251
  66.1 13.3 %all_to_all.23 = f32[32,4,256]{2,1,0:T(4,128)S(1)} all-to-all(f32[32,4,256]{2,1,0:T(4,128)S(1)} %get-tuple-element.26), channel_id=1, replica_groups=mesh['dp'=16,'rows'=2] {'dp','rows'}, dimensions={0} | all-to-all | bytes 262144 | tf_op jit(solution)/shard_map/all_to_all | solution.py:409
  79.4 0.8 finish.1
  80.2 0.4 copy.18
  80.6 14.8 %all_to_all.24 = bf16[2,6,64,256]{3,0,1,2:T(2,128)(2,1)S(1)} all-to-all(bf16[2,6,64,256]{3,0,1,2:T(2,128)(2,1)S(1)} %copy.18), channel_id=1, replica_groups=mesh['dp'=16,'rows'=2] {'dp'}, dimensions={2} | all-to-all | bytes 786432 | tf_op jit(solution)/shard_map/all_to_all | solution.py:418
  95.4 0.9 copy.19
  (29 shorter events, 0.1 us)
Async XLA Ops:
  0.0 20.5 %copy-start = (bf16[1024,256]{1,0:T(8,128)(2,1)S(1)}, bf16[1024,256]{1,0:T(8,128)(2,1)}, u32[]{:S(2)}) copy-start(bf16[1024,256]{1,0:T(8,128)(2,1)} %param.17) | copy-start | bytes 1572868
  0.0 28.0 %copy-start.1 = (bf16[2,6,64,1024]{3,2,1,0:T(8,128)(2,1)S(1)}, bf16[2,6,64,1024]{3,2,1,0:T(8,128)(2,1)}, u32[]{:S(2)}) copy-start(bf16[2,6,64,1024]{3,2,1,0:T(8,128)(2,1)} %x_ref.5) | copy-start | bytes 4718596
  0.0 28.0 %copy-start.3 = (bf16[1024,256]{1,0:T(8,128)(2,1)S(1)}, bf16[1024,256]{1,0:T(8,128)(2,1)}, u32[]{:S(2)}) copy-start(bf16[1024,256]{1,0:T(8,128)(2,1)} %rest_4_.1) | copy-start | bytes 1572868
  0.0 28.0 %copy-start.4 = (s32[32]{0:T(128)S(1)}, s32[32]{0:T(128)}, u32[]{:S(2)}) copy-start(s32[32]{0:T(128)} %index_ref.9) | copy-start | bytes 388
  1.2 10.2 %collective-permute-start.4 = (bf16[9,64,256]{2,1,0:T(8,128)(2,1)S(1)}, bf16[9,64,256]{2,1,0:T(8,128)(2,1)}, u32[]{:S(2)}, u32[]{:S(2)}) collective-permute-start(bf16[9,64,256]{2,1,0:T(8,128)(2,1)S(1)} %pick.1.rest_0_), channel_id=1, source_target_pairs={{0,4},{2,6},{4,0},{6,2},{8,12},{10,14},{12,8},{14,10},{16,20},{18,... | collective-permute-start | bytes 884744 | tf_op jit(solution)/shard_map/ppermute | solution.py:23
  4.2 15.8 %collective-permute-start = (bf16[9,64,256]{2,1,0:T(8,128)(2,1)S(1)}, bf16[9,64,256]{2,1,0:T(8,128)(2,1)S(1)}, u32[]{:S(2)}, u32[]{:S(2)}) collective-permute-start(bf16[9,64,256]{2,1,0:T(8,128)(2,1)S(1)} %pick.1.rest_0_), channel_id=1, source_target_pairs={{0,16},{1,25},{2,18},{3,27},{4,20},{5,29},{6,22},{7,31},{8,24},{9,... | collective-permute-start | bytes 884744 | tf_op jit(solution)/shard_map/ppermute | solution.py:271
  8.5 11.5 %collective-permute-start.3 = (f32[2,1024]{1,0:T(2,128)S(1)}, f32[2,1024]{1,0:T(2,128)S(1)}, u32[]{:S(2)}, u32[]{:S(2)}) collective-permute-start(f32[2,1024]{1,0:T(2,128)S(1)} %convert_reduce_fusion), channel_id=1, source_target_pairs={{0,1},{1,0},{2,3},{3,2},{4,5},{5,4},{6,7},{7,6},{8,9},{9,8},{10,11... | collective-permute-start | bytes 24584 | tf_op jit(solution)/shard_map/ppermute | solution.py:23
  11.1 10.6 %collective-permute-start.2 = (bf16[9,64,256]{2,1,0:T(8,128)(2,1)S(1)}, bf16[9,64,256]{2,1,0:T(8,128)(2,1)}, u32[]{:S(2)}, u32[]{:S(2)}) collective-permute-start(bf16[9,64,256]{2,1,0:T(8,128)(2,1)S(1)} %pick.1.rest_0_), channel_id=1, source_target_pairs={{0,2},{2,0},{4,6},{6,4},{8,10},{10,8},{12,14},{14,12},{16,18},{18,... | collective-permute-start | bytes 884744 | tf_op jit(solution)/shard_map/ppermute | solution.py:23
  11.1 14.3 %collective-permute-start.7 = (bf16[9,64,256]{2,1,0:T(8,128)(2,1)S(1)}, bf16[9,64,256]{2,1,0:T(8,128)(2,1)}, u32[]{:S(2)}, u32[]{:S(2)}) collective-permute-start(bf16[9,64,256]{2,1,0:T(8,128)(2,1)S(1)} %pick.1.rest_0_), channel_id=1, source_target_pairs={{0,8},{2,10},{4,12},{6,14},{8,0},{10,2},{12,4},{14,6},{16,24},{18,... | collective-permute-start | bytes 884744 | tf_op jit(solution)/shard_map/ppermute | solution.py:23
  11.3 14.1 %collective-permute-start.5 = (bf16[9,64,256]{2,1,0:T(8,128)(2,1)}, bf16[9,64,256]{2,1,0:T(8,128)(2,1)}, u32[]{:S(2)}, u32[]{:S(2)}) collective-permute-start(bf16[9,64,256]{2,1,0:T(8,128)(2,1)} %collective-permute-done.4.rest_2_), channel_id=1, source_target_pairs={{0,2},{2,0},{4,6},{6,4},{8,10},{10,8},{12,14},{14,12},{16,18},{18,... | collective-permute-start | bytes 884744 | tf_op jit(solution)/shard_map/ppermute | solution.py:23
  20.0 8.0 %collective-permute-start.11 = (bf16[9,64,256]{2,1,0:T(8,128)(2,1)S(1)}, bf16[9,64,256]{2,1,0:T(8,128)(2,1)}, u32[]{:S(2)}, u32[]{:S(2)}) collective-permute-start(bf16[9,64,256]{2,1,0:T(8,128)(2,1)S(1)} %collective-permute-done.rest_0_), channel_id=1, source_target_pairs={{0,1},{1,0},{2,3},{3,2},{4,5},{5,4},{6,7},{7,6},{8,9},{9,8},{10,11... | collective-permute-start | bytes 884744 | tf_op jit(solution)/shard_map/ppermute | solution.py:23
  20.0 10.8 %collective-permute-start.1 = (bf16[9,64,256]{2,1,0:T(8,128)(2,1)S(1)}, bf16[9,64,256]{2,1,0:T(8,128)(2,1)S(1)}, u32[]{:S(2)}, u32[]{:S(2)}) collective-permute-start(bf16[9,64,256]{2,1,0:T(8,128)(2,1)S(1)} %collective-permute-done.rest_0_), channel_id=1, source_target_pairs={{0,4},{2,6},{4,0},{6,2},{8,12},{10,14},{12,8},{14,10},{16,20},{18,... | collective-permute-start | bytes 884744 | tf_op jit(solution)/shard_map/ppermute | solution.py:23
  21.7 10.3 %collective-permute-start.9 = (bf16[9,64,256]{2,1,0:T(8,128)(2,1)S(1)}, bf16[9,64,256]{2,1,0:T(8,128)(2,1)S(1)}, u32[]{:S(2)}, u32[]{:S(2)}) collective-permute-start(bf16[9,64,256]{2,1,0:T(8,128)(2,1)S(1)} %collective-permute-done.rest_0_), channel_id=1, source_target_pairs={{0,2},{2,0},{4,6},{6,4},{8,10},{10,8},{12,14},{14,12},{16,18},{18,... | collective-permute-start | bytes 884744 | tf_op jit(solution)/shard_map/ppermute | solution.py:23
  25.4 6.5 %collective-permute-start.10 = (bf16[9,64,256]{2,1,0:T(8,128)(2,1)}, bf16[9,64,256]{2,1,0:T(8,128)(2,1)S(1)}, u32[]{:S(2)}, u32[]{:S(2)}) collective-permute-start(bf16[9,64,256]{2,1,0:T(8,128)(2,1)} %collective-permute-done.7.rest_2_), channel_id=1, source_target_pairs={{0,2},{2,0},{4,6},{6,4},{8,10},{10,8},{12,14},{14,12},{16,18},{18,... | collective-permute-start | bytes 884744 | tf_op jit(solution)/shard_map/ppermute | solution.py:23
  25.4 9.8 %collective-permute-start.8 = (bf16[9,64,256]{2,1,0:T(8,128)(2,1)}, bf16[9,64,256]{2,1,0:T(8,128)(2,1)S(1)}, u32[]{:S(2)}, u32[]{:S(2)}) collective-permute-start(bf16[9,64,256]{2,1,0:T(8,128)(2,1)} %collective-permute-done.7.rest_2_), channel_id=1, source_target_pairs={{0,4},{2,6},{4,0},{6,2},{8,12},{10,14},{12,8},{14,10},{16,20},{18,... | collective-permute-start | bytes 884744 | tf_op jit(solution)/shard_map/ppermute | solution.py:23
  28.0 4.0 %collective-permute-start.12 = (bf16[9,64,256]{2,1,0:T(8,128)(2,1)}, bf16[9,64,256]{2,1,0:T(8,128)(2,1)S(1)}, u32[]{:S(2)}, u32[]{:S(2)}) collective-permute-start(bf16[9,64,256]{2,1,0:T(8,128)(2,1)} %collective-permute-done.11.rest_4_), channel_id=1, source_target_pairs={{0,2},{2,0},{4,6},{6,4},{8,10},{10,8},{12,14},{14,12},{16,18},{18,... | collective-permute-start | bytes 884744 | tf_op jit(solution)/shard_map/ppermute | solution.py:23
  30.9 9.5 %collective-permute-start.14 = (bf16[9,64,256]{2,1,0:T(8,128)(2,1)S(1)}, bf16[9,64,256]{2,1,0:T(8,128)(2,1)S(1)}, u32[]{:S(2)}, u32[]{:S(2)}) collective-permute-start(bf16[9,64,256]{2,1,0:T(8,128)(2,1)S(1)} %collective-permute-done.1.rest_0_), channel_id=1, source_target_pairs={{0,1},{1,0},{2,3},{3,2},{4,5},{5,4},{6,7},{7,6},{8,9},{9,8},{10,11... | collective-permute-start | bytes 884744 | tf_op jit(solution)/shard_map/ppermute | solution.py:23
  31.9 8.4 %collective-permute-start.6 = (bf16[9,64,256]{2,1,0:T(8,128)(2,1)S(1)}, bf16[9,64,256]{2,1,0:T(8,128)(2,1)S(1)}, u32[]{:S(2)}, u32[]{:S(2)}) collective-permute-start(bf16[9,64,256]{2,1,0:T(8,128)(2,1)S(1)} %collective-permute-done.1.rest_0_), channel_id=1, source_target_pairs={{0,2},{2,0},{4,6},{6,4},{8,10},{10,8},{12,14},{14,12},{16,18},{18,... | collective-permute-start | bytes 884744 | tf_op jit(solution)/shard_map/ppermute | solution.py:23
  35.2 29.4 %copy-start.2 = (bf16[1280,256]{1,0:T(8,128)(2,1)S(1)}, bf16[1280,256]{1,0:T(8,128)(2,1)}, u32[]{:S(2)}) copy-start(bf16[1280,256]{1,0:T(8,128)(2,1)} %w_ref.1) | copy-start | bytes 1966084
  35.3 29.4 %copy-start.5 = (f32[4,256]{1,0:T(4,128)S(1)}, f32[4,256]{1,0:T(4,128)}, u32[]{:S(2)}) copy-start(f32[4,256]{1,0:T(4,128)} %gain_ref.1) | copy-start | bytes 12292
  35.3 29.4 %copy-start.6 = (f32[4,256]{1,0:T(4,128)S(1)}, f32[4,256]{1,0:T(4,128)}, u32[]{:S(2)}) copy-start(f32[4,256]{1,0:T(4,128)} %shift_ref.1) | copy-start | bytes 12292
  35.3 5.0 %collective-permute-start.13 = (bf16[9,64,256]{2,1,0:T(8,128)(2,1)S(1)}, bf16[9,64,256]{2,1,0:T(8,128)(2,1)S(1)}, u32[]{:S(2)}, u32[]{:S(2)}) collective-permute-start(bf16[9,64,256]{2,1,0:T(8,128)(2,1)S(1)} %collective-permute-done.8.rest_2_), channel_id=1, source_target_pairs={{0,2},{2,0},{4,6},{6,4},{8,10},{10,8},{12,14},{14,12},{16,18},{18,... | collective-permute-start | bytes 884744 | tf_op jit(solution)/shard_map/ppermute | solution.py:23
  40.3 1.6 %collective-permute-start.15 = (bf16[9,64,256]{2,1,0:T(8,128)(2,1)S(1)}, bf16[9,64,256]{2,1,0:T(8,128)(2,1)S(1)}, u32[]{:S(2)}, u32[]{:S(2)}) collective-permute-start(bf16[9,64,256]{2,1,0:T(8,128)(2,1)S(1)} %collective-permute-done.14.rest_4_), channel_id=1, source_target_pairs={{0,2},{2,0},{4,6},{6,4},{8,10},{10,8},{12,14},{14,12},{16,18},{18,... | collective-permute-start | bytes 884744 | tf_op jit(solution)/shard_map/ppermute | solution.py:23
  44.8 34.5 %copy-start.7 = (f32[256]{0:T(256)S(1)}, f32[256]{0:T(256)}, u32[]{:S(2)}) copy-start(f32[256]{0:T(256)} %param.21) | copy-start | bytes 3076
  44.9 34.5 %copy-start.8 = (f32[256]{0:T(256)S(1)}, f32[256]{0:T(256)}, u32[]{:S(2)}) copy-start(f32[256]{0:T(256)} %param.22) | copy-start | bytes 3076
  44.9 1.3 %collective-permute-start.16 = (f32[16,1024]{1,0:T(8,128)S(1)}, f32[16,1024]{1,0:T(8,128)S(1)}, u32[]{:S(2)}, u32[]{:S(2)}) collective-permute-start(f32[16,1024]{1,0:T(8,128)S(1)} %get-tuple-element.23), channel_id=1, source_target_pairs={{0,2},{2,0},{4,6},{6,4},{8,10},{10,8},{12,14},{14,12},{16,18},{18,... | collective-permute-start | bytes 196616 | tf_op jit(solution)/shard_map/ppermute | solution.py:23
  46.2 4.3 %collective-permute-start.17 = (f32[16,1024]{1,0:T(8,128)S(1)}, f32[16,1024]{1,0:T(8,128)S(1)}, u32[]{:S(2)}, u32[]{:S(2)}) collective-permute-start(f32[16,1024]{1,0:T(8,128)S(1)} %add.19), channel_id=1, source_target_pairs={{0,4},{2,6},{4,0},{6,2},{8,12},{10,14},{12,8},{14,10},{16,20},{18,... | collective-permute-start | bytes 196616 | tf_op jit(solution)/shard_map/ppermute | solution.py:23
  50.5 4.3 %collective-permute-start.18 = (f32[16,1024]{1,0:T(8,128)S(1)}, f32[16,1024]{1,0:T(8,128)S(1)}, u32[]{:S(2)}, u32[]{:S(2)}) collective-permute-start(f32[16,1024]{1,0:T(8,128)S(1)} %add.20), channel_id=1, source_target_pairs={{0,8},{2,10},{4,12},{6,14},{8,0},{10,2},{12,4},{14,6},{16,24},{18,... | collective-permute-start | bytes 196616 | tf_op jit(solution)/shard_map/ppermute | solution.py:23
  54.9 5.4 %collective-permute-start.19 = (f32[16,1024]{1,0:T(8,128)S(1)}, f32[16,1024]{1,0:T(8,128)S(1)}, u32[]{:S(2)}, u32[]{:S(2)}) collective-permute-start(f32[16,1024]{1,0:T(8,128)S(1)} %add.21), channel_id=1, source_target_pairs={{0,16},{2,18},{4,20},{6,22},{8,24},{10,26},{12,28},{14,30},{16,0},... | collective-permute-start | bytes 196616 | tf_op jit(solution)/shard_map/ppermute | solution.py:23
  60.3 4.3 %collective-permute-start.20 = (f32[16,1024]{1,0:T(8,128)S(1)}, f32[16,1024]{1,0:T(8,128)S(1)}, u32[]{:S(2)}, u32[]{:S(2)}) collective-permute-start(f32[16,1024]{1,0:T(8,128)S(1)} %add.22), channel_id=1, source_target_pairs={{0,1},{1,0},{2,3},{3,2},{4,5},{5,4},{6,7},{7,6},{8,9},{9,8},{10,11... | collective-permute-start | bytes 196616 | tf_op jit(solution)/shard_map/ppermute | solution.py:23

commit v4 on v3

--- a/solution.py
+++ b/solution.py
@@ -11,6 +11,7 @@
 VMEM = pltpu.VMEM
 SMEM = pltpu.SMEM
 VMEM_LIMIT = 26 * 2**20
+WIDE = 2
 
 
 def from_behind(array, axis, by):
@@ -40,6 +41,27 @@
         for mask in masks_of(axis):
             array = array + swap(array, axis, mask)
     return array
+
+
+def peer(array, dp_mask, rows_mask):
+    count = lax.axis_size("rows")
+    size = lax.axis_size("dp") * count
+    pairs = [(i, (i // count ^ dp_mask) * count + (i % count ^ rows_mask)) for i in range(size)]
+    return lax.ppermute(array, ("dp", "rows"), pairs)
+
+
+def total_over_all(stats):
+    quarter = lax.axis_size("dp") // 4
+    steps = [(mask, 0) for mask in masks_of("dp") if 1 < mask < quarter]
+    steps += [(0, mask) for mask in masks_of("rows")]
+    steps += [(quarter, 0), (2 * quarter, 0)]
+    total = stats + swap(stats, "dp", 1)
+    for i in range(0, len(steps), WIDE):
+        moves = [(0, 0)]
+        for a, b in steps[i : i + WIDE]:
+            moves += [(a ^ c, b ^ d) for c, d in moves]
+        total = sum((peer(total, *move) for move in moves[1:]), total)
+    return total
 
 
 def tap_span(cols, shift):
@@ -230,13 +252,18 @@
         inv = lax.rsqrt(var + 1e-05)
         proj = proj_ref[i].reshape(rows * cols, outs)
         scaled = (proj - mean) * inv * gain_ref[...] + shift_ref[...]
-        out_ref[i] = jnp.maximum(scaled, 0.0).astype(out_ref.dtype).reshape(rows, cols, outs)
+        tiles, wide = out_ref.shape[0], out_ref.shape[3]
+        result = jnp.maximum(scaled, 0.0).reshape(rows, tiles, wide, outs)
+        for h in range(rows):
+            out_ref[:, i, h] = result[h].astype(out_ref.dtype)
 
 
 def finished(proj, sums, index, gain, shift, count):
+    images, rows, cols, outs = proj.shape
+    tiles = lax.axis_size("dp")
     return pl.pallas_call(
         functools.partial(finish_kernel, count),
-        out_shape=jax.ShapeDtypeStruct(proj.shape, jnp.bfloat16),
+        out_shape=jax.ShapeDtypeStruct((tiles, images, rows, cols // tiles, outs), jnp.bfloat16),
         in_specs=[pl.BlockSpec(memory_space=SMEM)] + [pl.BlockSpec(memory_space=VMEM)] * 4,
         out_specs=pl.BlockSpec(memory_space=VMEM),
         compiler_params=pltpu.CompilerParams(vmem_limit_bytes=VMEM_LIMIT),
@@ -295,32 +322,34 @@
     pass_on(origin)
     for mask in beside:
         pass_on(mask)
-    held[origin], pool_term = lax.optimization_barrier((held[origin], pool_term))
-    opened = [origin] + beside
-    (done,) = conv_part(features, held, opened, index, groups, pointwise_weight)
+    got[first], pool_term = lax.optimization_barrier((got[first], pool_term))
     for mask in near:
         got[by(first, mask)] = swap(got[first], "dp", mask)
     got[second] = swap(got[first], "rows", 1)
     for mask in near:
         got[by(both, mask)] = swap(got[both], "dp", mask)
+    pass_on(both)
     pass_on(first)
-    pass_on(both)
+    opened = [origin, both, first] + beside
+    (done,) = conv_part(features, held, opened, index, groups, pointwise_weight)
+    relayed = []
     for mask in near:
         late = by(first, mask)
         got[late], done = lax.optimization_barrier((got[late], done))
         got[by(second, mask)] = swap(got[late], "rows", 1)
+        pass_on(late)
+        relayed.append(late)
     pass_on(second)
-    (done,) = conv_part(features, held, [first, both, second], index, groups, done=done)
+    (done,) = conv_part(features, held, [second] + relayed, index, groups, done=done)
     last = []
     for mask in near:
-        pass_on(by(first, mask))
         late, final = by(both, mask), by(second, mask)
         got[late], done = lax.optimization_barrier((got[late], done))
         pass_on(late)
         pass_on(final)
-        last += [by(first, mask), by(both, mask), final]
+        last += [late, final]
     pre, stats = conv_part(features, held, last, index, groups, done=done, closes=True)
-    return pre, stats, pool_term
+    return pre, total_over_all(stats), pool_term
 
 
 def row_tap_list(block_tensor, kernel_row_slice, dilation_rate):
@@ -381,7 +410,7 @@
     pool_term = jnp.dot(pool_act, projection_weight[width:], preferred_element_type=jnp.float32)
     middle_only = all(d // rows_dev >= rows_size for d in DILATIONS)
     if middle_only and rows_size % 2 == 0 and dp_size >= 8 and dp_size & (dp_size - 1) == 0:
-        pre, stats, pool_term = conv_branches(
+        pre, totals, pool_term = conv_branches(
             features, kernels, pointwise_weight, pool_term, ghost_group_index, groups
         )
     else:
@@ -394,7 +423,7 @@
             ],
             0,
         )
-    totals = sum_over(stats, ("dp", "rows"))
+        totals = sum_over(stats, ("dp", "rows"))
     proj, proj_stats = normed_project(
         pre,
         totals,
@@ -415,7 +444,8 @@
         projection_norm_shift.reshape(1, -1),
         count,
     )
-    return lax.all_to_all(local_out, "dp", split_axis=2, concat_axis=0, tiled=True)
+    local_out = local_out.reshape(dp_size * images, *local_out.shape[2:])
+    return lax.all_to_all(local_out, "dp", 0, 0, tiled=True)
 
 
 def solution(mesh):

time: 96.5 us -> 91.1 us (0.944)
  waiting for transfers between devices: 34.2 us -> 26.4 us
  starting transfers between devices: 17.1 us -> 23.6 us
  blocking collectives: 28.1 us -> 25.7 us
  Pallas kernels: 12.4 us -> 11.3 us
    ppermute x20 -> x16, waiting for transfers between devices: 25.8 us -> 13.8 us  [swap(): lax.ppermute(array, axis, [(i, i ^ mask) for i in range(lax.axis_size(axi...]
    ppermute x0 -> x6, waiting for transfers between devices: none -> 8.83 us  [peer(): return lax.ppermute(array, ('dp', 'rows'), pairs)]
    ppermute x0 -> x6, starting transfers between devices: none -> 8.01 us  [peer(): return lax.ppermute(array, ('dp', 'rows'), pairs)]
    ppermute x1, waiting for transfers between devices: 8.38 us -> 3.77 us  [far_swap(): return lax.ppermute(array, ('dp', 'rows'), pairs)]
    ppermute x20 -> x16, starting transfers between devices: 14.5 us -> 11.4 us  [swap(): lax.ppermute(array, axis, [(i, i ^ mask) for i in range(lax.axis_size(axi...]
    all_to_all x1, blocking collectives: 13.3 us -> 10.9 us  [shards(): sums = lax.all_to_all(proj_stats, ('dp', 'rows'), 0, 0, tiled=True)]
    ppermute x1, starting transfers between devices: 2.59 us -> 4.14 us  [far_swap(): return lax.ppermute(array, ('dp', 'rows'), pairs)]
    pallas_call x3, Pallas kernels: 9.05 us -> 7.9 us  [conv_part(): pl.pallas_call(functools.partial(conv_kernel, groups, tuple(masks), opens...]
  transfers between devices with their start and end apart: 21 -> 23, of which waited for: 11 -> 16; matrix products, arithmetic and copies ran while one was open for 3% -> 3% of each run, Pallas kernels for 6% -> 6%
where the time goes in v4:
time: 91.1 us; the launch traced here: 90.8 us
  waiting for transfers between devices  26.4 us (29%)
  blocking collectives  25.7 us (28%)
  starting transfers between devices  23.6 us (26%)
  Pallas kernels  11.3 us (12%)
  other arithmetic  1.74 us (2%)
  matrix products  1.17 us (1%)
    all_to_all x1, blocking collectives, shards(): return lax.all_to_all(local_out, 'dp', 0, 0, tiled=True)  14.8 us
    ppermute x16, waiting for transfers between devices, swap(): lax.ppermute(array, axis, [(i, i ^ mask) for i in range(lax.axis_size(axi...  13.8 us
    ppermute x16, starting transfers between devices, swap(): lax.ppermute(array, axis, [(i, i ^ mask) for i in range(lax.axis_size(axi...  11.4 us
    all_to_all x1, blocking collectives, shards(): sums = lax.all_to_all(proj_stats, ('dp', 'rows'), 0, 0, tiled=True)  10.9 us
    ppermute x6, waiting for transfers between devices, peer(): return lax.ppermute(array, ('dp', 'rows'), pairs)  8.83 us
    ppermute x6, starting transfers between devices, peer(): return lax.ppermute(array, ('dp', 'rows'), pairs)  8.01 us
    pallas_call x3, Pallas kernels, conv_part(): pl.pallas_call(functools.partial(conv_kernel, groups, tuple(masks), opens...  7.9 us
    ppermute x1, starting transfers between devices, far_swap(): return lax.ppermute(array, ('dp', 'rows'), pairs)  4.14 us
  transfers between devices with their start and end apart: 23, of which 16 were waited for; matrix products, arithmetic and copies ran while one was open for 3% of the time, Pallas kernels for 6%

profile of v4, /device:TPU:0, one launch (start us, length us, event | category | flops | bytes accessed | tf_op | source)
XLA Modules:
  0.0 90.8 jit_solution(9147645049517580117)
XLA Ops:
  0.0 1.2 %pick.1.rest_0_ = bf16[9,64,256]{2,1,0:T(8,128)(2,1)S(1)} custom-call(bf16[3,3,64,256]{3,2,1,0:T(8,128)(2,1)} %refs_0_.1, bf16[3,3,64,256]{3,2,1,0:T(8,128)(2,1)} %refs_1_.1, bf16[3,3,64,256]{3,2,1,0:T(8,128)(2,1)} %refs_2_.1), custom_call_target="tpu_custom_call" | custom-call | tf_op jit(solution)/shard_map/pick/pallas_call | solution.py:193
  1.2 4.1 %collective-permute-start.2 = (bf16[9,64,256]{2,1,0:T(8,128)(2,1)S(1)}, bf16[9,64,256]{2,1,0:T(8,128)(2,1)S(1)}, u32[]{:S(2)}, u32[]{:S(2)}) collective-permute-start(bf16[9,64,256]{2,1,0:T(8,128)(2,1)S(1)} %pick.1.rest_0_), channel_id=1, source_target_pairs={{0,16},{1,25},{2,18},{3,27},{4,20},{5,29},{6,22},{7,31},{8,24},{9,... | collective-permute-start | bytes 884744 | tf_op jit(solution)/shard_map/ppermute | solution.py:298
  5.3 1.6 %collective-permute-start = (bf16[9,64,256]{2,1,0:T(8,128)(2,1)S(1)}, bf16[9,64,256]{2,1,0:T(8,128)(2,1)S(1)}, u32[]{:S(2)}, u32[]{:S(2)}) collective-permute-start(bf16[9,64,256]{2,1,0:T(8,128)(2,1)S(1)} %pick.1.rest_0_), channel_id=1, source_target_pairs={{0,8},{2,10},{4,12},{6,14},{8,0},{10,2},{12,4},{14,6},{16,24},{18,... | collective-permute-start | bytes 884744 | tf_op jit(solution)/shard_map/ppermute | solution.py:24
  6.9 1.5 %collective-permute-start.10 = (bf16[9,64,256]{2,1,0:T(8,128)(2,1)S(1)}, bf16[9,64,256]{2,1,0:T(8,128)(2,1)}, u32[]{:S(2)}, u32[]{:S(2)}) collective-permute-start(bf16[9,64,256]{2,1,0:T(8,128)(2,1)S(1)} %pick.1.rest_0_), channel_id=1, source_target_pairs={{0,4},{2,6},{4,0},{6,2},{8,12},{10,14},{12,8},{14,10},{16,20},{18,... | collective-permute-start | bytes 884744 | tf_op jit(solution)/shard_map/ppermute | solution.py:24
  8.4 1.7 %convert_reduce_fusion = f32[2,1024]{1,0:T(2,128)S(1)} fusion(bf16[2,6,64,1024]{3,2,1,0:T(8,128)(2,1)} %x_ref.5), kind=kLoop, calls=%fused_computation | loop fusion | flops 1570816 | bytes 1581056 | tf_op jit(solution)/shard_map/reduce_sum | solution.py:405
  10.1 1.0 %collective-permute-start.3 = (f32[2,1024]{1,0:T(2,128)S(1)}, f32[2,1024]{1,0:T(2,128)S(1)}, u32[]{:S(2)}, u32[]{:S(2)}) collective-permute-start(f32[2,1024]{1,0:T(2,128)S(1)} %convert_reduce_fusion), channel_id=1, source_target_pairs={{0,1},{1,0},{2,3},{3,2},{4,5},{5,4},{6,7},{7,6},{8,9},{9,8},{10,11... | collective-permute-start | bytes 24584 | tf_op jit(solution)/shard_map/ppermute | solution.py:24
  11.1 2.7 %collective-permute-done.3 = f32[2,1024]{1,0:T(2,128)S(1)} collective-permute-done((f32[2,1024]{1,0:T(2,128)S(1)}, f32[2,1024]{1,0:T(2,128)S(1)}, u32[]{:S(2)}, u32[]{:S(2)}) %collective-permute-start.3) | collective-permute-done | bytes 8224 | tf_op jit(solution)/shard_map/ppermute | solution.py:24
  13.8 1.2 %fusion.1.pool_ref = f32[2,256]{1,0:T(2,128)S(1)} fusion(bf16[1024,256]{1,0:T(8,128)(2,1)S(1)} %copy-done, bf16[1280,256]{1,0:T(8,128)(2,1)} %w_ref.1, f32[2,1024]{1,0:T(2,128)S(1)} %convert_reduce_fusion, f32[2,1024]{1,0:T(2,128)S(1)} %collective-permute-done.3), kind=kOutput, calls=%fused_computation.3 | convolution fusion | flops 1317888 | bytes 673792 | tf_op jit(solution)/shard_map/dot_general | solution.py:410
  15.0 3.8 %collective-permute-done.2.rest_4_ = bf16[9,64,256]{2,1,0:T(8,128)(2,1)S(1)} collective-permute-done((bf16[9,64,256]{2,1,0:T(8,128)(2,1)S(1)}, bf16[9,64,256]{2,1,0:T(8,128)(2,1)S(1)}, u32[]{:S(2)}, u32[]{:S(2)}) %collective-permute-start.2) | collective-permute-done | bytes 294944 | tf_op jit(solution)/shard_map/ppermute | solution.py:298
  18.8 0.2 collective-permute-done.rest_2_
  18.9 0.3 collective-permute-start.8
  19.3 0.2 collective-permute-start.11
  19.5 1.5 %collective-permute-start.6 = (bf16[9,64,256]{2,1,0:T(8,128)(2,1)S(1)}, bf16[9,64,256]{2,1,0:T(8,128)(2,1)S(1)}, u32[]{:S(2)}, u32[]{:S(2)}) collective-permute-start(bf16[9,64,256]{2,1,0:T(8,128)(2,1)S(1)} %collective-permute-done.2.rest_4_), channel_id=1, source_target_pairs={{0,4},{2,6},{4,0},{6,2},{8,12},{10,14},{12,8},{14,10},{16,20},{18,... | collective-permute-start | bytes 884744 | tf_op jit(solution)/shard_map/ppermute | solution.py:24
  21.0 2.3 %collective-permute-start.4 = (bf16[9,64,256]{2,1,0:T(8,128)(2,1)S(1)}, bf16[9,64,256]{2,1,0:T(8,128)(2,1)S(1)}, u32[]{:S(2)}, u32[]{:S(2)}) collective-permute-start(bf16[9,64,256]{2,1,0:T(8,128)(2,1)S(1)} %collective-permute-done.2.rest_4_), channel_id=1, source_target_pairs={{0,1},{1,0},{2,3},{3,2},{4,5},{5,4},{6,7},{7,6},{8,9},{9,8},{10,11... | collective-permute-start | bytes 884744 | tf_op jit(solution)/shard_map/ppermute | solution.py:24
  23.3 3.7 %shard_map.118.rest_4_ = f32[2,6,64,1024]{3,2,1,0:T(8,128)S(1)} custom-call(s32[32]{0:T(128)S(1)} %copy-done.4, bf16[2,6,64,1024]{3,2,1,0:T(8,128)(2,1)S(1)} %copy-done.1, bf16[9,64,256]{2,1,0:T(8,128)(2,1)S(1)} %pick.1.rest_0_, bf16[9,64,256]{2,1,0:T(8,128)(2,1)} %collective-permute-done.7.rest_1_, bf16[9,64,256]{2,1,0:T(8,128)(2,1)S(1)} %collective-permute-done.rest_2_, ...), custom_call_target="tpu_custom_call" | custom-call | tf_op jit(solution)/shard_map/pallas_call | solution.py:165
  27.1 1.6 %collective-permute-done.6.rest_2_ = bf16[9,64,256]{2,1,0:T(8,128)(2,1)S(1)} collective-permute-done((bf16[9,64,256]{2,1,0:T(8,128)(2,1)S(1)}, bf16[9,64,256]{2,1,0:T(8,128)(2,1)S(1)}, u32[]{:S(2)}, u32[]{:S(2)}) %collective-permute-start.6) | collective-permute-done | bytes 294944 | tf_op jit(solution)/shard_map/ppermute | solution.py:24
  28.7 1.5 %collective-permute-done.4.rest_0_ = bf16[9,64,256]{2,1,0:T(8,128)(2,1)S(1)} collective-permute-done((bf16[9,64,256]{2,1,0:T(8,128)(2,1)S(1)}, bf16[9,64,256]{2,1,0:T(8,128)(2,1)S(1)}, u32[]{:S(2)}, u32[]{:S(2)}) %collective-permute-start.4) | collective-permute-done | bytes 294944 | tf_op jit(solution)/shard_map/ppermute | solution.py:24
  30.2 0.5 collective-permute-start.1
  30.7 2.0 %collective-permute-start.14 = (bf16[9,64,256]{2,1,0:T(8,128)(2,1)S(1)}, bf16[9,64,256]{2,1,0:T(8,128)(2,1)S(1)}, u32[]{:S(2)}, u32[]{:S(2)}) collective-permute-start(bf16[9,64,256]{2,1,0:T(8,128)(2,1)S(1)} %collective-permute-done.6.rest_2_), channel_id=1, source_target_pairs={{0,1},{1,0},{2,3},{3,2},{4,5},{5,4},{6,7},{7,6},{8,9},{9,8},{10,11... | collective-permute-start | bytes 884744 | tf_op jit(solution)/shard_map/ppermute | solution.py:24
  32.7 2.0 %shard_map.119.rest_4_ = f32[2,6,64,1024]{3,2,1,0:T(8,128)S(1)} custom-call(s32[32]{0:T(128)S(1)} %copy-done.4, bf16[2,6,64,1024]{3,2,1,0:T(8,128)(2,1)S(1)} %copy-done.1, bf16[9,64,256]{2,1,0:T(8,128)(2,1)S(1)} %collective-permute-done.4.rest_0_, bf16[9,64,256]{2,1,0:T(8,128)(2,1)S(1)} %collective-permute-done.5.rest_1_, ...), custom_call_target="tpu_custom_call", output_to_operand_aliasing={{}: (6, {})} | custom-call | tf_op jit(solution)/shard_map/pallas_call | solution.py:165
  34.7 0.0 copy-start.2
  34.7 0.0 copy-start.5
  34.7 0.0 copy-start.6
  34.8 4.9 %collective-permute-done.1.rest_0_ = bf16[9,64,256]{2,1,0:T(8,128)(2,1)S(1)} collective-permute-done((bf16[9,64,256]{2,1,0:T(8,128)(2,1)S(1)}, bf16[9,64,256]{2,1,0:T(8,128)(2,1)S(1)}, u32[]{:S(2)}, u32[]{:S(2)}) %collective-permute-start.1) | collective-permute-done | bytes 294944 | tf_op jit(solution)/shard_map/ppermute | solution.py:24
  39.6 0.3 collective-permute-done.14.rest_2_
  39.9 0.3 collective-permute-start.15
  40.1 1.1 %collective-permute-done.13.rest_1_ = bf16[9,64,256]{2,1,0:T(8,128)(2,1)S(1)} collective-permute-done((bf16[9,64,256]{2,1,0:T(8,128)(2,1)S(1)}, bf16[9,64,256]{2,1,0:T(8,128)(2,1)S(1)}, u32[]{:S(2)}, u32[]{:S(2)}) %collective-permute-start.13) | collective-permute-done | bytes 294944 | tf_op jit(solution)/shard_map/ppermute | solution.py:24
  41.2 0.4 collective-permute-done.15.rest_3_
  41.6 2.2 %shard_map.120 = (f32[2,6,64,1024]{3,2,1,0:T(8,128)S(1)}, f32[16,1024]{1,0:T(8,128)S(1)}) custom-call(s32[32]{0:T(128)S(1)} %copy-done.4, bf16[2,6,64,1024]{3,2,1,0:T(8,128)(2,1)S(1)} %copy-done.1, bf16[9,64,256]{2,1,0:T(8,128)(2,1)S(1)} %collective-permute-done.1.rest_0_, ...), custom_call_target="tpu_custom_call", output_to_operand_aliasing={{0}: (6, {})} | custom-call | tf_op jit(solution)/shard_map/pallas_call | solution.py:165
  43.9 0.2 collective-permute-start.16
  44.1 1.1 %collective-permute-done.16 = f32[16,1024]{1,0:T(8,128)S(1)} collective-permute-done((f32[16,1024]{1,0:T(8,128)S(1)}, f32[16,1024]{1,0:T(8,128)S(1)}, u32[]{:S(2)}, u32[]{:S(2)}) %collective-permute-start.16) | collective-permute-done | bytes 65568 | tf_op jit(solution)/shard_map/ppermute | solution.py:24
  45.2 1.4 %collective-permute-start.17 = (f32[16,1024]{1,0:T(8,128)S(1)}, f32[16,1024]{1,0:T(8,128)S(1)}, u32[]{:S(2)}, u32[]{:S(2)}) collective-permute-start(f32[16,1024]{1,0:T(8,128)S(1)} %add.25), channel_id=1, source_target_pairs={{0,4},{1,5},{2,6},{3,7},{4,0},{5,1},{6,2},{7,3},{8,12},{9,13},{10,... | collective-permute-start | bytes 196616 | tf_op jit(solution)/shard_map/ppermute | solution.py:50
  46.6 1.7 %collective-permute-start.18 = (f32[16,1024]{1,0:T(8,128)S(1)}, f32[16,1024]{1,0:T(8,128)S(1)}, u32[]{:S(2)}, u32[]{:S(2)}) collective-permute-start(f32[16,1024]{1,0:T(8,128)S(1)} %add.25), channel_id=1, source_target_pairs={{0,1},{1,0},{2,3},{3,2},{4,5},{5,4},{6,7},{7,6},{8,9},{9,8},{10,11... | collective-permute-start | bytes 196616 | tf_op jit(solution)/shard_map/ppermute | solution.py:50
  48.3 0.4 collective-permute-start.19
  48.8 0.8 collective-permute-done.17
  49.5 1.3 %collective-permute-done.18 = f32[16,1024]{1,0:T(8,128)S(1)} collective-permute-done((f32[16,1024]{1,0:T(8,128)S(1)}, f32[16,1024]{1,0:T(8,128)S(1)}, u32[]{:S(2)}, u32[]{:S(2)}) %collective-permute-start.18) | collective-permute-done | bytes 65568 | tf_op jit(solution)/shard_map/ppermute | solution.py:50
  50.9 2.6 %collective-permute-done.19 = f32[16,1024]{1,0:T(8,128)S(1)} collective-permute-done((f32[16,1024]{1,0:T(8,128)S(1)}, f32[16,1024]{1,0:T(8,128)S(1)}, u32[]{:S(2)}, u32[]{:S(2)}) %collective-permute-start.19) | collective-permute-done | bytes 65568 | tf_op jit(solution)/shard_map/ppermute | solution.py:50
  53.5 1.7 %collective-permute-start.20 = (f32[16,1024]{1,0:T(8,128)S(1)}, f32[16,1024]{1,0:T(8,128)S(1)}, u32[]{:S(2)}, u32[]{:S(2)}) collective-permute-start(f32[16,1024]{1,0:T(8,128)S(1)} %add_add_fusion.1), channel_id=1, source_target_pairs={{0,8},{1,9},{2,10},{3,11},{4,12},{5,13},{6,14},{7,15},{8,0},{9,1},... | collective-permute-start | bytes 196616 | tf_op jit(solution)/shard_map/ppermute | solution.py:50
  55.3 0.6 collective-permute-start.21
  55.9 2.1 %collective-permute-start.22 = (f32[16,1024]{1,0:T(8,128)S(1)}, f32[16,1024]{1,0:T(8,128)S(1)}, u32[]{:S(2)}, u32[]{:S(2)}) collective-permute-start(f32[16,1024]{1,0:T(8,128)S(1)} %add_add_fusion.1), channel_id=1, source_target_pairs={{0,24},{1,25},{2,26},{3,27},{4,28},{5,29},{6,30},{7,31},{8,16},{9,... | collective-permute-start | bytes 196616 | tf_op jit(solution)/shard_map/ppermute | solution.py:50
  58.0 1.3 %collective-permute-done.20 = f32[16,1024]{1,0:T(8,128)S(1)} collective-permute-done((f32[16,1024]{1,0:T(8,128)S(1)}, f32[16,1024]{1,0:T(8,128)S(1)}, u32[]{:S(2)}, u32[]{:S(2)}) %collective-permute-start.20) | collective-permute-done | bytes 65568 | tf_op jit(solution)/shard_map/ppermute | solution.py:50
  59.2 1.7 %collective-permute-done.21 = f32[16,1024]{1,0:T(8,128)S(1)} collective-permute-done((f32[16,1024]{1,0:T(8,128)S(1)}, f32[16,1024]{1,0:T(8,128)S(1)}, u32[]{:S(2)}, u32[]{:S(2)}) %collective-permute-start.21) | collective-permute-done | bytes 65568 | tf_op jit(solution)/shard_map/ppermute | solution.py:50
  60.9 1.1 %collective-permute-done.22 = f32[16,1024]{1,0:T(8,128)S(1)} collective-permute-done((f32[16,1024]{1,0:T(8,128)S(1)}, f32[16,1024]{1,0:T(8,128)S(1)}, u32[]{:S(2)}, u32[]{:S(2)}) %collective-permute-start.22) | collective-permute-done | bytes 65568 | tf_op jit(solution)/shard_map/ppermute | solution.py:50
  62.1 1.4 %project.1 = (f32[2,6,64,256]{3,2,1,0:T(8,128)S(1)}, f32[32,4,256]{2,1,0:T(4,128)S(1)}) custom-call(s32[32]{0:T(128)S(1)} %copy-done.4, f32[2,6,64,1024]{3,2,1,0:T(8,128)S(1)} %get-tuple-element.20.pre_ref, f32[16,1024]{1,0:T(8,128)S(1)} %add_add_fusion.total_ref, f32[4,256]{1,0:T(4,128)S(1)} %copy-done.5, f32[4,256]{1,0:T(4,128)S(1)} %copy-done.6, ...), custom_call_target="tpu_custom_call" | custom-call | tf_op jit(solution)/shard_map/project/pallas_call | solution.py:278
  63.6 10.9 %all_to_all.10 = f32[32,4,256]{2,1,0:T(4,128)S(1)} all-to-all(f32[32,4,256]{2,1,0:T(4,128)S(1)} %get-tuple-element.24), channel_id=1, replica_groups=mesh['dp'=16,'rows'=2] {'dp','rows'}, dimensions={0} | all-to-all | bytes 262144 | tf_op jit(solution)/shard_map/all_to_all | solution.py:438
  74.5 0.8 finish.1
  75.3 14.8 %all_to_all.11 = bf16[32,6,4,256]{3,2,1,0:T(4,128)(2,1)S(1)} all-to-all(bf16[32,6,4,256]{3,2,1,0:T(4,128)(2,1)S(1)} %bitcast.5), channel_id=1, replica_groups=mesh['dp'=16,'rows'=2] {'dp'}, dimensions={0} | all-to-all | bytes 786432 | tf_op jit(solution)/shard_map/all_to_all | solution.py:448
  90.1 0.7 copy.18
  (30 shorter events, 0.1 us)
Async XLA Ops:
  0.0 13.8 %copy-start = (bf16[1024,256]{1,0:T(8,128)(2,1)S(1)}, bf16[1024,256]{1,0:T(8,128)(2,1)}, u32[]{:S(2)}) copy-start(bf16[1024,256]{1,0:T(8,128)(2,1)} %param.17) | copy-start | bytes 1572868
  0.0 23.3 %copy-start.1 = (bf16[2,6,64,1024]{3,2,1,0:T(8,128)(2,1)S(1)}, bf16[2,6,64,1024]{3,2,1,0:T(8,128)(2,1)}, u32[]{:S(2)}) copy-start(bf16[2,6,64,1024]{3,2,1,0:T(8,128)(2,1)} %x_ref.5) | copy-start | bytes 4718596
  0.0 23.3 %copy-start.3 = (bf16[1024,256]{1,0:T(8,128)(2,1)S(1)}, bf16[1024,256]{1,0:T(8,128)(2,1)}, u32[]{:S(2)}) copy-start(bf16[1024,256]{1,0:T(8,128)(2,1)} %rest_8_.1) | copy-start | bytes 1572868
  0.0 23.3 %copy-start.4 = (s32[32]{0:T(128)S(1)}, s32[32]{0:T(128)}, u32[]{:S(2)}) copy-start(s32[32]{0:T(128)} %index_ref.9) | copy-start | bytes 388
  1.2 17.6 %collective-permute-start.2 = (bf16[9,64,256]{2,1,0:T(8,128)(2,1)S(1)}, bf16[9,64,256]{2,1,0:T(8,128)(2,1)S(1)}, u32[]{:S(2)}, u32[]{:S(2)}) collective-permute-start(bf16[9,64,256]{2,1,0:T(8,128)(2,1)S(1)} %pick.1.rest_0_), channel_id=1, source_target_pairs={{0,16},{1,25},{2,18},{3,27},{4,20},{5,29},{6,22},{7,31},{8,24},{9,... | collective-permute-start | bytes 884744 | tf_op jit(solution)/shard_map/ppermute | solution.py:298
  5.3 13.6 %collective-permute-start = (bf16[9,64,256]{2,1,0:T(8,128)(2,1)S(1)}, bf16[9,64,256]{2,1,0:T(8,128)(2,1)S(1)}, u32[]{:S(2)}, u32[]{:S(2)}) collective-permute-start(bf16[9,64,256]{2,1,0:T(8,128)(2,1)S(1)} %pick.1.rest_0_), channel_id=1, source_target_pairs={{0,8},{2,10},{4,12},{6,14},{8,0},{10,2},{12,4},{14,6},{16,24},{18,... | collective-permute-start | bytes 884744 | tf_op jit(solution)/shard_map/ppermute | solution.py:24
  6.9 12.4 %collective-permute-start.10 = (bf16[9,64,256]{2,1,0:T(8,128)(2,1)S(1)}, bf16[9,64,256]{2,1,0:T(8,128)(2,1)}, u32[]{:S(2)}, u32[]{:S(2)}) collective-permute-start(bf16[9,64,256]{2,1,0:T(8,128)(2,1)S(1)} %pick.1.rest_0_), channel_id=1, source_target_pairs={{0,4},{2,6},{4,0},{6,2},{8,12},{10,14},{12,8},{14,10},{16,20},{18,... | collective-permute-start | bytes 884744 | tf_op jit(solution)/shard_map/ppermute | solution.py:24
  8.4 12.6 %collective-permute-start.7 = (bf16[9,64,256]{2,1,0:T(8,128)(2,1)S(1)}, bf16[9,64,256]{2,1,0:T(8,128)(2,1)}, u32[]{:S(2)}, u32[]{:S(2)}) collective-permute-start(bf16[9,64,256]{2,1,0:T(8,128)(2,1)S(1)} %pick.1.rest_0_), channel_id=1, source_target_pairs={{0,2},{2,0},{4,6},{6,4},{8,10},{10,8},{12,14},{14,12},{16,18},{18,... | collective-permute-start | bytes 884744 | tf_op jit(solution)/shard_map/ppermute | solution.py:24
  10.1 3.7 %collective-permute-start.3 = (f32[2,1024]{1,0:T(2,128)S(1)}, f32[2,1024]{1,0:T(2,128)S(1)}, u32[]{:S(2)}, u32[]{:S(2)}) collective-permute-start(f32[2,1024]{1,0:T(2,128)S(1)} %convert_reduce_fusion), channel_id=1, source_target_pairs={{0,1},{1,0},{2,3},{3,2},{4,5},{5,4},{6,7},{7,6},{8,9},{9,8},{10,11... | collective-permute-start | bytes 24584 | tf_op jit(solution)/shard_map/ppermute | solution.py:24
  18.8 4.5 %collective-permute-start.9 = (bf16[9,64,256]{2,1,0:T(8,128)(2,1)S(1)}, bf16[9,64,256]{2,1,0:T(8,128)(2,1)S(1)}, u32[]{:S(2)}, u32[]{:S(2)}) collective-permute-start(bf16[9,64,256]{2,1,0:T(8,128)(2,1)S(1)} %collective-permute-done.2.rest_4_), channel_id=1, source_target_pairs={{0,2},{2,0},{4,6},{6,4},{8,10},{10,8},{12,14},{14,12},{16,18},{18,... | collective-permute-start | bytes 884744 | tf_op jit(solution)/shard_map/ppermute | solution.py:24
  18.9 4.4 %collective-permute-start.8 = (bf16[9,64,256]{2,1,0:T(8,128)(2,1)S(1)}, bf16[9,64,256]{2,1,0:T(8,128)(2,1)S(1)}, u32[]{:S(2)}, u32[]{:S(2)}) collective-permute-start(bf16[9,64,256]{2,1,0:T(8,128)(2,1)S(1)} %collective-permute-done.rest_2_), channel_id=1, source_target_pairs={{0,2},{2,0},{4,6},{6,4},{8,10},{10,8},{12,14},{14,12},{16,18},{18,... | collective-permute-start | bytes 884744 | tf_op jit(solution)/shard_map/ppermute | solution.py:24
  19.3 4.0 %collective-permute-start.11 = (bf16[9,64,256]{2,1,0:T(8,128)(2,1)}, bf16[9,64,256]{2,1,0:T(8,128)(2,1)S(1)}, u32[]{:S(2)}, u32[]{:S(2)}) collective-permute-start(bf16[9,64,256]{2,1,0:T(8,128)(2,1)} %collective-permute-done.10.rest_6_), channel_id=1, source_target_pairs={{0,2},{2,0},{4,6},{6,4},{8,10},{10,8},{12,14},{14,12},{16,18},{18,... | collective-permute-start | bytes 884744 | tf_op jit(solution)/shard_map/ppermute | solution.py:24
  19.5 9.2 %collective-permute-start.6 = (bf16[9,64,256]{2,1,0:T(8,128)(2,1)S(1)}, bf16[9,64,256]{2,1,0:T(8,128)(2,1)S(1)}, u32[]{:S(2)}, u32[]{:S(2)}) collective-permute-start(bf16[9,64,256]{2,1,0:T(8,128)(2,1)S(1)} %collective-permute-done.2.rest_4_), channel_id=1, source_target_pairs={{0,4},{2,6},{4,0},{6,2},{8,12},{10,14},{12,8},{14,10},{16,20},{18,... | collective-permute-start | bytes 884744 | tf_op jit(solution)/shard_map/ppermute | solution.py:24
  21.0 9.2 %collective-permute-start.4 = (bf16[9,64,256]{2,1,0:T(8,128)(2,1)S(1)}, bf16[9,64,256]{2,1,0:T(8,128)(2,1)S(1)}, u32[]{:S(2)}, u32[]{:S(2)}) collective-permute-start(bf16[9,64,256]{2,1,0:T(8,128)(2,1)S(1)} %collective-permute-done.2.rest_4_), channel_id=1, source_target_pairs={{0,1},{1,0},{2,3},{3,2},{4,5},{5,4},{6,7},{7,6},{8,9},{9,8},{10,11... | collective-permute-start | bytes 884744 | tf_op jit(solution)/shard_map/ppermute | solution.py:24
  28.7 4.0 %collective-permute-start.12 = (bf16[9,64,256]{2,1,0:T(8,128)(2,1)S(1)}, bf16[9,64,256]{2,1,0:T(8,128)(2,1)S(1)}, u32[]{:S(2)}, u32[]{:S(2)}) collective-permute-start(bf16[9,64,256]{2,1,0:T(8,128)(2,1)S(1)} %collective-permute-done.6.rest_2_), channel_id=1, source_target_pairs={{0,2},{2,0},{4,6},{6,4},{8,10},{10,8},{12,14},{14,12},{16,18},{18,... | collective-permute-start | bytes 884744 | tf_op jit(solution)/shard_map/ppermute | solution.py:24
  30.2 2.5 %collective-permute-start.5 = (bf16[9,64,256]{2,1,0:T(8,128)(2,1)S(1)}, bf16[9,64,256]{2,1,0:T(8,128)(2,1)S(1)}, u32[]{:S(2)}, u32[]{:S(2)}) collective-permute-start(bf16[9,64,256]{2,1,0:T(8,128)(2,1)S(1)} %collective-permute-done.4.rest_0_), channel_id=1, source_target_pairs={{0,2},{2,0},{4,6},{6,4},{8,10},{10,8},{12,14},{14,12},{16,18},{18,... | collective-permute-start | bytes 884744 | tf_op jit(solution)/shard_map/ppermute | solution.py:24
  30.2 9.4 %collective-permute-start.1 = (bf16[9,64,256]{2,1,0:T(8,128)(2,1)S(1)}, bf16[9,64,256]{2,1,0:T(8,128)(2,1)S(1)}, u32[]{:S(2)}, u32[]{:S(2)}) collective-permute-start(bf16[9,64,256]{2,1,0:T(8,128)(2,1)S(1)} %collective-permute-done.rest_2_), channel_id=1, source_target_pairs={{0,4},{2,6},{4,0},{6,2},{8,12},{10,14},{12,8},{14,10},{16,20},{18,... | collective-permute-start | bytes 884744 | tf_op jit(solution)/shard_map/ppermute | solution.py:24
  30.7 9.1 %collective-permute-start.14 = (bf16[9,64,256]{2,1,0:T(8,128)(2,1)S(1)}, bf16[9,64,256]{2,1,0:T(8,128)(2,1)S(1)}, u32[]{:S(2)}, u32[]{:S(2)}) collective-permute-start(bf16[9,64,256]{2,1,0:T(8,128)(2,1)S(1)} %collective-permute-done.6.rest_2_), channel_id=1, source_target_pairs={{0,1},{1,0},{2,3},{3,2},{4,5},{5,4},{6,7},{7,6},{8,9},{9,8},{10,11... | collective-permute-start | bytes 884744 | tf_op jit(solution)/shard_map/ppermute | solution.py:24
  34.7 27.4 %copy-start.2 = (bf16[1280,256]{1,0:T(8,128)(2,1)S(1)}, bf16[1280,256]{1,0:T(8,128)(2,1)}, u32[]{:S(2)}) copy-start(bf16[1280,256]{1,0:T(8,128)(2,1)} %w_ref.1) | copy-start | bytes 1966084
  34.7 27.4 %copy-start.5 = (f32[4,256]{1,0:T(4,128)S(1)}, f32[4,256]{1,0:T(4,128)}, u32[]{:S(2)}) copy-start(f32[4,256]{1,0:T(4,128)} %gain_ref.1) | copy-start | bytes 12292
  34.7 27.4 %copy-start.6 = (f32[4,256]{1,0:T(4,128)S(1)}, f32[4,256]{1,0:T(4,128)}, u32[]{:S(2)}) copy-start(f32[4,256]{1,0:T(4,128)} %shift_ref.1) | copy-start | bytes 12292
  39.6 1.6 %collective-permute-start.13 = (bf16[9,64,256]{2,1,0:T(8,128)(2,1)S(1)}, bf16[9,64,256]{2,1,0:T(8,128)(2,1)S(1)}, u32[]{:S(2)}, u32[]{:S(2)}) collective-permute-start(bf16[9,64,256]{2,1,0:T(8,128)(2,1)S(1)} %collective-permute-done.1.rest_0_), channel_id=1, source_target_pairs={{0,2},{2,0},{4,6},{6,4},{8,10},{10,8},{12,14},{14,12},{16,18},{18,... | collective-permute-start | bytes 884744 | tf_op jit(solution)/shard_map/ppermute | solution.py:24
  39.9 1.7 %collective-permute-start.15 = (bf16[9,64,256]{2,1,0:T(8,128)(2,1)S(1)}, bf16[9,64,256]{2,1,0:T(8,128)(2,1)S(1)}, u32[]{:S(2)}, u32[]{:S(2)}) collective-permute-start(bf16[9,64,256]{2,1,0:T(8,128)(2,1)S(1)} %collective-permute-done.14.rest_2_), channel_id=1, source_target_pairs={{0,2},{2,0},{4,6},{6,4},{8,10},{10,8},{12,14},{14,12},{16,18},{18,... | collective-permute-start | bytes 884744 | tf_op jit(solution)/shard_map/ppermute | solution.py:24
  43.8 30.6 %copy-start.7 = (f32[256]{0:T(256)S(1)}, f32[256]{0:T(256)}, u32[]{:S(2)}) copy-start(f32[256]{0:T(256)} %param.21) | copy-start | bytes 3076
  43.9 30.6 %copy-start.8 = (f32[256]{0:T(256)S(1)}, f32[256]{0:T(256)}, u32[]{:S(2)}) copy-start(f32[256]{0:T(256)} %param.22) | copy-start | bytes 3076
  43.9 1.3 %collective-permute-start.16 = (f32[16,1024]{1,0:T(8,128)S(1)}, f32[16,1024]{1,0:T(8,128)S(1)}, u32[]{:S(2)}, u32[]{:S(2)}) collective-permute-start(f32[16,1024]{1,0:T(8,128)S(1)} %get-tuple-element.21), channel_id=1, source_target_pairs={{0,2},{2,0},{4,6},{6,4},{8,10},{10,8},{12,14},{14,12},{16,18},{18,... | collective-permute-start | bytes 196616 | tf_op jit(solution)/shard_map/ppermute | solution.py:24
  45.2 4.3 %collective-permute-start.17 = (f32[16,1024]{1,0:T(8,128)S(1)}, f32[16,1024]{1,0:T(8,128)S(1)}, u32[]{:S(2)}, u32[]{:S(2)}) collective-permute-start(f32[16,1024]{1,0:T(8,128)S(1)} %add.25), channel_id=1, source_target_pairs={{0,4},{1,5},{2,6},{3,7},{4,0},{5,1},{6,2},{7,3},{8,12},{9,13},{10,... | collective-permute-start | bytes 196616 | tf_op jit(solution)/shard_map/ppermute | solution.py:50
  46.6 4.3 %collective-permute-start.18 = (f32[16,1024]{1,0:T(8,128)S(1)}, f32[16,1024]{1,0:T(8,128)S(1)}, u32[]{:S(2)}, u32[]{:S(2)}) collective-permute-start(f32[16,1024]{1,0:T(8,128)S(1)} %add.25), channel_id=1, source_target_pairs={{0,1},{1,0},{2,3},{3,2},{4,5},{5,4},{6,7},{7,6},{8,9},{9,8},{10,11... | collective-permute-start | bytes 196616 | tf_op jit(solution)/shard_map/ppermute | solution.py:50
  48.3 5.2 %collective-permute-start.19 = (f32[16,1024]{1,0:T(8,128)S(1)}, f32[16,1024]{1,0:T(8,128)S(1)}, u32[]{:S(2)}, u32[]{:S(2)}) collective-permute-start(f32[16,1024]{1,0:T(8,128)S(1)} %add.25), channel_id=1, source_target_pairs={{0,5},{1,4},{2,7},{3,6},{4,1},{5,0},{6,3},{7,2},{8,13},{9,12},{10,... | collective-permute-start | bytes 196616 | tf_op jit(solution)/shard_map/ppermute | solution.py:50
  53.5 5.7 %collective-permute-start.20 = (f32[16,1024]{1,0:T(8,128)S(1)}, f32[16,1024]{1,0:T(8,128)S(1)}, u32[]{:S(2)}, u32[]{:S(2)}) collective-permute-start(f32[16,1024]{1,0:T(8,128)S(1)} %add_add_fusion.1), channel_id=1, source_target_pairs={{0,8},{1,9},{2,10},{3,11},{4,12},{5,13},{6,14},{7,15},{8,0},{9,1},... | collective-permute-start | bytes 196616 | tf_op jit(solution)/shard_map/ppermute | solution.py:50
  55.3 5.7 %collective-permute-start.21 = (f32[16,1024]{1,0:T(8,128)S(1)}, f32[16,1024]{1,0:T(8,128)S(1)}, u32[]{:S(2)}, u32[]{:S(2)}) collective-permute-start(f32[16,1024]{1,0:T(8,128)S(1)} %add_add_fusion.1), channel_id=1, source_target_pairs={{0,16},{1,17},{2,18},{3,19},{4,20},{5,21},{6,22},{7,23},{8,24},{9,... | collective-permute-start | bytes 196616 | tf_op jit(solution)/shard_map/ppermute | solution.py:50
  55.9 6.2 %collective-permute-start.22 = (f32[16,1024]{1,0:T(8,128)S(1)}, f32[16,1024]{1,0:T(8,128)S(1)}, u32[]{:S(2)}, u32[]{:S(2)}) collective-permute-start(f32[16,1024]{1,0:T(8,128)S(1)} %add_add_fusion.1), channel_id=1, source_target_pairs={{0,24},{1,25},{2,26},{3,27},{4,28},{5,29},{6,30},{7,31},{8,16},{9,... | collective-permute-start | bytes 196616 | tf_op jit(solution)/shard_map/ppermute | solution.py:50

commit v5 on v4

--- a/solution.py
+++ b/solution.py
@@ -11,7 +11,6 @@
 VMEM = pltpu.VMEM
 SMEM = pltpu.SMEM
 VMEM_LIMIT = 26 * 2**20
-WIDE = 2
 
 
 def from_behind(array, axis, by):
@@ -43,25 +42,40 @@
     return array
 
 
-def peer(array, dp_mask, rows_mask):
-    count = lax.axis_size("rows")
-    size = lax.axis_size("dp") * count
-    pairs = [(i, (i // count ^ dp_mask) * count + (i % count ^ rows_mask)) for i in range(size)]
-    return lax.ppermute(array, ("dp", "rows"), pairs)
-
-
-def total_over_all(stats):
+def regroup_kernel(planes, index_ref, sums_ref, out_ref):
+    places, both, _ = sums_ref.shape
+    images = both // 2
+    groups = out_ref.shape[0] // 2
+    lines = places // planes
+    base = lax.axis_index("dp") // lines * lines * images
+    out_ref[...] = jnp.zeros_like(out_ref)
+    for p in range(lines):
+        for i in range(images):
+            group = index_ref[base + p * images + i]
+            for part in range(2):
+                row = sums_ref[p * planes, pl.ds(part * images + i, 1), :]
+                for r in range(1, planes):
+                    row = row + sums_ref[p * planes + r, pl.ds(part * images + i, 1), :]
+                span = pl.ds(part * groups, groups)
+                out_ref[span, :] += group_rows(groups, group, row)
+
+
+def total_over_all(sums, index, groups):
+    slab, _, width = sums.shape
+    size = lax.axis_size(("dp", "rows"))
+    teams = [list(range(i, i + slab)) for i in range(0, size, slab)]
+    sums = lax.all_to_all(sums, ("dp", "rows"), 0, 0, tiled=True, axis_index_groups=teams)
+    total = pl.pallas_call(
+        functools.partial(regroup_kernel, lax.axis_size("rows")),
+        out_shape=jax.ShapeDtypeStruct((2 * groups, width), jnp.float32),
+        in_specs=[pl.BlockSpec(memory_space=SMEM), pl.BlockSpec(memory_space=VMEM)],
+        out_specs=pl.BlockSpec(memory_space=VMEM),
+        compiler_params=pltpu.CompilerParams(vmem_limit_bytes=VMEM_LIMIT),
+        name="regroup",
+    )(index, sums)
     quarter = lax.axis_size("dp") // 4
-    steps = [(mask, 0) for mask in masks_of("dp") if 1 < mask < quarter]
-    steps += [(0, mask) for mask in masks_of("rows")]
-    steps += [(quarter, 0), (2 * quarter, 0)]
-    total = stats + swap(stats, "dp", 1)
-    for i in range(0, len(steps), WIDE):
-        moves = [(0, 0)]
-        for a, b in steps[i : i + WIDE]:
-            moves += [(a ^ c, b ^ d) for c, d in moves]
-        total = sum((peer(total, *move) for move in moves[1:]), total)
-    return total
+    total = sum((swap(total, "dp", quarter * j) for j in (1, 2, 3)), total)
+    return total, swap(total, "dp", 1)
 
 
 def tap_span(cols, shift):
@@ -89,7 +103,7 @@
     return jnp.sum(jnp.where(rows == group, table, 0.0), axis=0, keepdims=True)
 
 
-def conv_kernel(groups, masks, opens, closes, index_ref, x_ref, *rest):
+def conv_kernel(planes, masks, opens, closes, index_ref, x_ref, *rest):
     shares, rest = rest[: 2 * len(masks)], rest[2 * len(masks) :]
     if opens:
         pw_ref, pre_ref, *rest = rest
@@ -97,7 +111,7 @@
         done_ref, pre_ref, *rest = rest
     if closes:
         stats_ref, *rest = rest
-        stats_ref[...] = jnp.zeros_like(stats_ref)
+        copies = stats_ref.shape[0]
     w_ref, part_ref = rest
     images, _, cols, _ = x_ref.shape
     outs = w_ref.shape[2]
@@ -121,20 +135,24 @@
         return y.reshape(r, c, outs)
 
     def image(i, carry):
-        group = index_ref[me * images + i]
-
         def emit(branch, value):
             span = pl.ds(branch * outs, outs)
             if branch == 0 and not opens:
                 value = done_ref[i, :, :, span]
             elif not opens:
                 value = value + done_ref[i, :, :, span]
-            pre_ref[i, :, :, span] = value
+            if opens or branch:
+                pre_ref[i, :, :, span] = value
             if closes:
                 first = jnp.sum(value, axis=(0, 1)).reshape(1, outs)
                 second = jnp.sum(value * value, axis=(0, 1)).reshape(1, outs)
-                stats_ref[pl.ds(0, groups), span] += group_rows(groups, group, first)
-                stats_ref[pl.ds(groups, groups), span] += group_rows(groups, group, second)
+                wide = stats_ref.shape[2]
+                half, at = divmod(branch * outs, wide)
+                span = pl.ds(at, outs)
+                for j in range(copies):
+                    if j // planes % 2 == half:
+                        stats_ref[j, pl.ds(i, 1), span] = first
+                        stats_ref[j, pl.ds(images + i, 1), span] = second
 
         if opens:
             emit(0, product(x_ref[i], pw_ref[...]))
@@ -153,17 +171,18 @@
     lax.fori_loop(0, images, image, 0)
 
 
-def conv_part(features, held, masks, index, groups, opening=None, done=None, closes=False):
+def conv_part(features, held, masks, index, opening=None, done=None, closes=False):
     shares = [share for mask in masks for share in held[mask]]
     images, rows, cols, _ = features.shape
     taps, depth, outs = shares[0].shape
     share = 2 * depth * len(masks)
     width = outs * (1 + len(DILATIONS))
     pre = jax.ShapeDtypeStruct((images, rows, cols, width), jnp.float32)
-    stats = jax.ShapeDtypeStruct((2 * groups, width), jnp.float32)
+    slab = lax.axis_size("dp") // 4 * lax.axis_size("rows")
+    stats = jax.ShapeDtypeStruct((slab, 2 * images, width // 2), jnp.float32)
     opens = done is None
     return pl.pallas_call(
-        functools.partial(conv_kernel, groups, tuple(masks), opens, closes),
+        functools.partial(conv_kernel, lax.axis_size("rows"), tuple(masks), opens, closes),
         out_shape=(pre, stats) if closes else (pre,),
         in_specs=[pl.BlockSpec(memory_space=SMEM)] + [pl.BlockSpec(memory_space=VMEM)] * (2 + len(shares)),
         out_specs=(pl.BlockSpec(memory_space=VMEM),) * (2 if closes else 1),
@@ -201,7 +220,7 @@
     )(*[pltpu.with_memory_space_constraint(kernel, pltpu.HBM) for kernel in kernels])
 
 
-def project_kernel(groups, count, index_ref, pre_ref, total_ref, gain_ref, shift_ref, w_ref, pool_ref, proj_ref, stats_ref):
+def project_kernel(groups, count, index_ref, pre_ref, mine_ref, other_ref, gain_ref, shift_ref, w_ref, pool_ref, proj_ref, stats_ref):
     images, rows, cols, width = pre_ref.shape
     outs = w_ref.shape[1]
     copies = stats_ref.shape[0]
@@ -211,8 +230,16 @@
 
     def image(i, carry):
         group = index_ref[me * images + i]
-        mean = pick_row(total_ref[pl.ds(0, groups), :], group) / count
-        var = pick_row(total_ref[pl.ds(groups, groups), :], group) / count - mean * mean
+
+        def total(at):
+            mine = pick_row(mine_ref[pl.ds(at, groups), :], group)
+            other = pick_row(other_ref[pl.ds(at, groups), :], group)
+            low_here = lax.rem(me, 2) == 0
+            low, high = jnp.where(low_here, mine, other), jnp.where(low_here, other, mine)
+            return jnp.concatenate([low, high], 1)
+
+        mean = total(0) / count
+        var = total(groups) / count - mean * mean
         inv = lax.rsqrt(var + 1e-05)
         pre = pre_ref[i].reshape(rows * cols, width)
         scaled = (pre - mean) * inv * gain + shift
@@ -281,11 +308,11 @@
             jax.ShapeDtypeStruct((images, rows, cols, outs), jnp.float32),
             jax.ShapeDtypeStruct((devices, 2 * images, outs), jnp.float32),
         ),
-        in_specs=[pl.BlockSpec(memory_space=SMEM)] + [pl.BlockSpec(memory_space=VMEM)] * 6,
+        in_specs=[pl.BlockSpec(memory_space=SMEM)] + [pl.BlockSpec(memory_space=VMEM)] * 7,
         out_specs=(pl.BlockSpec(memory_space=VMEM),) * 2,
         compiler_params=pltpu.CompilerParams(vmem_limit_bytes=VMEM_LIMIT),
         name="project",
-    )(index, pre, totals, gain, shift, weight, pool_term)
+    )(index, pre, *totals, gain, shift, weight, pool_term)
 
 
 def far_swap(array, even, odd):
@@ -326,12 +353,13 @@
     for mask in near:
         got[by(first, mask)] = swap(got[first], "dp", mask)
     got[second] = swap(got[first], "rows", 1)
-    for mask in near:
-        got[by(both, mask)] = swap(got[both], "dp", mask)
     pass_on(both)
     pass_on(first)
     opened = [origin, both, first] + beside
-    (done,) = conv_part(features, held, opened, index, groups, pointwise_weight)
+    (done,) = conv_part(features, held, opened, index, pointwise_weight)
+    got[both], done = lax.optimization_barrier((got[both], done))
+    for mask in near:
+        got[by(both, mask)] = swap(got[both], "dp", mask)
     relayed = []
     for mask in near:
         late = by(first, mask)
@@ -340,7 +368,7 @@
         pass_on(late)
         relayed.append(late)
     pass_on(second)
-    (done,) = conv_part(features, held, [second] + relayed, index, groups, done=done)
+    (done,) = conv_part(features, held, [second] + relayed, index, done=done)
     last = []
     for mask in near:
         late, final = by(both, mask), by(second, mask)
@@ -348,8 +376,8 @@
         pass_on(late)
         pass_on(final)
         last += [late, final]
-    pre, stats = conv_part(features, held, last, index, groups, done=done, closes=True)
-    return pre, total_over_all(stats), pool_term
+    pre, stats = conv_part(features, held, last, index, done=done, closes=True)
+    return pre, total_over_all(stats, index, groups), pool_term
 
 
 def row_tap_list(block_tensor, kernel_row_slice, dilation_rate):
@@ -423,7 +451,9 @@
             ],
             0,
         )
-        totals = sum_over(stats, ("dp", "rows"))
+        low, high = jnp.split(sum_over(stats, ("dp", "rows")), 2, axis=1)
+        core = lax.axis_index("dp") % 2
+        totals = jnp.where(core == 0, low, high), jnp.where(core == 0, high, low)
     proj, proj_stats = normed_project(
         pre,
         totals,

time: 91.1 us -> 91.6 us (level)
  blocking collectives: 25.7 us -> 33.1 us
  starting transfers between devices: 23.6 us -> 17.5 us
  waiting for transfers between devices: 26.4 us -> 25.1 us
    ppermute x6 -> x0, waiting for transfers between devices: 8.83 us -> none  [peer(): return lax.ppermute(array, ('dp', 'rows'), pairs)]
    ppermute x6 -> x0, starting transfers between devices: 8.01 us -> none  [peer(): return lax.ppermute(array, ('dp', 'rows'), pairs)]
    all_to_all x0 -> x1, blocking collectives: none -> 7.15 us  [total_over_all(): lax.all_to_all(sums, ('dp', 'rows'), 0, 0, tiled=True, axis_index_groups=...]
    ppermute x16 -> x19, waiting for transfers between devices: 13.8 us -> 19.1 us  [swap(): lax.ppermute(array, axis, [(i, i ^ mask) for i in range(lax.axis_size(axi...]
    ppermute x16 -> x19, starting transfers between devices: 11.4 us -> 14.9 us  [swap(): lax.ppermute(array, axis, [(i, i ^ mask) for i in range(lax.axis_size(axi...]
    ppermute x1, waiting for transfers between devices: 3.77 us -> 6.02 us  [far_swap(): return lax.ppermute(array, ('dp', 'rows'), pairs)]
    ppermute x1, starting transfers between devices: 4.14 us -> 2.59 us  [far_swap(): return lax.ppermute(array, ('dp', 'rows'), pairs)]
    pallas_call x3 -> x4, Pallas kernels: 7.9 us -> 8.42 us  [the longest x3 7.84 us: conv_part(): pl.pallas_call(functools.partial(conv_kernel, lax.axis_size('rows'), tupl...]
  transfers between devices with their start and end apart: 23 -> 20, of which waited for: 16 -> 13; matrix products, arithmetic and copies ran while one was open for 3% -> 3% of each run, Pallas kernels for 6% -> 6%
where the time goes in v5:
time: 91.6 us; the launch traced here: 91.3 us
  blocking collectives  33.1 us (36%)
  waiting for transfers between devices  25.1 us (27%)
  starting transfers between devices  17.5 us (19%)
  Pallas kernels  11.8 us (13%)
  other arithmetic  1.71 us (2%)
  matrix products  1.17 us (1%)
    ppermute x19, waiting for transfers between devices, swap(): lax.ppermute(array, axis, [(i, i ^ mask) for i in range(lax.axis_size(axi...  19.1 us
    ppermute x19, starting transfers between devices, swap(): lax.ppermute(array, axis, [(i, i ^ mask) for i in range(lax.axis_size(axi...  14.9 us
    all_to_all x1, blocking collectives, shards(): return lax.all_to_all(local_out, 'dp', 0, 0, tiled=True)  14.8 us
    all_to_all x1, blocking collectives, shards(): sums = lax.all_to_all(proj_stats, ('dp', 'rows'), 0, 0, tiled=True)  11.1 us
    pallas_call x3, Pallas kernels, conv_part(): pl.pallas_call(functools.partial(conv_kernel, lax.axis_size('rows'), tupl...  7.84 us
    all_to_all x1, blocking collectives, total_over_all(): lax.all_to_all(sums, ('dp', 'rows'), 0, 0, tiled=True, axis_index_groups=...  7.15 us
    ppermute x1, waiting for transfers between devices, far_swap(): return lax.ppermute(array, ('dp', 'rows'), pairs)  6.02 us
    ppermute x1, starting transfers between devices, far_swap(): return lax.ppermute(array, ('dp', 'rows'), pairs)  2.59 us
  transfers between devices with their start and end apart: 20, of which 13 were waited for; matrix products, arithmetic and copies ran while one was open for 3% of the time, Pallas kernels for 6%

profile of v5, /device:TPU:0, one launch (start us, length us, event | category | flops | bytes accessed | tf_op | source)
XLA Modules:
  0.0 91.3 jit_solution(16696232344325809688)
XLA Ops:
  0.0 1.2 %pick.1.rest_0_ = bf16[9,64,256]{2,1,0:T(8,128)(2,1)S(1)} custom-call(bf16[3,3,64,256]{3,2,1,0:T(8,128)(2,1)} %refs_0_.1, bf16[3,3,64,256]{3,2,1,0:T(8,128)(2,1)} %refs_1_.1, bf16[3,3,64,256]{3,2,1,0:T(8,128)(2,1)} %refs_2_.1), custom_call_target="tpu_custom_call" | custom-call | tf_op jit(solution)/shard_map/pick/pallas_call | solution.py:212
  1.2 3.1 %collective-permute-start = (bf16[9,64,256]{2,1,0:T(8,128)(2,1)S(1)}, bf16[9,64,256]{2,1,0:T(8,128)(2,1)S(1)}, u32[]{:S(2)}, u32[]{:S(2)}) collective-permute-start(bf16[9,64,256]{2,1,0:T(8,128)(2,1)S(1)} %pick.1.rest_0_), channel_id=1, source_target_pairs={{0,8},{2,10},{4,12},{6,14},{8,0},{10,2},{12,4},{14,6},{16,24},{18,... | collective-permute-start | bytes 884744 | tf_op jit(solution)/shard_map/ppermute | solution.py:23
  4.3 0.0 collective-permute-start.1
  4.3 2.6 %collective-permute-start.3 = (bf16[9,64,256]{2,1,0:T(8,128)(2,1)S(1)}, bf16[9,64,256]{2,1,0:T(8,128)(2,1)S(1)}, u32[]{:S(2)}, u32[]{:S(2)}) collective-permute-start(bf16[9,64,256]{2,1,0:T(8,128)(2,1)S(1)} %pick.1.rest_0_), channel_id=1, source_target_pairs={{0,16},{1,25},{2,18},{3,27},{4,20},{5,29},{6,22},{7,31},{8,24},{9,... | collective-permute-start | bytes 884744 | tf_op jit(solution)/shard_map/ppermute | solution.py:325
  6.9 1.5 %collective-permute-start.6 = (bf16[9,64,256]{2,1,0:T(8,128)(2,1)S(1)}, bf16[9,64,256]{2,1,0:T(8,128)(2,1)}, u32[]{:S(2)}, u32[]{:S(2)}) collective-permute-start(bf16[9,64,256]{2,1,0:T(8,128)(2,1)S(1)} %pick.1.rest_0_), channel_id=1, source_target_pairs={{0,4},{2,6},{4,0},{6,2},{8,12},{10,14},{12,8},{14,10},{16,20},{18,... | collective-permute-start | bytes 884744 | tf_op jit(solution)/shard_map/ppermute | solution.py:23
  8.4 1.7 %convert_reduce_fusion = f32[2,1024]{1,0:T(2,128)S(1)} fusion(bf16[2,6,64,1024]{3,2,1,0:T(8,128)(2,1)} %x_ref.5), kind=kLoop, calls=%fused_computation | loop fusion | flops 1570816 | bytes 1581056 | tf_op jit(solution)/shard_map/reduce_sum | solution.py:433
  10.1 1.5 %collective-permute-start.4 = (f32[2,1024]{1,0:T(2,128)S(1)}, f32[2,1024]{1,0:T(2,128)S(1)}, u32[]{:S(2)}, u32[]{:S(2)}) collective-permute-start(f32[2,1024]{1,0:T(2,128)S(1)} %convert_reduce_fusion), channel_id=1, source_target_pairs={{0,1},{1,0},{2,3},{3,2},{4,5},{5,4},{6,7},{7,6},{8,9},{9,8},{10,11... | collective-permute-start | bytes 24584 | tf_op jit(solution)/shard_map/ppermute | solution.py:23
  11.6 2.2 %collective-permute-done.4 = f32[2,1024]{1,0:T(2,128)S(1)} collective-permute-done((f32[2,1024]{1,0:T(2,128)S(1)}, f32[2,1024]{1,0:T(2,128)S(1)}, u32[]{:S(2)}, u32[]{:S(2)}) %collective-permute-start.4) | collective-permute-done | bytes 8224 | tf_op jit(solution)/shard_map/ppermute | solution.py:23
  13.8 1.2 %fusion.1.pool_ref = f32[2,256]{1,0:T(2,128)S(1)} fusion(bf16[1024,256]{1,0:T(8,128)(2,1)S(1)} %copy-done, bf16[1280,256]{1,0:T(8,128)(2,1)} %w_ref.1, f32[2,1024]{1,0:T(2,128)S(1)} %convert_reduce_fusion, f32[2,1024]{1,0:T(2,128)S(1)} %collective-permute-done.4), kind=kOutput, calls=%fused_computation.3 | convolution fusion | flops 1317888 | bytes 673792 | tf_op jit(solution)/shard_map/dot_general | solution.py:438
  15.0 6.0 %collective-permute-done.3.rest_4_ = bf16[9,64,256]{2,1,0:T(8,128)(2,1)S(1)} collective-permute-done((bf16[9,64,256]{2,1,0:T(8,128)(2,1)S(1)}, bf16[9,64,256]{2,1,0:T(8,128)(2,1)S(1)}, u32[]{:S(2)}, u32[]{:S(2)}) %collective-permute-start.3) | collective-permute-done | bytes 294944 | tf_op jit(solution)/shard_map/ppermute | solution.py:325
  21.0 0.5 collective-permute-start.2
  21.5 0.1 collective-permute-start.7
  21.6 1.5 %collective-permute-start.11 = (bf16[9,64,256]{2,1,0:T(8,128)(2,1)S(1)}, bf16[9,64,256]{2,1,0:T(8,128)(2,1)S(1)}, u32[]{:S(2)}, u32[]{:S(2)}) collective-permute-start(bf16[9,64,256]{2,1,0:T(8,128)(2,1)S(1)} %collective-permute-done.3.rest_4_), channel_id=1, source_target_pairs={{0,4},{2,6},{4,0},{6,2},{8,12},{10,14},{12,8},{14,10},{16,20},{18,... | collective-permute-start | bytes 884744 | tf_op jit(solution)/shard_map/ppermute | solution.py:23
  23.1 0.4 collective-permute-start.9
  23.6 3.7 %shard_map.118.rest_4_ = f32[2,6,64,1024]{3,2,1,0:T(8,128)S(1)} custom-call(s32[32]{0:T(128)S(1)} %copy-done.4, bf16[2,6,64,1024]{3,2,1,0:T(8,128)(2,1)S(1)} %copy-done.1, bf16[9,64,256]{2,1,0:T(8,128)(2,1)S(1)} %pick.1.rest_0_, bf16[9,64,256]{2,1,0:T(8,128)(2,1)} %collective-permute-done.1.rest_1_, bf16[9,64,256]{2,1,0:T(8,128)(2,1)S(1)} %collective-permute-done.rest_2_, ...), custom_call_target="tpu_custom_call" | custom-call | tf_op jit(solution)/shard_map/pallas_call | solution.py:184
  27.3 3.6 %collective-permute-done.11.rest_2_ = bf16[9,64,256]{2,1,0:T(8,128)(2,1)S(1)} collective-permute-done((bf16[9,64,256]{2,1,0:T(8,128)(2,1)S(1)}, bf16[9,64,256]{2,1,0:T(8,128)(2,1)S(1)}, u32[]{:S(2)}, u32[]{:S(2)}) %collective-permute-start.11) | collective-permute-done | bytes 294944 | tf_op jit(solution)/shard_map/ppermute | solution.py:23
  30.9 1.2 %collective-permute-done.9.rest_0_ = bf16[9,64,256]{2,1,0:T(8,128)(2,1)S(1)} collective-permute-done((bf16[9,64,256]{2,1,0:T(8,128)(2,1)S(1)}, bf16[9,64,256]{2,1,0:T(8,128)(2,1)S(1)}, u32[]{:S(2)}, u32[]{:S(2)}) %collective-permute-start.9) | collective-permute-done | bytes 294944 | tf_op jit(solution)/shard_map/ppermute | solution.py:23
  32.2 0.5 collective-permute-start.12
  32.7 0.5 collective-permute-start.8
  33.2 0.4 collective-permute-start.14
  33.7 0.1 collective-permute-done.10.rest_1_
  33.7 0.4 collective-permute-done.12.rest_3_
  34.2 2.0 %shard_map.119.rest_4_ = f32[2,6,64,1024]{3,2,1,0:T(8,128)S(1)} custom-call(s32[32]{0:T(128)S(1)} %copy-done.4, bf16[2,6,64,1024]{3,2,1,0:T(8,128)(2,1)S(1)} %copy-done.1, bf16[9,64,256]{2,1,0:T(8,128)(2,1)S(1)} %collective-permute-done.9.rest_0_, bf16[9,64,256]{2,1,0:T(8,128)(2,1)S(1)} %collective-permute-done.10.rest_1_, ...), custom_call_target="tpu_custom_call", output_to_operand_aliasing={{}: (6, {})} | custom-call | tf_op jit(solution)/shard_map/pallas_call | solution.py:184
  36.1 0.0 copy-start.2
  36.2 0.0 copy-start.5
  36.2 0.0 copy-start.6
  36.2 5.4 %collective-permute-done.8.rest_0_ = bf16[9,64,256]{2,1,0:T(8,128)(2,1)S(1)} collective-permute-done((bf16[9,64,256]{2,1,0:T(8,128)(2,1)S(1)}, bf16[9,64,256]{2,1,0:T(8,128)(2,1)S(1)}, u32[]{:S(2)}, u32[]{:S(2)}) %collective-permute-start.8) | collective-permute-done | bytes 294944 | tf_op jit(solution)/shard_map/ppermute | solution.py:23
  41.6 0.3 collective-permute-done.14.rest_2_
  41.8 0.3 collective-permute-start.15
  42.1 1.1 %collective-permute-done.13.rest_1_ = bf16[9,64,256]{2,1,0:T(8,128)(2,1)S(1)} collective-permute-done((bf16[9,64,256]{2,1,0:T(8,128)(2,1)S(1)}, bf16[9,64,256]{2,1,0:T(8,128)(2,1)S(1)}, u32[]{:S(2)}, u32[]{:S(2)}) %collective-permute-start.13) | collective-permute-done | bytes 294944 | tf_op jit(solution)/shard_map/ppermute | solution.py:23
  43.2 0.4 collective-permute-done.15.rest_3_
  43.6 2.1 %shard_map.120 = (f32[2,6,64,1024]{3,2,1,0:T(8,128)S(1)}, f32[8,4,512]{2,1,0:T(4,128)S(1)}) custom-call(s32[32]{0:T(128)S(1)} %copy-done.4, bf16[2,6,64,1024]{3,2,1,0:T(8,128)(2,1)S(1)} %copy-done.1, bf16[9,64,256]{2,1,0:T(8,128)(2,1)S(1)} %collective-permute-done.8.rest_0_, ...), custom_call_target="tpu_custom_call", output_to_operand_aliasing={{0}: (6, {})} | custom-call | tf_op jit(solution)/shard_map/pallas_call | solution.py:184
  45.7 0.0 copy-start.7
  45.8 0.0 copy-start.8
  45.8 7.2 %all_to_all.15.sums_ref = f32[8,4,512]{2,1,0:T(4,128)S(1)} all-to-all(f32[8,4,512]{2,1,0:T(4,128)S(1)} %get-tuple-element.25), channel_id=1, replica_groups={{0,1,2,3,4,5,6,7},{8,9,10,11,12,13,14,15},{16,17,18,19,20,21,22,23},{24..., dimensions={0} | all-to-all | bytes 131072 | tf_op jit(solution)/shard_map/all_to_all | solution.py:67
  52.9 0.6 regroup.1
  53.5 2.5 %collective-permute-start.18 = (f32[16,512]{1,0:T(8,128)S(1)}, f32[16,512]{1,0:T(8,128)S(1)}, u32[]{:S(2)}, u32[]{:S(2)}) collective-permute-start(f32[16,512]{1,0:T(8,128)S(1)} %regroup.1), channel_id=1, source_target_pairs={{0,24},{2,26},{4,28},{6,30},{8,16},{10,18},{12,20},{14,22},{16,8},... | collective-permute-start | bytes 98312 | tf_op jit(solution)/shard_map/ppermute | solution.py:23
  56.1 0.4 collective-permute-start.17
  56.5 1.5 %collective-permute-start.16 = (f32[16,512]{1,0:T(8,128)S(1)}, f32[16,512]{1,0:T(8,128)S(1)}, u32[]{:S(2)}, u32[]{:S(2)}) collective-permute-start(f32[16,512]{1,0:T(8,128)S(1)} %regroup.1), channel_id=1, source_target_pairs={{0,8},{2,10},{4,12},{6,14},{8,0},{10,2},{12,4},{14,6},{16,24},{18,... | collective-permute-start | bytes 98312 | tf_op jit(solution)/shard_map/ppermute | solution.py:23
  58.0 1.4 %collective-permute-done.18 = f32[16,512]{1,0:T(8,128)S(1)} collective-permute-done((f32[16,512]{1,0:T(8,128)S(1)}, f32[16,512]{1,0:T(8,128)S(1)}, u32[]{:S(2)}, u32[]{:S(2)}) %collective-permute-start.18) | collective-permute-done | bytes 32800 | tf_op jit(solution)/shard_map/ppermute | solution.py:23
  59.4 1.7 %collective-permute-done.17 = f32[16,512]{1,0:T(8,128)S(1)} collective-permute-done((f32[16,512]{1,0:T(8,128)S(1)}, f32[16,512]{1,0:T(8,128)S(1)}, u32[]{:S(2)}, u32[]{:S(2)}) %collective-permute-start.17) | collective-permute-done | bytes 32800 | tf_op jit(solution)/shard_map/ppermute | solution.py:23
  61.1 0.1 collective-permute-start.19
  61.2 1.2 %collective-permute-done.19.other_ref = f32[16,512]{1,0:T(8,128)S(1)} collective-permute-done((f32[16,512]{1,0:T(8,128)S(1)}, f32[16,512]{1,0:T(8,128)S(1)}, u32[]{:S(2)}, u32[]{:S(2)}) %collective-permute-start.19) | collective-permute-done | bytes 32800 | tf_op jit(solution)/shard_map/ppermute | solution.py:23
  62.4 1.4 %project.1 = (f32[2,6,64,256]{3,2,1,0:T(8,128)S(1)}, f32[32,4,256]{2,1,0:T(4,128)S(1)}) custom-call(s32[32]{0:T(128)S(1)} %copy-done.4, f32[2,6,64,1024]{3,2,1,0:T(8,128)S(1)} %get-tuple-element.24.pre_ref, f32[16,512]{1,0:T(8,128)S(1)} %add_add_fusion.mine_ref, f32[16,512]{1,0:T(8,128)S(1)} %collective-permute-done.19.other_ref, f32[4,256]{1,0:T(4,128)S(1)} %copy-done.5, ...), custom_call_target="tpu_custom_call" | custom-call | tf_op jit(solution)/shard_map/project/pallas_call | solution.py:305
  63.8 11.1 %all_to_all.16 = f32[32,4,256]{2,1,0:T(4,128)S(1)} all-to-all(f32[32,4,256]{2,1,0:T(4,128)S(1)} %get-tuple-element.28), channel_id=1, replica_groups=mesh['dp'=16,'rows'=2] {'dp','rows'}, dimensions={0} | all-to-all | bytes 262144 | tf_op jit(solution)/shard_map/all_to_all | solution.py:468
  74.9 0.8 finish.1
  75.8 14.8 %all_to_all.17 = bf16[32,6,4,256]{3,2,1,0:T(4,128)(2,1)S(1)} all-to-all(bf16[32,6,4,256]{3,2,1,0:T(4,128)(2,1)S(1)} %bitcast.5), channel_id=1, replica_groups=mesh['dp'=16,'rows'=2] {'dp'}, dimensions={0} | all-to-all | bytes 786432 | tf_op jit(solution)/shard_map/all_to_all | solution.py:478
  90.6 0.7 copy.18
  (24 shorter events, 0.1 us)
Async XLA Ops:
  0.0 13.8 %copy-start = (bf16[1024,256]{1,0:T(8,128)(2,1)S(1)}, bf16[1024,256]{1,0:T(8,128)(2,1)}, u32[]{:S(2)}) copy-start(bf16[1024,256]{1,0:T(8,128)(2,1)} %param.17) | copy-start | bytes 1572868
  0.0 23.5 %copy-start.1 = (bf16[2,6,64,1024]{3,2,1,0:T(8,128)(2,1)S(1)}, bf16[2,6,64,1024]{3,2,1,0:T(8,128)(2,1)}, u32[]{:S(2)}) copy-start(bf16[2,6,64,1024]{3,2,1,0:T(8,128)(2,1)} %x_ref.5) | copy-start | bytes 4718596
  0.0 23.6 %copy-start.4 = (s32[32]{0:T(128)S(1)}, s32[32]{0:T(128)}, u32[]{:S(2)}) copy-start(s32[32]{0:T(128)} %index_ref.11) | copy-start | bytes 388
  0.0 23.6 %copy-start.3 = (bf16[1024,256]{1,0:T(8,128)(2,1)S(1)}, bf16[1024,256]{1,0:T(8,128)(2,1)}, u32[]{:S(2)}) copy-start(bf16[1024,256]{1,0:T(8,128)(2,1)} %rest_8_.1) | copy-start | bytes 1572868
  1.2 19.8 %collective-permute-start = (bf16[9,64,256]{2,1,0:T(8,128)(2,1)S(1)}, bf16[9,64,256]{2,1,0:T(8,128)(2,1)S(1)}, u32[]{:S(2)}, u32[]{:S(2)}) collective-permute-start(bf16[9,64,256]{2,1,0:T(8,128)(2,1)S(1)} %pick.1.rest_0_), channel_id=1, source_target_pairs={{0,8},{2,10},{4,12},{6,14},{8,0},{10,2},{12,4},{14,6},{16,24},{18,... | collective-permute-start | bytes 884744 | tf_op jit(solution)/shard_map/ppermute | solution.py:23
  4.3 18.8 %collective-permute-start.1 = (bf16[9,64,256]{2,1,0:T(8,128)(2,1)S(1)}, bf16[9,64,256]{2,1,0:T(8,128)(2,1)}, u32[]{:S(2)}, u32[]{:S(2)}) collective-permute-start(bf16[9,64,256]{2,1,0:T(8,128)(2,1)S(1)} %pick.1.rest_0_), channel_id=1, source_target_pairs={{0,2},{2,0},{4,6},{6,4},{8,10},{10,8},{12,14},{14,12},{16,18},{18,... | collective-permute-start | bytes 884744 | tf_op jit(solution)/shard_map/ppermute | solution.py:23
  4.3 16.7 %collective-permute-start.3 = (bf16[9,64,256]{2,1,0:T(8,128)(2,1)S(1)}, bf16[9,64,256]{2,1,0:T(8,128)(2,1)S(1)}, u32[]{:S(2)}, u32[]{:S(2)}) collective-permute-start(bf16[9,64,256]{2,1,0:T(8,128)(2,1)S(1)} %pick.1.rest_0_), channel_id=1, source_target_pairs={{0,16},{1,25},{2,18},{3,27},{4,20},{5,29},{6,22},{7,31},{8,24},{9,... | collective-permute-start | bytes 884744 | tf_op jit(solution)/shard_map/ppermute | solution.py:325
  6.9 14.6 %collective-permute-start.6 = (bf16[9,64,256]{2,1,0:T(8,128)(2,1)S(1)}, bf16[9,64,256]{2,1,0:T(8,128)(2,1)}, u32[]{:S(2)}, u32[]{:S(2)}) collective-permute-start(bf16[9,64,256]{2,1,0:T(8,128)(2,1)S(1)} %pick.1.rest_0_), channel_id=1, source_target_pairs={{0,4},{2,6},{4,0},{6,2},{8,12},{10,14},{12,8},{14,10},{16,20},{18,... | collective-permute-start | bytes 884744 | tf_op jit(solution)/shard_map/ppermute | solution.py:23
  10.1 3.7 %collective-permute-start.4 = (f32[2,1024]{1,0:T(2,128)S(1)}, f32[2,1024]{1,0:T(2,128)S(1)}, u32[]{:S(2)}, u32[]{:S(2)}) collective-permute-start(f32[2,1024]{1,0:T(2,128)S(1)} %convert_reduce_fusion), channel_id=1, source_target_pairs={{0,1},{1,0},{2,3},{3,2},{4,5},{5,4},{6,7},{7,6},{8,9},{9,8},{10,11... | collective-permute-start | bytes 24584 | tf_op jit(solution)/shard_map/ppermute | solution.py:23
  21.0 2.5 %collective-permute-start.5 = (bf16[9,64,256]{2,1,0:T(8,128)(2,1)S(1)}, bf16[9,64,256]{2,1,0:T(8,128)(2,1)S(1)}, u32[]{:S(2)}, u32[]{:S(2)}) collective-permute-start(bf16[9,64,256]{2,1,0:T(8,128)(2,1)S(1)} %collective-permute-done.3.rest_4_), channel_id=1, source_target_pairs={{0,2},{2,0},{4,6},{6,4},{8,10},{10,8},{12,14},{14,12},{16,18},{18,... | collective-permute-start | bytes 884744 | tf_op jit(solution)/shard_map/ppermute | solution.py:23
  21.0 2.5 %collective-permute-start.2 = (bf16[9,64,256]{2,1,0:T(8,128)(2,1)S(1)}, bf16[9,64,256]{2,1,0:T(8,128)(2,1)S(1)}, u32[]{:S(2)}, u32[]{:S(2)}) collective-permute-start(bf16[9,64,256]{2,1,0:T(8,128)(2,1)S(1)} %collective-permute-done.rest_2_), channel_id=1, source_target_pairs={{0,2},{2,0},{4,6},{6,4},{8,10},{10,8},{12,14},{14,12},{16,18},{18,... | collective-permute-start | bytes 884744 | tf_op jit(solution)/shard_map/ppermute | solution.py:23
  21.5 2.0 %collective-permute-start.7 = (bf16[9,64,256]{2,1,0:T(8,128)(2,1)}, bf16[9,64,256]{2,1,0:T(8,128)(2,1)S(1)}, u32[]{:S(2)}, u32[]{:S(2)}) collective-permute-start(bf16[9,64,256]{2,1,0:T(8,128)(2,1)} %collective-permute-done.6.rest_6_), channel_id=1, source_target_pairs={{0,2},{2,0},{4,6},{6,4},{8,10},{10,8},{12,14},{14,12},{16,18},{18,... | collective-permute-start | bytes 884744 | tf_op jit(solution)/shard_map/ppermute | solution.py:23
  21.6 9.4 %collective-permute-start.11 = (bf16[9,64,256]{2,1,0:T(8,128)(2,1)S(1)}, bf16[9,64,256]{2,1,0:T(8,128)(2,1)S(1)}, u32[]{:S(2)}, u32[]{:S(2)}) collective-permute-start(bf16[9,64,256]{2,1,0:T(8,128)(2,1)S(1)} %collective-permute-done.3.rest_4_), channel_id=1, source_target_pairs={{0,4},{2,6},{4,0},{6,2},{8,12},{10,14},{12,8},{14,10},{16,20},{18,... | collective-permute-start | bytes 884744 | tf_op jit(solution)/shard_map/ppermute | solution.py:23
  23.1 9.1 %collective-permute-start.9 = (bf16[9,64,256]{2,1,0:T(8,128)(2,1)S(1)}, bf16[9,64,256]{2,1,0:T(8,128)(2,1)S(1)}, u32[]{:S(2)}, u32[]{:S(2)}) collective-permute-start(bf16[9,64,256]{2,1,0:T(8,128)(2,1)S(1)} %collective-permute-done.3.rest_4_), channel_id=1, source_target_pairs={{0,1},{1,0},{2,3},{3,2},{4,5},{5,4},{6,7},{7,6},{8,9},{9,8},{10,11... | collective-permute-start | bytes 884744 | tf_op jit(solution)/shard_map/ppermute | solution.py:23
  32.2 1.6 %collective-permute-start.10 = (bf16[9,64,256]{2,1,0:T(8,128)(2,1)S(1)}, bf16[9,64,256]{2,1,0:T(8,128)(2,1)S(1)}, u32[]{:S(2)}, u32[]{:S(2)}) collective-permute-start(bf16[9,64,256]{2,1,0:T(8,128)(2,1)S(1)} %collective-permute-done.9.rest_0_), channel_id=1, source_target_pairs={{0,2},{2,0},{4,6},{6,4},{8,10},{10,8},{12,14},{14,12},{16,18},{18,... | collective-permute-start | bytes 884744 | tf_op jit(solution)/shard_map/ppermute | solution.py:23
  32.2 2.0 %collective-permute-start.12 = (bf16[9,64,256]{2,1,0:T(8,128)(2,1)S(1)}, bf16[9,64,256]{2,1,0:T(8,128)(2,1)S(1)}, u32[]{:S(2)}, u32[]{:S(2)}) collective-permute-start(bf16[9,64,256]{2,1,0:T(8,128)(2,1)S(1)} %collective-permute-done.11.rest_2_), channel_id=1, source_target_pairs={{0,2},{2,0},{4,6},{6,4},{8,10},{10,8},{12,14},{14,12},{16,18},{18,... | collective-permute-start | bytes 884744 | tf_op jit(solution)/shard_map/ppermute | solution.py:23
  32.7 8.9 %collective-permute-start.8 = (bf16[9,64,256]{2,1,0:T(8,128)(2,1)S(1)}, bf16[9,64,256]{2,1,0:T(8,128)(2,1)S(1)}, u32[]{:S(2)}, u32[]{:S(2)}) collective-permute-start(bf16[9,64,256]{2,1,0:T(8,128)(2,1)S(1)} %collective-permute-done.rest_2_), channel_id=1, source_target_pairs={{0,4},{2,6},{4,0},{6,2},{8,12},{10,14},{12,8},{14,10},{16,20},{18,... | collective-permute-start | bytes 884744 | tf_op jit(solution)/shard_map/ppermute | solution.py:23
  33.2 8.6 %collective-permute-start.14 = (bf16[9,64,256]{2,1,0:T(8,128)(2,1)S(1)}, bf16[9,64,256]{2,1,0:T(8,128)(2,1)S(1)}, u32[]{:S(2)}, u32[]{:S(2)}) collective-permute-start(bf16[9,64,256]{2,1,0:T(8,128)(2,1)S(1)} %collective-permute-done.11.rest_2_), channel_id=1, source_target_pairs={{0,1},{1,0},{2,3},{3,2},{4,5},{5,4},{6,7},{7,6},{8,9},{9,8},{10,11... | collective-permute-start | bytes 884744 | tf_op jit(solution)/shard_map/ppermute | solution.py:23
  36.1 26.3 %copy-start.2 = (bf16[1280,256]{1,0:T(8,128)(2,1)S(1)}, bf16[1280,256]{1,0:T(8,128)(2,1)}, u32[]{:S(2)}) copy-start(bf16[1280,256]{1,0:T(8,128)(2,1)} %w_ref.1) | copy-start | bytes 1966084
  36.2 26.2 %copy-start.5 = (f32[4,256]{1,0:T(4,128)S(1)}, f32[4,256]{1,0:T(4,128)}, u32[]{:S(2)}) copy-start(f32[4,256]{1,0:T(4,128)} %gain_ref.1) | copy-start | bytes 12292
  36.2 26.2 %copy-start.6 = (f32[4,256]{1,0:T(4,128)S(1)}, f32[4,256]{1,0:T(4,128)}, u32[]{:S(2)}) copy-start(f32[4,256]{1,0:T(4,128)} %shift_ref.1) | copy-start | bytes 12292
  41.6 1.6 %collective-permute-start.13 = (bf16[9,64,256]{2,1,0:T(8,128)(2,1)S(1)}, bf16[9,64,256]{2,1,0:T(8,128)(2,1)S(1)}, u32[]{:S(2)}, u32[]{:S(2)}) collective-permute-start(bf16[9,64,256]{2,1,0:T(8,128)(2,1)S(1)} %collective-permute-done.8.rest_0_), channel_id=1, source_target_pairs={{0,2},{2,0},{4,6},{6,4},{8,10},{10,8},{12,14},{14,12},{16,18},{18,... | collective-permute-start | bytes 884744 | tf_op jit(solution)/shard_map/ppermute | solution.py:23
  41.8 1.7 %collective-permute-start.15 = (bf16[9,64,256]{2,1,0:T(8,128)(2,1)S(1)}, bf16[9,64,256]{2,1,0:T(8,128)(2,1)S(1)}, u32[]{:S(2)}, u32[]{:S(2)}) collective-permute-start(bf16[9,64,256]{2,1,0:T(8,128)(2,1)S(1)} %collective-permute-done.14.rest_2_), channel_id=1, source_target_pairs={{0,2},{2,0},{4,6},{6,4},{8,10},{10,8},{12,14},{14,12},{16,18},{18,... | collective-permute-start | bytes 884744 | tf_op jit(solution)/shard_map/ppermute | solution.py:23
  45.7 29.2 %copy-start.7 = (f32[256]{0:T(256)S(1)}, f32[256]{0:T(256)}, u32[]{:S(2)}) copy-start(f32[256]{0:T(256)} %param.21) | copy-start | bytes 3076
  45.8 29.2 %copy-start.8 = (f32[256]{0:T(256)S(1)}, f32[256]{0:T(256)}, u32[]{:S(2)}) copy-start(f32[256]{0:T(256)} %param.22) | copy-start | bytes 3076
  53.5 5.9 %collective-permute-start.18 = (f32[16,512]{1,0:T(8,128)S(1)}, f32[16,512]{1,0:T(8,128)S(1)}, u32[]{:S(2)}, u32[]{:S(2)}) collective-permute-start(f32[16,512]{1,0:T(8,128)S(1)} %regroup.1), channel_id=1, source_target_pairs={{0,24},{2,26},{4,28},{6,30},{8,16},{10,18},{12,20},{14,22},{16,8},... | collective-permute-start | bytes 98312 | tf_op jit(solution)/shard_map/ppermute | solution.py:23
  56.1 5.0 %collective-permute-start.17 = (f32[16,512]{1,0:T(8,128)S(1)}, f32[16,512]{1,0:T(8,128)S(1)}, u32[]{:S(2)}, u32[]{:S(2)}) collective-permute-start(f32[16,512]{1,0:T(8,128)S(1)} %regroup.1), channel_id=1, source_target_pairs={{0,16},{2,18},{4,20},{6,22},{8,24},{10,26},{12,28},{14,30},{16,0},... | collective-permute-start | bytes 98312 | tf_op jit(solution)/shard_map/ppermute | solution.py:23
  56.5 4.6 %collective-permute-start.16 = (f32[16,512]{1,0:T(8,128)S(1)}, f32[16,512]{1,0:T(8,128)S(1)}, u32[]{:S(2)}, u32[]{:S(2)}) collective-permute-start(f32[16,512]{1,0:T(8,128)S(1)} %regroup.1), channel_id=1, source_target_pairs={{0,8},{2,10},{4,12},{6,14},{8,0},{10,2},{12,4},{14,6},{16,24},{18,... | collective-permute-start | bytes 98312 | tf_op jit(solution)/shard_map/ppermute | solution.py:23
  61.1 1.3 %collective-permute-start.19 = (f32[16,512]{1,0:T(8,128)S(1)}, f32[16,512]{1,0:T(8,128)S(1)}, u32[]{:S(2)}, u32[]{:S(2)}) collective-permute-start(f32[16,512]{1,0:T(8,128)S(1)} %add_add_fusion.mine_ref), channel_id=1, source_target_pairs={{0,2},{2,0},{4,6},{6,4},{8,10},{10,8},{12,14},{14,12},{16,18},{18,... | collective-permute-start | bytes 98312 | tf_op jit(solution)/shard_map/ppermute | solution.py:23
